TPU v7x, 32 devices: a whole 2x2x4 slice. The times are simulated.
32 devices in a mesh: macro: 16 (over z, x, core), vox: 2 (over y).
Axes of the slice: x: 2, y: 2, z: 4, core: 2. Of those that a mesh axis runs over, the one named last changes fastest.
Arguments:
- displacement: float32 [3, 1024], P(None, 'macro'), may hold values from -1.2 to 1.2
- load: float32 [3, 1024], P(None, 'macro'), may hold values from -6 to 6
- conn: int32 [8, 1024], P(None, 'macro'), may hold values from 0 to 79
- halo_list: int32 [256], P('macro'), may hold values from 0 to 63
- grad_ops: float32 [3, 8, 1024], P(None, None, 'macro'), may hold values from -3 to 3
- volume: float32 [1024], P('macro'), may hold values from 0.5 to 2
- elastic_moduli: float32 [2, 1024], P(None, 'macro'), may hold values from 1 to 4
- plastic_mask: int32 [1024], P('macro'), may hold values from 0 to 1, as said below
- new_owner: int32 [1024], P('macro'), may hold values from -1 to 15, as said below
- state: float32 [7, 1024, 16, 256], P(None, 'macro', 'vox'), may hold values from -0.6 to 1, as said below
- micro_moduli: float32 [4, 16, 256], P(None, 'vox'), may hold values from 0.5 to 6
Outputs:
- residual: float32 [3, 1024], P(None, 'macro')
- moved_state: float32 [7, 384, 16, 256], P(None, 'macro', 'vox')
Inputs may be any that keep to these rules, and one draw needn't show every extreme that they name: `plastic_mask`: each group's 64 points hold at most 48 plastic ones, 384 in all. `new_owner`: -1 exactly at elastic points; every group becomes the owner of exactly 24 plastic points, at most 3 of them from any one group. `state`: component 6 is nonnegative.
All inputs are finite; a program needn't handle non-finite values.
Results may differ from a plain program's by a relative error of at most 0.0001.
Values sent between devices are 32-bit elements; how exact they have to be, the bound alone decides.
A program may use at most 64 MiB of HBM per device.

v0:
```python
import math

import jax
import jax.numpy as jnp
from jax import lax
from jax.sharding import PartitionSpec as P

RECV_AGG = 24
PLASTIC_MAX = 48
VOX_SIDE = 16
VOX_PLANE = 256
SWEEPS = 4


LAM_REF = 3.0
MU_REF = 3.0
FULL_PREC = lax.Precision.HIGHEST


def shifted(block, axis, distance):
    devices = range(lax.axis_size(axis))
    route = [((i - distance) % len(devices), i) for i in devices]
    return lax.ppermute(block, axis, route)


def strain_tensor(disp_el, grad_el):
    products = [[jnp.sum(disp_el[i] * grad_el[j], axis=0) for j in range(3)] for i in range(3)]
    return jnp.stack(
        [
            products[0][0],
            products[1][1],
            products[2][2],
            0.5 * (products[1][2] + products[2][1]),
            0.5 * (products[0][2] + products[2][0]),
            0.5 * (products[0][1] + products[1][0]),
        ]
    )


def full_tensor(voigt):
    return [
        [voigt[0], voigt[5], voigt[4]],
        [voigt[5], voigt[1], voigt[3]],
        [voigt[4], voigt[3], voigt[2]],
    ]


def nodal_forces(stress, grad_el, volume):
    tensor = full_tensor(stress)
    return jnp.stack(
        [
            volume
            * (tensor[i][0] * grad_el[0] + tensor[i][1] * grad_el[1] + tensor[i][2] * grad_el[2])
            for i in range(3)
        ]
    )


def elastic_stress(strain, moduli):
    lame_first = moduli[0]
    shear_mod = moduli[1]
    trace = strain[0] + strain[1] + strain[2]
    return jnp.stack(
        [lame_first * trace + 2.0 * shear_mod * strain[c] for c in range(3)]
        + [2.0 * shear_mod * strain[c] for c in range(3, 6)]
    )


def return_map(strain, state, props):
    lame_first, shear_mod, yield_base, harden = (props[0], props[1], props[2], props[3])
    elastic = [strain[c] - state[c] for c in range(6)]
    trace = elastic[0] + elastic[1] + elastic[2]
    trial = [lame_first * trace + 2.0 * shear_mod * elastic[c] for c in range(3)] + [
        2.0 * shear_mod * elastic[c] for c in range(3, 6)
    ]
    pressure = (trial[0] + trial[1] + trial[2]) / 3.0
    deviator = [
        trial[0] - pressure,
        trial[1] - pressure,
        trial[2] - pressure,
        trial[3],
        trial[4],
        trial[5],
    ]
    squared = (
        deviator[0] ** 2
        + deviator[1] ** 2
        + deviator[2] ** 2
        + 2.0 * (deviator[3] ** 2 + deviator[4] ** 2 + deviator[5] ** 2)
    )
    equivalent = jnp.sqrt(1.5 * squared)
    strength = yield_base + harden * state[6]
    excess = jnp.maximum(equivalent - strength, 0.0)
    stiffer = 3.0 * shear_mod + harden
    factor = excess / (stiffer * jnp.maximum(equivalent, strength))
    stress = jnp.stack([trial[c] - 3.0 * shear_mod * factor * deviator[c] for c in range(6)])
    new_state = jnp.stack(
        [state[c] + 1.5 * factor * deviator[c] for c in range(6)] + [state[6] + excess / stiffer]
    )
    return (stress, new_state)


def green_apply(tau, freq_x, freq_y, freq_z):
    trac_x = tau[0] * freq_x + tau[5] * freq_y + tau[4] * freq_z
    trac_y = tau[5] * freq_x + tau[1] * freq_y + tau[3] * freq_z
    trac_z = tau[4] * freq_x + tau[3] * freq_y + tau[2] * freq_z
    norm_sq = freq_x * freq_x + freq_y * freq_y + freq_z * freq_z
    inverse = jnp.where(norm_sq > 0, 1.0 / jnp.maximum(norm_sq, 1.0), 0.0)
    coupling = (LAM_REF + MU_REF) / (LAM_REF + 2.0 * MU_REF)
    along = (freq_x * trac_x + freq_y * trac_y + freq_z * trac_z) * inverse
    wave_x = (trac_x - coupling * along * freq_x) * inverse / MU_REF
    wave_y = (trac_y - coupling * along * freq_y) * inverse / MU_REF
    wave_z = (trac_z - coupling * along * freq_z) * inverse / MU_REF
    return [
        freq_x * wave_x,
        freq_y * wave_y,
        freq_z * wave_z,
        0.5 * (freq_y * wave_z + freq_z * wave_y),
        0.5 * (freq_x * wave_z + freq_z * wave_x),
        0.5 * (freq_x * wave_y + freq_y * wave_x),
    ]


def dft_tables():
    line_index = jnp.arange(VOX_SIDE, dtype=jnp.int32)
    line_phase = line_index[:, None] * line_index[None, :] % VOX_SIDE
    plane_index = jnp.arange(VOX_PLANE, dtype=jnp.int32)
    plane_rows = plane_index // VOX_SIDE
    plane_cols = plane_index % VOX_SIDE
    plane_phase = (
        plane_rows[:, None] * plane_rows[None, :] + plane_cols[:, None] * plane_cols[None, :]
    ) % VOX_SIDE
    radians = 2.0 * math.pi / VOX_SIDE
    line_angle = line_phase.astype(jnp.float32) * radians
    plane_angle = plane_phase.astype(jnp.float32) * radians
    signed = jnp.where(line_index < VOX_SIDE // 2, line_index, line_index - VOX_SIDE).astype(
        jnp.float32
    )
    return (
        jnp.cos(line_angle),
        jnp.sin(line_angle),
        jnp.cos(plane_angle),
        jnp.sin(plane_angle),
        signed[:, None],
        signed[plane_rows],
        signed[plane_cols],
    )


def line_apply(table, field):
    return jnp.einsum("kx,cbxn->cbkn", table, field, precision=FULL_PREC)


def spectral_correction(stress, tables):
    cos_line, sin_line, cos_plane, sin_plane, freq_x, freq_y, freq_z = tables
    real_plane = jnp.dot(stress, cos_plane, precision=FULL_PREC)
    imag_plane = -jnp.dot(stress, sin_plane, precision=FULL_PREC)
    real_full = line_apply(cos_line, real_plane) + line_apply(sin_line, imag_plane)
    imag_full = line_apply(cos_line, imag_plane) - line_apply(sin_line, real_plane)
    green_real = jnp.stack(green_apply([real_full[c] for c in range(6)], freq_x, freq_y, freq_z))
    green_imag = jnp.stack(green_apply([imag_full[c] for c in range(6)], freq_x, freq_y, freq_z))
    back_real = line_apply(cos_line, green_real) - line_apply(sin_line, green_imag)
    back_imag = line_apply(cos_line, green_imag) + line_apply(sin_line, green_real)
    spatial = jnp.dot(back_real, cos_plane, precision=FULL_PREC) - jnp.dot(
        back_imag, sin_plane, precision=FULL_PREC
    )
    return spatial / VOX_SIDE**3


def micro_solve(states, strains, moduli_slab):
    tables = dft_tables()
    aggregates = states.shape[1]
    thickness = states.shape[2]
    ranks_vox = lax.axis_size("vox")
    per_rank = aggregates // ranks_vox
    full_moduli = lax.all_gather(moduli_slab, "vox", axis=1, tiled=True)
    gathered = lax.all_to_all(
        states.reshape(7, ranks_vox, per_rank, thickness, VOX_PLANE),
        "vox",
        split_axis=1,
        concat_axis=3,
        tiled=True,
    )
    gathered = gathered.reshape(7, per_rank, VOX_SIDE, VOX_PLANE)
    own_strain = lax.dynamic_slice_in_dim(strains, lax.axis_index("vox") * per_rank, per_rank, 1)
    strain_field = jnp.broadcast_to(own_strain[:, :, None, None], (6,) + gathered.shape[1:])
    for iteration in range(SWEEPS):
        stress, _ = return_map(strain_field, gathered, full_moduli)
        strain_field = strain_field - spectral_correction(stress, tables)
    stress, updated = return_map(strain_field, gathered, full_moduli)
    averaged = lax.all_gather(jnp.mean(stress, axis=(2, 3)), "vox", axis=1, tiled=True)
    returned = lax.all_to_all(
        updated.reshape(7, per_rank, ranks_vox, thickness, VOX_PLANE),
        "vox",
        split_axis=2,
        concat_axis=1,
        tiled=True,
    )
    return (returned.reshape(states.shape), averaged)


def pick_slots(valid, count):
    position = jnp.cumsum(valid.astype(jnp.int32)) - 1
    wanted = jnp.arange(count, dtype=jnp.int32)
    matching = (wanted[:, None] == position[None, :]) & valid[None, :]
    sources = jnp.arange(valid.shape[0], dtype=jnp.int32)
    return (jnp.sum(jnp.where(matching, sources[None, :], 0), axis=1), matching)


def local(
    displacement,
    load,
    conn,
    halo_list,
    grad_ops,
    volume,
    elastic_moduli,
    plastic_mask,
    new_owner,
    state,
    micro_moduli,
):
    groups = lax.axis_size("macro")
    own_nodes = displacement.shape[1]
    elements = conn.shape[1]
    halo_disp = shifted(displacement[:, halo_list], "macro", 1)
    local_disp = jnp.concatenate([displacement, halo_disp], axis=1)
    strain = strain_tensor(local_disp[:, conn], grad_ops)
    plastic = plastic_mask == 1
    point_ids = jnp.arange(elements, dtype=jnp.int32)
    same_owner = (
        (new_owner[:, None] == new_owner[None, :])
        & plastic[:, None]
        & plastic[None, :]
        & (point_ids[None, :] < point_ids[:, None])
    )
    owner_rank = jnp.sum(same_owner.astype(jnp.int32), axis=1)
    capacity = (PLASTIC_MAX + groups - 1) // groups
    send_slot = jnp.where(plastic, new_owner * capacity + owner_rank, -1)
    slot_ids = jnp.arange(groups * capacity, dtype=jnp.int32)
    slot_match = slot_ids[:, None] == send_slot[None, :]
    slot_valid = jnp.any(slot_match, axis=1)
    valid_float = slot_valid.astype(jnp.float32)
    slot_source = jnp.sum(jnp.where(slot_match, point_ids[None, :], 0), axis=1)
    outgoing = state[:, slot_source] * valid_float[None, :, None, None]
    strain_rows = strain[:, slot_source] * valid_float[None, :]
    received, got_strain, got_valid = (
        lax.all_to_all(outgoing, "macro", split_axis=1, concat_axis=1, tiled=True),
        lax.all_to_all(strain_rows, "macro", split_axis=1, concat_axis=1, tiled=True),
        lax.all_to_all(valid_float[None, :], "macro", split_axis=1, concat_axis=1, tiled=True),
    )
    recv_index, recv_match = pick_slots(got_valid[0] > 0.5, RECV_AGG)
    moved_state, averaged = micro_solve(
        received[:, recv_index], got_strain[:, recv_index], micro_moduli
    )
    slot_stress = jnp.dot(averaged, recv_match.astype(jnp.float32), precision=FULL_PREC)
    got_stress = lax.all_to_all(slot_stress, "macro", split_axis=1, concat_axis=1, tiled=True)
    stress_plastic = jnp.dot(got_stress, slot_match.astype(jnp.float32), precision=FULL_PREC)
    stress = jnp.where(plastic[None, :], stress_plastic, elastic_stress(strain, elastic_moduli))
    forces = nodal_forces(stress, grad_ops, volume)
    node_ids = jnp.arange(local_disp.shape[1], dtype=jnp.int32)
    node_match = (conn[:, :, None] == node_ids[None, None, :]).astype(jnp.float32)
    assembled = jnp.einsum("iae,aen->in", forces, node_match, precision=FULL_PREC)
    returned_force = shifted(assembled[:, own_nodes:], "macro", -1)
    own_ids = jnp.arange(own_nodes, dtype=jnp.int32)
    halo_match = (halo_list[:, None] == own_ids[None, :]).astype(jnp.float32)
    residual = (
        assembled[:, :own_nodes] + jnp.dot(returned_force, halo_match, precision=FULL_PREC) - load
    )
    return (residual, moved_state)


def solution(mesh):
    return jax.shard_map(
        local,
        mesh=mesh,
        in_specs=(
            P(None, "macro"),
            P(None, "macro"),
            P(None, "macro"),
            P("macro"),
            P(None, None, "macro"),
            P("macro"),
            P(None, "macro"),
            P("macro"),
            P("macro"),
            P(None, "macro", "vox", None),
            P(None, "vox", None),
        ),
        out_specs=(P(None, "macro"), P(None, "macro", "vox", None)),
        check_vma=False,
    )
```

profile of v0, /device:TPU:0, one launch (start us, length us, event | category | flops | bytes accessed | tf_op | source)
XLA Modules:
  0.0 243.7 jit_solution(13568793401414966940)
XLA Ops:
  3.7 7.4 %all-to-all-start.1 = ((f32[1,16,3]{2,0,1:T(1,128)}), f32[1,16,3]{2,0,1:T(1,128)S(1)}, u32[]{:S(2)}, u32[]{:S(2)}) async-start(f32[1,16,3]{2,0,1:T(1,128)} %bitcast.13), calls=%async_computation.1 | async-start | bytes 16384 | tf_op jit(solution)/shard_map/all_to_all | solution.py:250
  11.9 2.8 %gather_fusion.4 = f32[48,7,8,256]{3,2,1,0:T(8,128)S(1)} fusion(f32[7,64,8,256]{3,2,1,0:T(8,128)} %param.20, s32[1024]{0:T(1024)S(1)} %get-tuple-element.240), kind=kCustom, calls=%fused_computation.4 | custom fusion | bytes 5505216 | tf_op jit(solution)/shard_map/gather | solution.py:245
  17.5 5.2 %all-to-all-start.2 = ((f32[7,48,8,256]{3,2,0,1:T(8,128)}), f32[7,48,8,256]{3,2,0,1:T(8,128)S(1)}, u32[]{:S(2)}, u32[]{:S(2)}) async-start(f32[7,48,8,256]{3,2,0,1:T(8,128)} %multiply_bitcast_fusion), calls=%async_computation.2 | async-start | bytes 5505024 | tf_op jit(solution)/shard_map/all_to_all | solution.py:248
  25.3 4.2 %compare_select_fusion.3 = (f32[256,1]{0,1:T(1,128)S(1)}, f32[256,1]{0,1:T(1,128)S(1)}) fusion(f32[]{:T(128)} %bitcast.53, f32[]{:T(128)} %bitcast.54, f32[]{:T(128)} %bitcast.55, f32[]{:T(128)} %bitcast.56, f32[]{:T(128)} %bitcast.57, f32[]{:T(128)} %bitcast.59, f32[]{:T(128)} %bitcast.58), kind=kLoop, calls=%fused_computation.506 | loop fusion | flops 10752 | bytes 2076 | tf_op jit(solution)/shard_map/gather | solution.py:146
  29.6 5.6 %broadcast_multiply_fusion.1 = (f32[256]{0:T(256)S(1)}, f32[256]{0:T(256)S(1)}) fusion(pred[256]{0:T(512)(128)(4,1)S(1)} %compare_reduce_fusion.1, pred[256]{0:T(512)(128)(4,1)S(1)} %compare_reduce_fusion.2, pred[256]{0:T(512)(128)(4,1)S(1)} %compare_reduce_fusion.3, pred[256]{0:T(512)(128)(4,1)S(1)} %compare_reduce_fusion.4, ...), kind=kLoop, calls=%fused_computation.559 | loop fusion | flops 2560 | bytes 5412 | tf_op jit(solution)/shard_map/mul | solution.py:117
  35.2 5.6 %broadcast_multiply_fusion.2 = (f32[256]{0:T(256)S(1)}, f32[256]{0:T(256)S(1)}) fusion(pred[256]{0:T(512)(128)(4,1)S(1)} %compare_reduce_fusion.10, pred[256]{0:T(512)(128)(4,1)S(1)} %compare_reduce_fusion.11, pred[256]{0:T(512)(128)(4,1)S(1)} %compare_reduce_fusion.12, pred[256]{0:T(512)(128)(4,1)S(1)} %compare_reduce_fusion.13, ...), kind=kLoop, calls=%fused_computation.560 | loop fusion | flops 2560 | bytes 5412 | tf_op jit(solution)/shard_map/mul | solution.py:116
  40.9 31.7 %collective-permute-done = f32[3,16]{0,1:T(8,128)S(1)} collective-permute-done((f32[3,16]{0,1:T(8,128)S(1)}, f32[3,16]{0,1:T(8,128)S(1)}, u32[]{:S(2)}, u32[]{:S(2)}) %collective-permute-start) | collective-permute-done | bytes 224 | tf_op jit(solution)/shard_map/ppermute | solution.py:23
  76.2 15.5 %all-to-all-start = ((f32[6,16,3]{0,2,1:T(4,128)}), f32[6,16,3]{0,2,1:T(4,128)S(1)}, u32[]{:S(2)}, u32[]{:S(2)}) async-start(f32[6,16,3]{0,2,1:T(4,128)} %copy.230), calls=%async_computation | async-start | bytes 65536 | tf_op jit(solution)/shard_map/all_to_all | solution.py:249
  93.5 2.4 gather_fusion.5
  98.3 3.6 %all-to-all-start.3 = ((f32[7,2,12,8,256]{4,3,2,0,1:T(8,128)}), f32[7,2,12,8,256]{4,3,2,0,1:T(8,128)S(1)}, u32[]{:S(2)}, u32[]{:S(2)}) async-start(f32[7,2,12,8,256]{4,3,2,0,1:T(8,128)} %copy.238), calls=%async_computation.3 | async-start | bytes 2752512 | tf_op jit(solution)/shard_map/all_to_all | solution.py:177
  102.0 17.9 %all_gather.6 = f32[4,16,256]{2,1,0:T(8,128)S(1)} all-gather(f32[4,8,256]{2,1,0:T(8,128)S(1)} %copy-done.1), channel_id=1, replica_groups=mesh['macro'=16,'vox'=2] {'vox'}, dimensions={1}, use_global_device_ids=true | all-gather | bytes 98304 | tf_op jit(solution)/shard_map/all_gather | solution.py:176
  139.3 2.2 fusion.7
  144.3 2.5 %convolution_negate_fusion.2 = f32[6,12,16,256]{3,2,1,0:T(8,128)S(1)} fusion(f32[6,12,16,256]{3,2,1,0:T(8,128)S(1)} %fusion.57, s32[256]{0:T(256)S(1)} %get-tuple-element.244, s32[256]{0:T(256)S(1)} %get-tuple-element.245), kind=kOutput, calls=%fused_computation.18 | convolution fusion | flops 907313152 | bytes 2361344 | tf_op jit(solution)/shard_map/dot_general | solution.py:157
  157.4 2.3 fusion.36
  159.8 2.2 fusion.5
  177.8 2.1 fusion.32
  179.9 2.6 %fusion.3 = f32[6,12,16,256]{3,2,1,0:T(8,128)S(1)} fusion(f32[6,12,16,256]{3,2,1,0:T(8,128)S(1)} %fusion.5, f32[6,12,16,256]{3,2,1,0:T(8,128)S(1)} %fusion.32, f32[6,12,16,256]{3,2,1,0:T(8,128)S(1)} %fusion.12, s32[256]{0:T(256)S(1)} %get-tuple-element.244, s32[256]{0:T(256)S(1)} %get-tuple-element.245), kind=kOutput, calls=%fused_computation.13 | convolution fusion | flops 907902976 | bytes 4720640 | tf_op jit(solution)/shard_map/dot_general | solution.py:164
  198.3 2.2 fusion.28
  200.5 2.2 fusion.1
  203.9 4.4 %all-gather = f32[2,12,6]{1,2,0:T(8,128)S(1)} all-gather(f32[1,12,6]{1,2,0:T(8,128)S(1)} %multiply_bitcast_fusion.2), channel_id=1, replica_groups=mesh['macro'=16,'vox'=2] {'vox'}, dimensions={0}, use_global_device_ids=true | all-gather | bytes 864 | tf_op jit(solution)/shard_map/all_gather | solution.py:191
  209.3 5.4 %all-to-all-start.4 = ((f32[6,16,3]{0,2,1:T(4,128)}), f32[6,16,3]{0,2,1:T(4,128)S(1)}, u32[]{:S(2)}, u32[]{:S(2)}) async-start(f32[6,16,3]{0,2,1:T(4,128)} %copy.247), calls=%async_computation.4 | async-start | bytes 65536 | tf_op jit(solution)/shard_map/all_to_all | solution.py:257
  216.0 5.3 %all-to-all-done.4 = f32[6,16,3]{0,2,1:T(4,128)S(1)} async-done(((f32[6,16,3]{0,2,1:T(4,128)}), f32[6,16,3]{0,2,1:T(4,128)S(1)}, u32[]{:S(2)}, u32[]{:S(2)}) %all-to-all-start.4) | async-done | bytes 1184 | tf_op jit(solution)/shard_map/all_to_all | solution.py:257
  221.4 3.6 %all-to-all-start.5 = ((f32[7,12,2,8,256]{4,3,1,0,2:T(8,128)}), f32[7,12,2,8,256]{4,3,1,0,2:T(8,128)S(1)}, u32[]{:S(2)}, u32[]{:S(2)}) async-start(f32[7,12,2,8,256]{4,3,1,0,2:T(8,128)} %copy.267), calls=%async_computation.5 | async-start | bytes 2752512 | tf_op jit(solution)/shard_map/all_to_all | solution.py:192
  227.9 14.3 %all-to-all-done.5 = f32[7,12,2,8,256]{4,3,1,0,2:T(8,128)S(1)} async-done(((f32[7,12,2,8,256]{4,3,1,0,2:T(8,128)}), f32[7,12,2,8,256]{4,3,1,0,2:T(8,128)S(1)}, u32[]{:S(2)}, u32[]{:S(2)}) %all-to-all-start.5) | async-done | bytes 1376288 | tf_op jit(solution)/shard_map/all_to_all | solution.py:192
  (216 shorter events, 88.4 us)
Async XLA Ops:
  3.7 13.8 %all-to-all-start.1 = ((f32[1,16,3]{2,0,1:T(1,128)}), f32[1,16,3]{2,0,1:T(1,128)S(1)}, u32[]{:S(2)}, u32[]{:S(2)}) async-start(f32[1,16,3]{2,0,1:T(1,128)} %bitcast.13), calls=%async_computation.1 | async-start | bytes 16384 | tf_op jit(solution)/shard_map/all_to_all | solution.py:250
  16.5 6.2 %copy-start.4 = (f32[3,64]{1,0:T(4,128)S(1)}, f32[3,64]{1,0:T(4,128)}, u32[]{:S(2)}) copy-start(f32[3,64]{1,0:T(4,128)} %param.11) | copy-start | bytes 2308
  16.5 7.4 %copy-start.2 = (s32[8,64]{1,0:T(8,128)S(1)}, s32[8,64]{1,0:T(8,128)}, u32[]{:S(2)}) copy-start(s32[8,64]{1,0:T(8,128)} %param.13) | copy-start | bytes 6148
  16.5 57.3 %copy-start = (f32[3,8,64]{2,1,0:T(8,128)S(1)}, f32[3,8,64]{2,1,0:T(8,128)}, u32[]{:S(2)}) copy-start(f32[3,8,64]{2,1,0:T(8,128)} %param.15) | copy-start | bytes 18436
  16.5 57.4 %copy-start.3 = (f32[2,64]{1,0:T(2,128)S(1)}, f32[2,64]{1,0:T(2,128)}, u32[]{:S(2)}) copy-start(f32[2,64]{1,0:T(2,128)} %param.17) | copy-start | bytes 1540
  17.5 58.7 %all-to-all-start.2 = ((f32[7,48,8,256]{3,2,0,1:T(8,128)}), f32[7,48,8,256]{3,2,0,1:T(8,128)S(1)}, u32[]{:S(2)}, u32[]{:S(2)}) async-start(f32[7,48,8,256]{3,2,0,1:T(8,128)} %multiply_bitcast_fusion), calls=%async_computation.2 | async-start | bytes 5505024 | tf_op jit(solution)/shard_map/all_to_all | solution.py:248
  23.3 49.3 %collective-permute-start = (f32[3,16]{0,1:T(8,128)S(1)}, f32[3,16]{0,1:T(8,128)S(1)}, u32[]{:S(2)}, u32[]{:S(2)}) collective-permute-start(f32[3,16]{0,1:T(8,128)S(1)} %bitcast.583), channel_id=1, source_target_pairs={{30,0},{0,2},{2,4},{4,6},{6,8},{8,10},{10,12},{12,14},{14,16},{16,... | collective-permute-start | bytes 584 | tf_op jit(solution)/shard_map/ppermute | solution.py:23
  76.2 22.1 %all-to-all-start = ((f32[6,16,3]{0,2,1:T(4,128)}), f32[6,16,3]{0,2,1:T(4,128)S(1)}, u32[]{:S(2)}, u32[]{:S(2)}) async-start(f32[6,16,3]{0,2,1:T(4,128)} %copy.230), calls=%async_computation | async-start | bytes 65536 | tf_op jit(solution)/shard_map/all_to_all | solution.py:249
  97.1 4.8 %copy-start.1 = (f32[4,8,256]{2,1,0:T(8,128)S(1)}, f32[4,8,256]{2,1,0:T(8,128)}, u32[]{:S(2)}) copy-start(f32[4,8,256]{2,1,0:T(8,128)} %param.21) | copy-start | bytes 98308
  98.3 22.6 %all-to-all-start.3 = ((f32[7,2,12,8,256]{4,3,2,0,1:T(8,128)}), f32[7,2,12,8,256]{4,3,2,0,1:T(8,128)S(1)}, u32[]{:S(2)}, u32[]{:S(2)}) async-start(f32[7,2,12,8,256]{4,3,2,0,1:T(8,128)} %copy.238), calls=%async_computation.3 | async-start | bytes 2752512 | tf_op jit(solution)/shard_map/all_to_all | solution.py:177
  209.3 12.1 %all-to-all-start.4 = ((f32[6,16,3]{0,2,1:T(4,128)}), f32[6,16,3]{0,2,1:T(4,128)S(1)}, u32[]{:S(2)}, u32[]{:S(2)}) async-start(f32[6,16,3]{0,2,1:T(4,128)} %copy.247), calls=%async_computation.4 | async-start | bytes 65536 | tf_op jit(solution)/shard_map/all_to_all | solution.py:257
  216.0 9.2 %copy-start.5 = (f32[64]{0:T(128)S(1)}, f32[64]{0:T(128)}, u32[]{:S(2)}) copy-start(f32[64]{0:T(128)} %param.16) | copy-start | bytes 772
  216.0 11.1 %copy-start.6 = (f32[3,64]{1,0:T(4,128)S(1)}, f32[3,64]{1,0:T(4,128)}, u32[]{:S(2)}) copy-start(f32[3,64]{1,0:T(4,128)} %param.12) | copy-start | bytes 2308
  216.0 11.1 %copy-start.7 = (s32[16]{0:T(128)S(1)}, s32[16]{0:T(128)}, u32[]{:S(2)}) copy-start(s32[16]{0:T(128)} %param.14) | copy-start | bytes 196
  221.4 20.9 %all-to-all-start.5 = ((f32[7,12,2,8,256]{4,3,1,0,2:T(8,128)}), f32[7,12,2,8,256]{4,3,1,0,2:T(8,128)S(1)}, u32[]{:S(2)}, u32[]{:S(2)}) async-start(f32[7,12,2,8,256]{4,3,1,0,2:T(8,128)} %copy.267), calls=%async_computation.5 | async-start | bytes 2752512 | tf_op jit(solution)/shard_map/all_to_all | solution.py:192
  225.6 1.5 collective-permute-start.1
where the time goes:
time: 248 us; the launch traced here: 244 us
  matrix products  74.8 us (30%)
  waiting for transfers between devices  54.8 us (22%)
  starting transfers between devices  41.4 us (17%)
  other arithmetic  30.3 us (12%)
  blocking collectives  22.3 us (9%)
  local copies, waits for them, and re-layouts  18.1 us (7%)
    dot_general x32, matrix products, line_apply(): return jnp.einsum('kx,cbxn->cbkn', table, field, precision=FULL_PREC)  38.1 us
    ppermute x2, waiting for transfers between devices, shifted(): return lax.ppermute(block, axis, route)  33 us
    all_gather x1, blocking collectives, micro_solve(): full_moduli = lax.all_gather(moduli_slab, 'vox', axis=1, tiled=True)  17.9 us
    all_to_all x1, starting transfers between devices, local(): lax.all_to_all(strain_rows, 'macro', split_axis=1, concat_axis=1, tiled=T...  15.5 us
    all_to_all x1, waiting for transfers between devices, micro_solve(): lax.all_to_all(updated.reshape(7, per_rank, ranks_vox, thickness, VOX_PLA...  14.3 us
    dot_general x4, matrix products, spectral_correction(): jnp.dot(back_imag, sin_plane, precision=FULL_PREC)  9.12 us
    dot_general x4, matrix products, spectral_correction(): imag_plane = -jnp.dot(stress, sin_plane, precision=FULL_PREC)  8.95 us
    dot_general x4, matrix products, spectral_correction(): jnp.dot(back_real, cos_plane, precision=FULL_PREC)  8.75 us
  transfers between devices with their start and end apart: 8, of which 6 were waited for; matrix products, arithmetic and copies ran while one was open for 15% of the time, Pallas kernels for 0%

commit v1 on v0

v1 whole, which is shorter than its diff:
```python
import functools
import math

import jax
import jax.numpy as jnp
import numpy as np
from jax import lax
from jax.experimental import pallas as pl
from jax.experimental.pallas import tpu as pltpu
from jax.sharding import PartitionSpec as P

RECV_AGG = 24
PLASTIC_MAX = 48
VOX_SIDE = 16
VOX_PLANE = 256
SWEEPS = 4
HALF = VOX_SIDE // 2

LAM_REF = 3.0
MU_REF = 3.0
FULL_PREC = lax.Precision.HIGHEST

ROOT = math.sqrt(0.5)
COS1 = math.cos(math.pi / 8)
COS3 = math.cos(3 * math.pi / 8)
PAIRS = [(i, j) for i in range(6) for j in range(i, 6)]


def shifted(block, axis, distance):
    devices = range(lax.axis_size(axis))
    route = [((i - distance) % len(devices), i) for i in devices]
    return lax.ppermute(block, axis, route)


def gather_vox(block):
    ranks = lax.axis_size("vox")
    pieces = jnp.stack([block] + [shifted(block, "vox", d) for d in range(1, ranks)])
    me = lax.axis_index("vox")
    if ranks == 2:
        return jnp.where(me == 0, pieces, pieces[::-1])
    return pieces[(me - jnp.arange(ranks)) % ranks]


def green_tables():
    line = np.arange(VOX_SIDE)
    signed = np.where(line < HALF, line, line - VOX_SIDE).astype(np.float64)
    freq = np.stack(np.meshgrid(signed, signed, signed, indexing="ij"))
    norm = np.sum(freq * freq, axis=0)
    inverse = np.where(norm > 0, 1.0 / np.maximum(norm, 1.0), 0.0)
    coupling = (LAM_REF + MU_REF) / (LAM_REF + 2.0 * MU_REF)
    spots = [(0, 0), (1, 1), (2, 2), (1, 2), (0, 2), (0, 1)]
    table = np.zeros((6, 6) + norm.shape)
    for j, (a, b) in enumerate(spots):
        tau = np.zeros((3, 3))
        tau[a, b] = tau[b, a] = 1.0
        trac = np.einsum("ij,jxyz->ixyz", tau, freq)
        along = np.sum(freq * trac, axis=0) * inverse
        wave = (trac - coupling * along * freq) * inverse / MU_REF
        for i, (c, d) in enumerate(spots):
            table[i, j] = 0.5 * (freq[c] * wave[d] + freq[d] * wave[c])
    back = -line % VOX_SIDE
    flipped = table[:, :, back][:, :, :, back][:, :, :, :, back]
    even = 0.5 * (table + flipped) / VOX_SIDE**3
    even[:, 3:] *= 0.5
    stacked = np.stack([even[i, j] for i, j in PAIRS])
    return stacked.reshape(len(PAIRS), VOX_SIDE, VOX_PLANE).astype(np.float32)


def plane_tables():
    plane = np.arange(VOX_PLANE)
    rows, cols = plane // VOX_SIDE, plane % VOX_SIDE
    phase = (rows[:, None] * rows[None, :] + cols[:, None] * cols[None, :]) % VOX_SIDE
    angle = phase * (2.0 * math.pi / VOX_SIDE)
    plus = jnp.asarray((np.cos(angle) + np.sin(angle)).astype(np.float32))
    minus = jnp.asarray((np.cos(angle) - np.sin(angle)).astype(np.float32))
    out = []
    for table in (plus, minus):
        high = table.astype(jnp.bfloat16)
        out += [high, (table - high.astype(jnp.float32)).astype(jnp.bfloat16)]
    return jnp.stack(out)


def cosine_line(a):
    sums = [None] + [a[x] + a[8 - x] for x in (1, 2, 3)]
    diffs = [None] + [a[x] - a[8 - x] for x in (1, 2, 3)]
    even0, odd0 = a[0] + a[8], a[0] - a[8]
    outer, inner = even0 + a[4], even0 - a[4]
    spread = sums[1] + sums[3]
    slant = ROOT * (sums[1] - sums[3])
    mid = ROOT * diffs[2]
    first = COS1 * diffs[1] + COS3 * diffs[3]
    second = COS3 * diffs[1] - COS1 * diffs[3]
    top, low = odd0 + mid, odd0 - mid
    core = outer + sums[2]
    return [
        core + spread,
        top + first,
        inner + slant,
        low + second,
        outer - sums[2],
        low - second,
        inner - slant,
        top - first,
        core - spread,
    ]


def sine_line(b):
    sums = [None] + [b[x] + b[8 - x] for x in (1, 2, 3)]
    diffs = [None] + [b[x] - b[8 - x] for x in (1, 2, 3)]
    slant = ROOT * (diffs[1] + diffs[3])
    mid = ROOT * sums[2]
    first = COS3 * sums[1] + COS1 * sums[3]
    second = COS1 * sums[1] - COS3 * sums[3]
    return [
        None,
        (first + mid) + b[4],
        slant + diffs[2],
        (second + mid) - b[4],
        diffs[1] - diffs[3],
        (second - mid) + b[4],
        slant - diffs[2],
        (first - mid) - b[4],
    ]


def split_dot(block, table_ref, first):
    high = block.astype(jnp.bfloat16)
    low = (block - high.astype(jnp.float32)).astype(jnp.bfloat16)
    dot = functools.partial(jnp.dot, preferred_element_type=jnp.float32)
    return dot(high, table_ref[first]) + (dot(high, table_ref[first + 1]) + dot(low, table_ref[first]))


def voxel_law(strain, state_ref, props_ref, x):
    row = pl.ds(x, 1)
    lam, mu = props_ref[0, row, :], props_ref[1, row, :]
    yield_base, harden = props_ref[2, row, :], props_ref[3, row, :]
    two_mu, three_mu = 2.0 * mu, 3.0 * mu
    stiff_inv = 1.0 / (three_mu + harden)
    bulk = lam + two_mu * (1.0 / 3.0)
    elastic = [strain[c] - state_ref[c, x] for c in range(6)]
    trace = elastic[0] + elastic[1] + elastic[2]
    third = trace * (1.0 / 3.0)
    shape = [elastic[c] - third for c in range(3)] + elastic[3:]
    normal = shape[0] * shape[0] + shape[1] * shape[1] + shape[2] * shape[2]
    shear = shape[3] * shape[3] + shape[4] * shape[4] + shape[5] * shape[5]
    equivalent = two_mu * jnp.sqrt(1.5 * (normal + 2.0 * shear))
    strength = yield_base + harden * state_ref[6, x]
    gain = jnp.maximum(equivalent - strength, 0.0) * stiff_inv
    factor = gain / jnp.maximum(equivalent, strength)
    keep = two_mu * (1.0 - three_mu * factor)
    pressure = bulk * trace
    stress = [pressure + keep * shape[c] for c in range(3)] + [keep * shape[c] for c in range(3, 6)]
    return stress, shape, (1.5 * two_mu) * factor, gain


def solve_kernel(strain_ref, valid_ref, state_ref, props_ref, green_ref, plane_ref, new_ref, mean_ref, eps, work, cos_ref, sin_ref):
    rows = state_ref.shape[2]
    for c in range(6):
        start = jnp.broadcast_to(strain_ref[c], (VOX_SIDE, rows, VOX_PLANE))
        eps[c] = start

    def sweep(step, carry):
        def law(x, inner):
            stress, _, _, _ = voxel_law([eps[c, x] for c in range(6)], state_ref, props_ref, x)
            for c in range(6):
                work[c, x] = stress[c]
            return inner

        lax.fori_loop(0, VOX_SIDE, law, 0)

        def forward(c, inner):
            field = [work[c, x] for x in range(VOX_SIDE)]
            sums = [field[0]] + [field[x] + field[VOX_SIDE - x] for x in range(1, HALF)] + [field[HALF]]
            diffs = [None] + [field[x] - field[VOX_SIDE - x] for x in range(1, HALF)]
            for k, value in enumerate(cosine_line(sums)):
                cos_ref[c, k] = value
            for k, value in enumerate(sine_line(diffs)):
                if k > 0:
                    sin_ref[c, k - 1] = value
            return inner

        lax.fori_loop(0, 6, forward, 0)

        def plane():
            for ref, first in ((cos_ref, 0), (sin_ref, 2)):
                flat = ref[...].reshape(6 * ref.shape[1] * rows, VOX_PLANE)
                ref[...] = split_dot(flat, plane_ref, first).reshape(ref.shape)

        def apply(field, k):
            row = pl.ds(k, 1)
            field = field[:3] + [2.0 * field[c] for c in range(3, 6)]
            total = [None] * 6
            for n, (i, j) in enumerate(PAIRS):
                entry = green_ref[n, row, :]
                for a, b in [(i, j), (j, i)][: 1 + (i != j)]:
                    term = entry * field[b]
                    total[a] = term if total[a] is None else total[a] + term
            return total

        plane()
        for k in (0, HALF):
            result = apply([cos_ref[c, k] for c in range(6)], k)
            for c in range(6):
                cos_ref[c, k] = result[c]

        def mix(k, inner):
            even = [cos_ref[c, k] for c in range(6)]
            odd = [sin_ref[c, k - 1] for c in range(6)]
            ahead = apply([even[c] + odd[c] for c in range(6)], k)
            behind = apply([even[c] - odd[c] for c in range(6)], VOX_SIDE - k)
            for c in range(6):
                cos_ref[c, k] = ahead[c] + behind[c]
                sin_ref[c, k - 1] = ahead[c] - behind[c]
            return inner

        lax.fori_loop(1, HALF, mix, 0)
        plane()

        def backward(c, inner):
            even = cosine_line([cos_ref[c, k] for k in range(HALF + 1)])
            odd = sine_line([None] + [sin_ref[c, k - 1] for k in range(1, HALF)])
            eps[c, 0] = eps[c, 0] - even[0]
            eps[c, HALF] = eps[c, HALF] - even[HALF]
            for x in range(1, HALF):
                eps[c, x] = eps[c, x] - (even[x] + odd[x])
                eps[c, VOX_SIDE - x] = eps[c, VOX_SIDE - x] - (even[x] - odd[x])
            return inner

        lax.fori_loop(0, 6, backward, 0)
        return carry

    lax.fori_loop(0, SWEEPS, sweep, 0)
    valid = valid_ref[...] > 0.5

    def finish(x, totals):
        stress, shape, scale, gain = voxel_law([eps[c, x] for c in range(6)], state_ref, props_ref, x)
        for c in range(6):
            new_ref[c, x] = state_ref[c, x] + scale * shape[c]
        new_ref[6, x] = jnp.where(valid, state_ref[6, x] + gain, -1.0)
        return tuple(totals[c] + stress[c] for c in range(6))

    zero = jnp.zeros((rows, VOX_PLANE), jnp.float32)
    totals = lax.fori_loop(0, VOX_SIDE, finish, (zero,) * 6)
    for c in range(6):
        total = jnp.sum(totals[c], axis=1, keepdims=True) / VOX_SIDE**3
        mean_ref[c] = jnp.broadcast_to(total, mean_ref.shape[1:])


def micro_solve(states, strains, valid, moduli, tables):
    rows = states.shape[2]
    strain_rows = jnp.broadcast_to(strains[:, :, None], (6, rows, VOX_PLANE))
    valid_rows = jnp.broadcast_to(valid[:, None], (rows, VOX_PLANE))
    vmem = pl.BlockSpec(memory_space=pltpu.VMEM)
    cells = VOX_SIDE * rows * VOX_PLANE
    updated, mean = pl.pallas_call(
        solve_kernel,
        out_shape=(
            jax.ShapeDtypeStruct(states.shape, jnp.float32),
            jax.ShapeDtypeStruct((6, rows, 128), jnp.float32),
        ),
        in_specs=[vmem] * 6,
        out_specs=(vmem, vmem),
        scratch_shapes=[
            pltpu.VMEM((6, VOX_SIDE, rows, VOX_PLANE), jnp.float32),
            pltpu.VMEM((6, VOX_SIDE, rows, VOX_PLANE), jnp.float32),
            pltpu.VMEM((6, HALF + 1, rows, VOX_PLANE), jnp.float32),
            pltpu.VMEM((6, HALF - 1, rows, VOX_PLANE), jnp.float32),
        ],
        compiler_params=pltpu.CompilerParams(vmem_limit_bytes=24 * 2**20),
        cost_estimate=pl.CostEstimate(
            flops=SWEEPS * 2 * 3 * 2 * 6 * cells * VOX_PLANE,
            bytes_accessed=2 * 7 * cells * 4,
            transcendentals=SWEEPS * cells,
        ),
    )(strain_rows, valid_rows, states, moduli, *tables)
    return updated, mean[:, :, 0]


def strain_tensor(disp_el, grad_el):
    products = [[jnp.sum(disp_el[i] * grad_el[j], axis=0) for j in range(3)] for i in range(3)]
    return jnp.stack(
        [
            products[0][0],
            products[1][1],
            products[2][2],
            0.5 * (products[1][2] + products[2][1]),
            0.5 * (products[0][2] + products[2][0]),
            0.5 * (products[0][1] + products[1][0]),
        ]
    )


def full_tensor(voigt):
    return [
        [voigt[0], voigt[5], voigt[4]],
        [voigt[5], voigt[1], voigt[3]],
        [voigt[4], voigt[3], voigt[2]],
    ]


def nodal_forces(stress, grad_el, volume):
    tensor = full_tensor(stress)
    return jnp.stack(
        [
            volume
            * (tensor[i][0] * grad_el[0] + tensor[i][1] * grad_el[1] + tensor[i][2] * grad_el[2])
            for i in range(3)
        ]
    )


def elastic_stress(strain, moduli):
    lame_first = moduli[0]
    shear_mod = moduli[1]
    trace = strain[0] + strain[1] + strain[2]
    return jnp.stack(
        [lame_first * trace + 2.0 * shear_mod * strain[c] for c in range(3)]
        + [2.0 * shear_mod * strain[c] for c in range(3, 6)]
    )


def local(
    displacement,
    load,
    conn,
    halo_list,
    grad_ops,
    volume,
    elastic_moduli,
    plastic_mask,
    new_owner,
    state,
    micro_moduli,
):
    groups = lax.axis_size("macro")
    ranks = lax.axis_size("vox")
    me = lax.axis_index("vox")
    own_nodes = displacement.shape[1]
    elements = conn.shape[1]
    thickness = state.shape[2]
    per_rank = groups // ranks
    tables = (jnp.asarray(green_tables()), plane_tables())
    moduli = jnp.transpose(gather_vox(micro_moduli), (1, 0, 2, 3)).reshape(4, VOX_SIDE, VOX_PLANE)
    node_ids = jnp.arange(own_nodes, dtype=jnp.int32)
    halo_match = (halo_list[:, None] == node_ids[None, :]).astype(jnp.float32)
    halo_out = jnp.dot(displacement, halo_match.T, precision=FULL_PREC)
    halo_disp = shifted(halo_out, "macro", 1)
    local_disp = jnp.concatenate([displacement, halo_disp], axis=1)
    all_ids = jnp.arange(local_disp.shape[1], dtype=jnp.int32)
    node_match = (conn[:, :, None] == all_ids[None, None, :]).astype(jnp.float32)
    disp_el = jnp.einsum("in,aen->iae", local_disp, node_match, precision=FULL_PREC)
    strain = strain_tensor(disp_el, grad_ops)
    plastic = plastic_mask == 1
    point_ids = jnp.arange(elements, dtype=jnp.int32)
    same_owner = (
        (new_owner[:, None] == new_owner[None, :])
        & plastic[:, None]
        & plastic[None, :]
        & (point_ids[None, :] < point_ids[:, None])
    )
    owner_rank = jnp.sum(same_owner.astype(jnp.int32), axis=1)
    capacity = (PLASTIC_MAX + groups - 1) // groups
    send_slot = jnp.where(plastic, owner_rank * groups + new_owner, -1)
    slot_ids = jnp.arange(groups * capacity, dtype=jnp.int32)
    slot_match = slot_ids[:, None] == send_slot[None, :]
    match_float = slot_match.astype(jnp.float32)
    slot_valid = jnp.sum(match_float, axis=1)
    slot_source = jnp.sum(jnp.where(slot_match, point_ids[None, :], 0), axis=1)
    slot_strain = jnp.dot(strain, match_float.T, precision=FULL_PREC)
    moved, means = [], []
    for chunk in range(capacity):
        base = chunk * groups
        picked = state[:, slot_source[base : base + groups]]
        picked = picked.reshape(7, ranks, per_rank, thickness, VOX_PLANE)
        picked = jnp.swapaxes(picked, 2, 3)
        whole = lax.all_to_all(picked, "vox", split_axis=1, concat_axis=1, tiled=True)
        whole = whole.reshape(7, VOX_SIDE, per_rank, VOX_PLANE)
        mine = base + me * per_rank
        updated, mean = micro_solve(
            whole,
            lax.dynamic_slice_in_dim(slot_strain, mine, per_rank, 1),
            lax.dynamic_slice_in_dim(slot_valid, mine, per_rank, 0),
            moduli,
            tables,
        )
        means.append(mean)
        slabs = updated.reshape(7, ranks, thickness, per_rank, VOX_PLANE)
        slabs = lax.all_to_all(slabs, "vox", split_axis=1, concat_axis=1, tiled=True)
        slabs = jnp.swapaxes(slabs, 2, 3).reshape(7, groups, thickness, VOX_PLANE)
        moved.append(lax.all_to_all(slabs, "macro", split_axis=1, concat_axis=1, tiled=True))
    averaged = jnp.moveaxis(gather_vox(jnp.stack(means, axis=1)), 0, 2)
    averaged = averaged.reshape(6, capacity * groups)
    stress_plastic = jnp.dot(averaged, match_float, precision=FULL_PREC)
    stress = jnp.where(plastic[None, :], stress_plastic, elastic_stress(strain, elastic_moduli))
    forces = nodal_forces(stress, grad_ops, volume)
    assembled = jnp.einsum("iae,aen->in", forces, node_match, precision=FULL_PREC)
    returned_force = shifted(assembled[:, own_nodes:], "macro", -1)
    residual = (
        assembled[:, :own_nodes] + jnp.dot(returned_force, halo_match, precision=FULL_PREC) - load
    )
    arrived = jnp.concatenate(moved, axis=1)
    full = jnp.stack([block[6, :, 0, 0] >= 0.0 for block in moved], axis=1).reshape(-1)
    position = jnp.cumsum(full.astype(jnp.int32)) - 1
    wanted = jnp.arange(RECV_AGG, dtype=jnp.int32)
    places = jnp.arange(groups * capacity, dtype=jnp.int32)
    places = (places % capacity) * groups + places // capacity
    chosen = jnp.sum(
        jnp.where((wanted[:, None] == position[None, :]) & full[None, :], places[None, :], 0), axis=1
    )
    return (residual, arrived[:, chosen])


def solution(mesh):
    return jax.shard_map(
        local,
        mesh=mesh,
        in_specs=(
            P(None, "macro"),
            P(None, "macro"),
            P(None, "macro"),
            P("macro"),
            P(None, None, "macro"),
            P("macro"),
            P(None, "macro"),
            P("macro"),
            P("macro"),
            P(None, "macro", "vox", None),
            P(None, "vox", None),
        ),
        out_specs=(P(None, "macro"), P(None, "macro", "vox", None)),
        check_vma=False,
    )
```

time: 248 us -> 200 us (0.81)
  matrix products: 74.8 us -> 2.64 us
  Pallas kernels: 0 us -> 31.8 us
  other arithmetic: 30.3 us -> 6.09 us
  waiting for transfers between devices: 54.8 us -> 78 us
  blocking collectives: 22.3 us -> 0 us
  local copies, waits for them, and re-layouts: 18.1 us -> 28 us
  starting transfers between devices: 41.4 us -> 48.8 us
    dot_general x50 -> x4, matrix products: 73.8 us -> 1.59 us  [the longest x1 0.89 us: local(): halo_out = jnp.dot(displacement, halo_match.T, precision=FULL_PREC)]
    all_to_all x6 -> x9, waiting for transfers between devices: 21.8 us -> 67.1 us  [the longest x3 41.9 us: local(): lax.all_to_all(slabs, 'macro', split_axis=1, concat_axis=1, tiled=True)]
    pallas_call x0 -> x3, Pallas kernels: none -> 31.8 us  [micro_solve(): pl.pallas_call(solve_kernel, out_shape=(jax.ShapeDtypeStruct(states.shape...]
    all_gather x2 -> x0, blocking collectives: 22.3 us -> none  [the longest x1 17.9 us: micro_solve(): full_moduli = lax.all_gather(moduli_slab, 'vox', axis=1, tiled=True)]
    ppermute x2 -> x4, waiting for transfers between devices: 33 us -> 10.9 us  [shifted(): return lax.ppermute(block, axis, route)]
    mul x9 -> x0, other arithmetic: 13.1 us -> none  [the longest x1 5.64 us: green_apply(): freq_z * wave_z]
    unnamed x52 -> x0, other arithmetic: 7.66 us -> none
    ppermute x2 -> x4, starting transfers between devices: 0.64 us -> 7.59 us  [shifted(): return lax.ppermute(block, axis, route)]
  transfers between devices with their start and end apart: 8 -> 13, of which waited for: 6 -> 8; matrix products, arithmetic and copies ran while one was open for 15% -> 14% of each run, Pallas kernels for 0% -> 16%
where the time goes in v1:
time: 200 us; the launch traced here: 196 us
  waiting for transfers between devices  78 us (39%)
  starting transfers between devices  48.8 us (24%)
  Pallas kernels  31.8 us (16%)
  local copies, waits for them, and re-layouts  28 us (14%)
  other arithmetic  6.09 us (3%)
  matrix products  2.64 us (1%)
    all_to_all x3, waiting for transfers between devices, local(): lax.all_to_all(slabs, 'macro', split_axis=1, concat_axis=1, tiled=True)  41.9 us
    pallas_call x3, Pallas kernels, micro_solve(): pl.pallas_call(solve_kernel, out_shape=(jax.ShapeDtypeStruct(states.shape...  31.8 us
    all_to_all x3, starting transfers between devices, local(): lax.all_to_all(slabs, 'macro', split_axis=1, concat_axis=1, tiled=True)  18.1 us
    all_to_all x3, waiting for transfers between devices, local(): lax.all_to_all(picked, 'vox', split_axis=1, concat_axis=1, tiled=True)  15.5 us
    all_to_all x3, starting transfers between devices, local(): lax.all_to_all(picked, 'vox', split_axis=1, concat_axis=1, tiled=True)  11.7 us
    all_to_all x3, starting transfers between devices, local(): lax.all_to_all(slabs, 'vox', split_axis=1, concat_axis=1, tiled=True)  11.5 us
    ppermute x4, waiting for transfers between devices, shifted(): return lax.ppermute(block, axis, route)  10.9 us
    all_to_all x3, waiting for transfers between devices, local(): lax.all_to_all(slabs, 'vox', split_axis=1, concat_axis=1, tiled=True)  9.69 us
  transfers between devices with their start and end apart: 13, of which 8 were waited for; matrix products, arithmetic and copies ran while one was open for 14% of the time, Pallas kernels for 16%

profile of v1, /device:TPU:0, one launch (start us, length us, event | category | flops | bytes accessed | tf_op | source)
XLA Modules:
  0.0 196.5 jit_solution(4937260180583641283)
XLA Ops:
  4.5 2.7 %gather_fusion.2 = f32[16,7,8,256]{3,2,1,0:T(8,128)S(1)} fusion(f32[7,64,8,256]{3,2,1,0:T(8,128)} %param.23, s32[1024]{0:T(1024)S(1)} %get-tuple-element.84), kind=kCustom, calls=%fused_computation.2 | custom fusion | bytes 1835072 | tf_op jit(solution)/shard_map/gather | solution.py:374
  8.4 3.8 %all-to-all-start.2 = ((f32[7,2,8,8,256]{4,3,2,0,1:T(8,128)}), f32[7,2,8,8,256]{4,3,2,0,1:T(8,128)S(1)}, u32[]{:S(2)}, u32[]{:S(2)}) async-start(f32[7,2,8,8,256]{4,3,2,0,1:T(8,128)} %copy.175), calls=%async_computation.2 | async-start | bytes 1835008 | tf_op jit(solution)/shard_map/all_to_all | solution.py:377
  12.1 2.4 %collective-permute-start.1 = (f32[4,8,256]{2,1,0:T(8,128)S(1)}, f32[4,8,256]{2,1,0:T(8,128)S(1)}, u32[]{:S(2)}, u32[]{:S(2)}) collective-permute-start(f32[4,8,256]{2,1,0:T(8,128)S(1)} %copy-done.8), channel_id=1, source_target_pairs={{1,0},{0,1},{3,2},{2,3},{5,4},{4,5},{7,6},{6,7},{9,8},{8,9},{11,10... | collective-permute-start | bytes 98312 | tf_op jit(solution)/shard_map/ppermute | solution.py:32
  14.6 2.6 %gather_fusion.1 = f32[16,7,8,256]{3,2,1,0:T(8,128)S(1)} fusion(f32[7,64,8,256]{3,2,1,0:T(8,128)} %param.23, s32[1024]{0:T(1024)S(1)} %get-tuple-element.85), kind=kCustom, calls=%fused_computation.1 | custom fusion | bytes 1835072 | tf_op jit(solution)/shard_map/gather | solution.py:374
  18.7 2.7 %gather_fusion = f32[16,7,8,256]{3,2,1,0:T(8,128)S(1)} fusion(f32[7,64,8,256]{3,2,1,0:T(8,128)} %param.23, s32[1024]{0:T(1024)S(1)} %pad_clamp_fusion.3), kind=kCustom, calls=%fused_computation | custom fusion | bytes 1835072 | tf_op jit(solution)/shard_map/gather | solution.py:374
  24.9 3.6 %all-to-all-start.1 = ((f32[7,2,8,8,256]{4,3,2,0,1:T(8,128)}), f32[7,2,8,8,256]{4,3,2,0,1:T(8,128)S(1)}, u32[]{:S(2)}, u32[]{:S(2)}) async-start(f32[7,2,8,8,256]{4,3,2,0,1:T(8,128)} %copy.172), calls=%async_computation.1 | async-start | bytes 1835008 | tf_op jit(solution)/shard_map/all_to_all | solution.py:377
  28.7 13.0 %all-to-all-done.1 = f32[7,2,8,8,256]{4,3,2,0,1:T(8,128)S(1)} async-done(((f32[7,2,8,8,256]{4,3,2,0,1:T(8,128)}), f32[7,2,8,8,256]{4,3,2,0,1:T(8,128)S(1)}, u32[]{:S(2)}, u32[]{:S(2)}) %all-to-all-start.1) | async-done | bytes 917536 | tf_op jit(solution)/shard_map/all_to_all | solution.py:377
  41.7 4.4 %all-to-all-start = ((f32[7,2,8,8,256]{4,3,2,0,1:T(8,128)}), f32[7,2,8,8,256]{4,3,2,0,1:T(8,128)}, u32[]{:S(2)}, u32[]{:S(2)}) async-start(f32[7,2,8,8,256]{4,3,2,0,1:T(8,128)} %copy.168), calls=%async_computation | async-start | bytes 1835008 | tf_op jit(solution)/shard_map/all_to_all | solution.py:377
  46.3 10.6 %shard_map.151 = (f32[7,16,8,256]{3,2,1,0:T(8,128)S(1)}, f32[6,8,128]{2,1,0:T(8,128)S(1)}) custom-call(f32[6,8,256]{2,1,0:T(8,128)S(1)} %broadcast_in_dim.60.strain_ref, f32[8,256]{1,0:T(8,128)S(1)} %broadcast_in_dim.61.valid_ref, f32[7,16,8,256]{3,2,1,0:T(8,128)S(1)} %bitcast.99, f32[4,16,256]{2,1,0:T(8,128)S(1)} %copy_bitcast_fusion.props_ref, ...), custom_call_target="tpu_custom_call" | custom-call | flops 2415919104 | bytes 1835008 | tf_op jit(solution)/shard_map/pallas_call | solution.py:256
  58.9 4.4 %all-to-all-start.7 = ((f32[7,2,8,8,256]{4,2,3,0,1:T(8,128)}), f32[7,2,8,8,256]{4,2,3,0,1:T(8,128)}, u32[]{:S(2)}, u32[]{:S(2)}) async-start(f32[7,2,8,8,256]{4,2,3,0,1:T(8,128)} %copy.185), calls=%async_computation.7 | async-start | bytes 1835008 | tf_op jit(solution)/shard_map/all_to_all | solution.py:389
  63.5 10.6 %shard_map.150 = (f32[7,16,8,256]{3,2,1,0:T(8,128)S(1)}, f32[6,8,128]{2,1,0:T(8,128)S(1)}) custom-call(f32[6,8,256]{2,1,0:T(8,128)S(1)} %broadcast_in_dim.57.strain_ref, f32[8,256]{1,0:T(8,128)S(1)} %broadcast_in_dim.58.valid_ref, f32[7,16,8,256]{3,2,1,0:T(8,128)S(1)} %bitcast.100, f32[4,16,256]{2,1,0:T(8,128)S(1)} %copy_bitcast_fusion.props_ref, ...), custom_call_target="tpu_custom_call" | custom-call | flops 2415919104 | bytes 1835008 | tf_op jit(solution)/shard_map/pallas_call | solution.py:256
  75.4 3.6 %all-to-all-start.5 = ((f32[7,2,8,8,256]{4,2,3,0,1:T(8,128)}), f32[7,2,8,8,256]{4,2,3,0,1:T(8,128)S(1)}, u32[]{:S(2)}, u32[]{:S(2)}) async-start(f32[7,2,8,8,256]{4,2,3,0,1:T(8,128)} %copy.182), calls=%async_computation.5 | async-start | bytes 1835008 | tf_op jit(solution)/shard_map/all_to_all | solution.py:389
  80.4 10.6 %shard_map.149 = (f32[7,16,8,256]{3,2,1,0:T(8,128)S(1)}, f32[6,8,128]{2,1,0:T(8,128)S(1)}) custom-call(f32[6,8,256]{2,1,0:T(8,128)S(1)} %broadcast_in_dim.49.strain_ref, f32[8,256]{1,0:T(8,128)S(1)} %broadcast_in_dim.50.valid_ref, f32[7,16,8,256]{3,2,1,0:T(8,128)S(1)} %bitcast.97, f32[4,16,256]{2,1,0:T(8,128)S(1)} %copy_bitcast_fusion.props_ref, ...), custom_call_target="tpu_custom_call" | custom-call | flops 2415919104 | bytes 1835008 | tf_op jit(solution)/shard_map/pallas_call | solution.py:256
  93.1 3.6 %all-to-all-start.3 = ((f32[7,2,8,8,256]{4,2,3,0,1:T(8,128)}), f32[7,2,8,8,256]{4,2,3,0,1:T(8,128)S(1)}, u32[]{:S(2)}, u32[]{:S(2)}) async-start(f32[7,2,8,8,256]{4,2,3,0,1:T(8,128)} %copy.179), calls=%async_computation.3 | async-start | bytes 1835008 | tf_op jit(solution)/shard_map/all_to_all | solution.py:389
  99.1 9.6 %all-to-all-done.3 = f32[7,2,8,8,256]{4,2,3,0,1:T(8,128)S(1)} async-done(((f32[7,2,8,8,256]{4,2,3,0,1:T(8,128)}), f32[7,2,8,8,256]{4,2,3,0,1:T(8,128)S(1)}, u32[]{:S(2)}, u32[]{:S(2)}) %all-to-all-start.3) | async-done | bytes 917536 | tf_op jit(solution)/shard_map/all_to_all | solution.py:389
  108.7 5.9 %all-to-all-start.8 = ((f32[7,16,8,256]{3,2,0,1:T(8,128)}), f32[7,16,8,256]{3,2,0,1:T(8,128)S(1)}, u32[]{:S(2)}, u32[]{:S(2)}) async-start(f32[7,16,8,256]{3,2,0,1:T(8,128)} %copy.187), calls=%async_computation.8 | async-start | bytes 1835008 | tf_op jit(solution)/shard_map/all_to_all | solution.py:391
  115.7 19.7 %all-to-all-done.8 = f32[7,16,8,256]{3,2,0,1:T(8,128)S(1)} async-done(((f32[7,16,8,256]{3,2,0,1:T(8,128)}), f32[7,16,8,256]{3,2,0,1:T(8,128)S(1)}, u32[]{:S(2)}, u32[]{:S(2)}) %all-to-all-start.8) | async-done | bytes 917536 | tf_op jit(solution)/shard_map/all_to_all | solution.py:391
  135.4 6.1 %all-to-all-start.6 = ((f32[7,16,8,256]{3,2,0,1:T(8,128)}), f32[7,16,8,256]{3,2,0,1:T(8,128)S(1)}, u32[]{:S(2)}, u32[]{:S(2)}) async-start(f32[7,16,8,256]{3,2,0,1:T(8,128)} %copy.184), calls=%async_computation.6 | async-start | bytes 1835008 | tf_op jit(solution)/shard_map/all_to_all | solution.py:391
  143.3 18.9 %all-to-all-done.6 = f32[7,16,8,256]{3,2,0,1:T(8,128)S(1)} async-done(((f32[7,16,8,256]{3,2,0,1:T(8,128)}), f32[7,16,8,256]{3,2,0,1:T(8,128)S(1)}, u32[]{:S(2)}, u32[]{:S(2)}) %all-to-all-start.6) | async-done | bytes 917536 | tf_op jit(solution)/shard_map/all_to_all | solution.py:391
  162.3 6.1 %all-to-all-start.4 = ((f32[7,16,8,256]{3,2,0,1:T(8,128)}), f32[7,16,8,256]{3,2,0,1:T(8,128)S(1)}, u32[]{:S(2)}, u32[]{:S(2)}) async-start(f32[7,16,8,256]{3,2,0,1:T(8,128)} %copy.181), calls=%async_computation.4 | async-start | bytes 1835008 | tf_op jit(solution)/shard_map/all_to_all | solution.py:391
  169.1 4.4 %collective-permute-start.3 = (f32[3,16]{1,0:T(4,128)S(1)}, f32[3,16]{1,0:T(4,128)S(1)}, u32[]{:S(2)}, u32[]{:S(2)}) collective-permute-start(f32[3,16]{1,0:T(4,128)S(1)} %slice.120), channel_id=1, source_target_pairs={{2,0},{4,2},{6,4},{8,6},{10,8},{12,10},{14,12},{16,14},{18,16},{20... | collective-permute-start | bytes 584 | tf_op jit(solution)/shard_map/ppermute | solution.py:32
  173.4 10.9 %collective-permute-done.3 = f32[3,16]{1,0:T(4,128)S(1)} collective-permute-done((f32[3,16]{1,0:T(4,128)S(1)}, f32[3,16]{1,0:T(4,128)S(1)}, u32[]{:S(2)}, u32[]{:S(2)}) %collective-permute-start.3) | collective-permute-done | bytes 224 | tf_op jit(solution)/shard_map/ppermute | solution.py:32
  185.9 3.2 %all-to-all-done.4 = f32[7,16,8,256]{3,2,0,1:T(8,128)S(1)} async-done(((f32[7,16,8,256]{3,2,0,1:T(8,128)}), f32[7,16,8,256]{3,2,0,1:T(8,128)S(1)}, u32[]{:S(2)}, u32[]{:S(2)}) %all-to-all-start.4) | async-done | bytes 917536 | tf_op jit(solution)/shard_map/all_to_all | solution.py:391
  193.9 2.5 %copy.191 = f32[7,24,8,256]{3,2,1,0:T(8,128)} copy(f32[7,24,8,256]{3,2,0,1:T(8,128)} %bitcast.103) | data formatting | bytes 2752512
  (115 shorter events, 29.7 us)
Async XLA Ops:
  1.5 21.0 %collective-permute-start = (f32[3,16]{1,0:T(4,128)S(1)}, f32[3,16]{1,0:T(4,128)S(1)}, u32[]{:S(2)}, u32[]{:S(2)}) collective-permute-start(f32[3,16]{1,0:T(4,128)S(1)} %convolution_bitcast_fusion.1), channel_id=1, source_target_pairs={{30,0},{0,2},{2,4},{4,6},{6,8},{8,10},{10,12},{12,14},{14,16},{16,... | collective-permute-start | bytes 584 | tf_op jit(solution)/shard_map/ppermute | solution.py:32
  4.5 7.7 %copy-start.8 = (f32[4,8,256]{2,1,0:T(8,128)S(1)}, f32[4,8,256]{2,1,0:T(8,128)}, u32[]{:S(2)}) copy-start(f32[4,8,256]{2,1,0:T(8,128)} %param.24) | copy-start | bytes 98308
  8.4 16.5 %all-to-all-start.2 = ((f32[7,2,8,8,256]{4,3,2,0,1:T(8,128)}), f32[7,2,8,8,256]{4,3,2,0,1:T(8,128)S(1)}, u32[]{:S(2)}, u32[]{:S(2)}) async-start(f32[7,2,8,8,256]{4,3,2,0,1:T(8,128)} %copy.175), calls=%async_computation.2 | async-start | bytes 1835008 | tf_op jit(solution)/shard_map/all_to_all | solution.py:377
  12.1 33.9 %collective-permute-start.1 = (f32[4,8,256]{2,1,0:T(8,128)S(1)}, f32[4,8,256]{2,1,0:T(8,128)S(1)}, u32[]{:S(2)}, u32[]{:S(2)}) collective-permute-start(f32[4,8,256]{2,1,0:T(8,128)S(1)} %copy-done.8), channel_id=1, source_target_pairs={{1,0},{0,1},{3,2},{2,3},{5,4},{4,5},{7,6},{6,7},{9,8},{8,9},{11,10... | collective-permute-start | bytes 98312 | tf_op jit(solution)/shard_map/ppermute | solution.py:32
  17.3 5.8 %copy-start.7 = (f32[3,8,64]{2,1,0:T(8,128)S(1)}, f32[3,8,64]{2,1,0:T(8,128)}, u32[]{:S(2)}) copy-start(f32[3,8,64]{2,1,0:T(8,128)} %param.18) | copy-start | bytes 18436
  18.7 9.8 %copy-start.9 = (f32[2,64]{1,0:T(2,128)S(1)}, f32[2,64]{1,0:T(2,128)}, u32[]{:S(2)}) copy-start(f32[2,64]{1,0:T(2,128)} %param.20) | copy-start | bytes 1540
  23.1 23.2 %copy-start = (bf16[4,256,256]{2,1,0:T(8,128)(2,1)S(1)}, bf16[4,256,256]{2,1,0:T(8,128)(2,1)}, u32[]{:S(2)}) copy-start(bf16[4,256,256]{2,1,0:T(8,128)(2,1)} %constant.78.plane_ref) | copy-start | bytes 1572868
  23.1 23.2 %copy-start.1 = (f32[21,16,256]{2,1,0:T(8,128)S(1)}, f32[21,16,256]{2,1,0:T(8,128)}, u32[]{:S(2)}) copy-start(f32[21,16,256]{2,1,0:T(8,128)} %constant.63.clone.green_ref) | copy-start | bytes 1032196
  24.9 16.8 %all-to-all-start.1 = ((f32[7,2,8,8,256]{4,3,2,0,1:T(8,128)}), f32[7,2,8,8,256]{4,3,2,0,1:T(8,128)S(1)}, u32[]{:S(2)}, u32[]{:S(2)}) async-start(f32[7,2,8,8,256]{4,3,2,0,1:T(8,128)} %copy.172), calls=%async_computation.1 | async-start | bytes 1835008 | tf_op jit(solution)/shard_map/all_to_all | solution.py:377
  41.7 17.3 %all-to-all-start = ((f32[7,2,8,8,256]{4,3,2,0,1:T(8,128)}), f32[7,2,8,8,256]{4,3,2,0,1:T(8,128)}, u32[]{:S(2)}, u32[]{:S(2)}) async-start(f32[7,2,8,8,256]{4,3,2,0,1:T(8,128)} %copy.168), calls=%async_computation | async-start | bytes 1835008 | tf_op jit(solution)/shard_map/all_to_all | solution.py:377
  58.9 16.5 %all-to-all-start.7 = ((f32[7,2,8,8,256]{4,2,3,0,1:T(8,128)}), f32[7,2,8,8,256]{4,2,3,0,1:T(8,128)}, u32[]{:S(2)}, u32[]{:S(2)}) async-start(f32[7,2,8,8,256]{4,2,3,0,1:T(8,128)} %copy.185), calls=%async_computation.7 | async-start | bytes 1835008 | tf_op jit(solution)/shard_map/all_to_all | solution.py:389
  75.4 16.8 %all-to-all-start.5 = ((f32[7,2,8,8,256]{4,2,3,0,1:T(8,128)}), f32[7,2,8,8,256]{4,2,3,0,1:T(8,128)S(1)}, u32[]{:S(2)}, u32[]{:S(2)}) async-start(f32[7,2,8,8,256]{4,2,3,0,1:T(8,128)} %copy.182), calls=%async_computation.5 | async-start | bytes 1835008 | tf_op jit(solution)/shard_map/all_to_all | solution.py:389
  93.1 15.5 %all-to-all-start.3 = ((f32[7,2,8,8,256]{4,2,3,0,1:T(8,128)}), f32[7,2,8,8,256]{4,2,3,0,1:T(8,128)S(1)}, u32[]{:S(2)}, u32[]{:S(2)}) async-start(f32[7,2,8,8,256]{4,2,3,0,1:T(8,128)} %copy.179), calls=%async_computation.3 | async-start | bytes 1835008 | tf_op jit(solution)/shard_map/all_to_all | solution.py:389
  96.7 17.9 %copy-start.6 = (f32[7,2,8,8,256]{4,2,3,0,1:T(8,128)S(1)}, f32[7,2,8,8,256]{4,2,3,0,1:T(8,128)}, u32[]{:S(2)}) copy-start(f32[7,2,8,8,256]{4,2,3,0,1:T(8,128)} %copy-done.5) | copy-start | bytes 2752516
  108.7 26.7 %all-to-all-start.8 = ((f32[7,16,8,256]{3,2,0,1:T(8,128)}), f32[7,16,8,256]{3,2,0,1:T(8,128)S(1)}, u32[]{:S(2)}, u32[]{:S(2)}) async-start(f32[7,16,8,256]{3,2,0,1:T(8,128)} %copy.187), calls=%async_computation.8 | async-start | bytes 1835008 | tf_op jit(solution)/shard_map/all_to_all | solution.py:391
  135.4 49.7 %copy-start.2 = (f32[7,16,8,256]{3,2,0,1:T(8,128)}, f32[7,16,8,256]{3,2,0,1:T(8,128)S(1)}, u32[]{:S(2)}) copy-start(f32[7,16,8,256]{3,2,0,1:T(8,128)S(1)} %all-to-all-done.8) | copy-start | bytes 2752516
  135.4 26.9 %all-to-all-start.6 = ((f32[7,16,8,256]{3,2,0,1:T(8,128)}), f32[7,16,8,256]{3,2,0,1:T(8,128)S(1)}, u32[]{:S(2)}, u32[]{:S(2)}) async-start(f32[7,16,8,256]{3,2,0,1:T(8,128)} %copy.184), calls=%async_computation.6 | async-start | bytes 1835008 | tf_op jit(solution)/shard_map/all_to_all | solution.py:391
  141.8 26.6 %collective-permute-start.2 = (f32[6,3,8]{2,1,0:T(4,128)S(1)}, f32[6,3,8]{2,1,0:T(4,128)S(1)}, u32[]{:S(2)}, u32[]{:S(2)}) collective-permute-start(f32[6,3,8]{2,1,0:T(4,128)S(1)} %get-tuple-element.60), channel_id=1, source_target_pairs={{1,0},{0,1},{3,2},{2,3},{5,4},{4,5},{7,6},{6,7},{9,8},{8,9},{11,10... | collective-permute-start | bytes 1736 | tf_op jit(solution)/shard_map/ppermute | solution.py:32
  142.2 26.5 %copy-start.10 = (f32[64]{0:T(128)S(1)}, f32[64]{0:T(128)}, u32[]{:S(2)}) copy-start(f32[64]{0:T(128)} %param.19) | copy-start | bytes 772
  142.2 42.2 %copy-start.13 = (f32[3,64]{1,0:T(4,128)S(1)}, f32[3,64]{1,0:T(4,128)}, u32[]{:S(2)}) copy-start(f32[3,64]{1,0:T(4,128)} %param.15) | copy-start | bytes 2308
  142.2 42.2 %copy-start.14 = (s32[16]{0:T(128)S(1)}, s32[16]{0:T(128)}, u32[]{:S(2)}) copy-start(s32[16]{0:T(128)} %param.17) | copy-start | bytes 196
  162.3 28.0 %copy-start.3 = (f32[7,16,8,256]{3,2,0,1:T(8,128)}, f32[7,16,8,256]{3,2,0,1:T(8,128)S(1)}, u32[]{:S(2)}) copy-start(f32[7,16,8,256]{3,2,0,1:T(8,128)S(1)} %all-to-all-done.6) | copy-start | bytes 2752516
  162.3 26.9 %all-to-all-start.4 = ((f32[7,16,8,256]{3,2,0,1:T(8,128)}), f32[7,16,8,256]{3,2,0,1:T(8,128)S(1)}, u32[]{:S(2)}, u32[]{:S(2)}) async-start(f32[7,16,8,256]{3,2,0,1:T(8,128)} %copy.181), calls=%async_computation.4 | async-start | bytes 1835008 | tf_op jit(solution)/shard_map/all_to_all | solution.py:391
  169.1 15.3 %collective-permute-start.3 = (f32[3,16]{1,0:T(4,128)S(1)}, f32[3,16]{1,0:T(4,128)S(1)}, u32[]{:S(2)}, u32[]{:S(2)}) collective-permute-start(f32[3,16]{1,0:T(4,128)S(1)} %slice.120), channel_id=1, source_target_pairs={{2,0},{4,2},{6,4},{8,6},{10,8},{12,10},{14,12},{16,14},{18,16},{20... | collective-permute-start | bytes 584 | tf_op jit(solution)/shard_map/ppermute | solution.py:32
  (4 other events, 12.5 us)

commit v2 on v1

--- a/solution.py
+++ b/solution.py
@@ -32,13 +32,17 @@
     return lax.ppermute(block, axis, route)
 
 
-def gather_vox(block):
-    ranks = lax.axis_size("vox")
-    pieces = jnp.stack([block] + [shifted(block, "vox", d) for d in range(1, ranks)])
+def by_rank(pieces, axis):
+    ranks = len(pieces)
     me = lax.axis_index("vox")
     if ranks == 2:
-        return jnp.where(me == 0, pieces, pieces[::-1])
-    return pieces[(me - jnp.arange(ranks)) % ranks]
+        straight = jnp.concatenate(pieces, axis=axis)
+        return jnp.where(me == 0, straight, jnp.concatenate(pieces[::-1], axis=axis))
+    order = (me - jnp.arange(ranks)) % ranks
+    stacked = jnp.moveaxis(jnp.stack(pieces)[order], 0, axis)
+    shape = list(pieces[0].shape)
+    shape[axis] *= ranks
+    return stacked.reshape(shape)
 
 
 def green_tables():
@@ -131,21 +135,21 @@
     return dot(high, table_ref[first]) + (dot(high, table_ref[first + 1]) + dot(low, table_ref[first]))
 
 
-def voxel_law(strain, state_ref, props_ref, x):
+def voxel_law(strain, state_ref, props_ref, place, x):
     row = pl.ds(x, 1)
     lam, mu = props_ref[0, row, :], props_ref[1, row, :]
     yield_base, harden = props_ref[2, row, :], props_ref[3, row, :]
     two_mu, three_mu = 2.0 * mu, 3.0 * mu
     stiff_inv = 1.0 / (three_mu + harden)
     bulk = lam + two_mu * (1.0 / 3.0)
-    elastic = [strain[c] - state_ref[c, x] for c in range(6)]
+    elastic = [strain[c] - state_ref[c, place] for c in range(6)]
     trace = elastic[0] + elastic[1] + elastic[2]
     third = trace * (1.0 / 3.0)
     shape = [elastic[c] - third for c in range(3)] + elastic[3:]
     normal = shape[0] * shape[0] + shape[1] * shape[1] + shape[2] * shape[2]
     shear = shape[3] * shape[3] + shape[4] * shape[4] + shape[5] * shape[5]
     equivalent = two_mu * jnp.sqrt(1.5 * (normal + 2.0 * shear))
-    strength = yield_base + harden * state_ref[6, x]
+    strength = yield_base + harden * state_ref[6, place]
     gain = jnp.maximum(equivalent - strength, 0.0) * stiff_inv
     factor = gain / jnp.maximum(equivalent, strength)
     keep = two_mu * (1.0 - three_mu * factor)
@@ -154,20 +158,26 @@
     return stress, shape, (1.5 * two_mu) * factor, gain
 
 
-def solve_kernel(strain_ref, valid_ref, state_ref, props_ref, green_ref, plane_ref, new_ref, mean_ref, eps, work, cos_ref, sin_ref):
-    rows = state_ref.shape[2]
+def solve_kernel(ranks, strain_ref, valid_ref, props_ref, green_ref, plane_ref, *refs):
+    state_refs, new_refs = refs[:ranks], refs[ranks : 2 * ranks]
+    mean_ref, eps, work, cos_ref, sin_ref = refs[2 * ranks :]
+    thickness, rows = state_refs[0].shape[1:3]
     for c in range(6):
         start = jnp.broadcast_to(strain_ref[c], (VOX_SIDE, rows, VOX_PLANE))
         eps[c] = start
 
     def sweep(step, carry):
-        def law(x, inner):
-            stress, _, _, _ = voxel_law([eps[c, x] for c in range(6)], state_ref, props_ref, x)
-            for c in range(6):
-                work[c, x] = stress[c]
-            return inner
-
-        lax.fori_loop(0, VOX_SIDE, law, 0)
+        for slab, state_ref in enumerate(state_refs):
+
+            def law(place, inner, slab=slab, state_ref=state_ref):
+                x = slab * thickness + place
+                strain = [eps[c, x] for c in range(6)]
+                stress = voxel_law(strain, state_ref, props_ref, place, x)[0]
+                for c in range(6):
+                    work[c, x] = stress[c]
+                return inner
+
+            lax.fori_loop(0, thickness, law, 0)
 
         def forward(c, inner):
             field = [work[c, x] for x in range(VOX_SIDE)]
@@ -233,34 +243,38 @@
     lax.fori_loop(0, SWEEPS, sweep, 0)
     valid = valid_ref[...] > 0.5
 
-    def finish(x, totals):
-        stress, shape, scale, gain = voxel_law([eps[c, x] for c in range(6)], state_ref, props_ref, x)
-        for c in range(6):
-            new_ref[c, x] = state_ref[c, x] + scale * shape[c]
-        new_ref[6, x] = jnp.where(valid, state_ref[6, x] + gain, -1.0)
-        return tuple(totals[c] + stress[c] for c in range(6))
-
     zero = jnp.zeros((rows, VOX_PLANE), jnp.float32)
-    totals = lax.fori_loop(0, VOX_SIDE, finish, (zero,) * 6)
+    totals = (zero,) * 6
+    for slab, (state_ref, new_ref) in enumerate(zip(state_refs, new_refs)):
+
+        def finish(place, totals, slab=slab, state_ref=state_ref, new_ref=new_ref):
+            x = slab * thickness + place
+            strain = [eps[c, x] for c in range(6)]
+            stress, shape, scale, gain = voxel_law(strain, state_ref, props_ref, place, x)
+            for c in range(6):
+                new_ref[c, place] = state_ref[c, place] + scale * shape[c]
+            new_ref[6, place] = jnp.where(valid, state_ref[6, place] + gain, -1.0)
+            return tuple(totals[c] + stress[c] for c in range(6))
+
+        totals = lax.fori_loop(0, thickness, finish, totals)
     for c in range(6):
         total = jnp.sum(totals[c], axis=1, keepdims=True) / VOX_SIDE**3
         mean_ref[c] = jnp.broadcast_to(total, mean_ref.shape[1:])
 
 
-def micro_solve(states, strains, valid, moduli, tables):
-    rows = states.shape[2]
+def micro_solve(pieces, strains, valid, moduli, tables):
+    ranks = len(pieces)
+    rows = pieces[0].shape[2]
     strain_rows = jnp.broadcast_to(strains[:, :, None], (6, rows, VOX_PLANE))
     valid_rows = jnp.broadcast_to(valid[:, None], (rows, VOX_PLANE))
     vmem = pl.BlockSpec(memory_space=pltpu.VMEM)
     cells = VOX_SIDE * rows * VOX_PLANE
-    updated, mean = pl.pallas_call(
-        solve_kernel,
-        out_shape=(
-            jax.ShapeDtypeStruct(states.shape, jnp.float32),
-            jax.ShapeDtypeStruct((6, rows, 128), jnp.float32),
-        ),
-        in_specs=[vmem] * 6,
-        out_specs=(vmem, vmem),
+    results = pl.pallas_call(
+        functools.partial(solve_kernel, ranks),
+        out_shape=[jax.ShapeDtypeStruct(pieces[0].shape, jnp.float32)] * ranks
+        + [jax.ShapeDtypeStruct((6, rows, 128), jnp.float32)],
+        in_specs=[vmem] * (5 + ranks),
+        out_specs=[vmem] * (ranks + 1),
         scratch_shapes=[
             pltpu.VMEM((6, VOX_SIDE, rows, VOX_PLANE), jnp.float32),
             pltpu.VMEM((6, VOX_SIDE, rows, VOX_PLANE), jnp.float32),
@@ -273,8 +287,8 @@
             bytes_accessed=2 * 7 * cells * 4,
             transcendentals=SWEEPS * cells,
         ),
-    )(strain_rows, valid_rows, states, moduli, *tables)
-    return updated, mean[:, :, 0]
+    )(strain_rows, valid_rows, moduli, *tables, *pieces)
+    return results[:ranks], results[ranks][:, :, 0]
 
 
 def strain_tensor(disp_el, grad_el):
@@ -341,7 +355,9 @@
     thickness = state.shape[2]
     per_rank = groups // ranks
     tables = (jnp.asarray(green_tables()), plane_tables())
-    moduli = jnp.transpose(gather_vox(micro_moduli), (1, 0, 2, 3)).reshape(4, VOX_SIDE, VOX_PLANE)
+    moduli = jnp.concatenate(
+        [micro_moduli] + [shifted(micro_moduli, "vox", -d) for d in range(1, ranks)], axis=1
+    )
     node_ids = jnp.arange(own_nodes, dtype=jnp.int32)
     halo_match = (halo_list[:, None] == node_ids[None, :]).astype(jnp.float32)
     halo_out = jnp.dot(displacement, halo_match.T, precision=FULL_PREC)
@@ -371,26 +387,27 @@
     moved, means = [], []
     for chunk in range(capacity):
         base = chunk * groups
-        picked = state[:, slot_source[base : base + groups]]
-        picked = picked.reshape(7, ranks, per_rank, thickness, VOX_PLANE)
-        picked = jnp.swapaxes(picked, 2, 3)
-        whole = lax.all_to_all(picked, "vox", split_axis=1, concat_axis=1, tiled=True)
-        whole = whole.reshape(7, VOX_SIDE, per_rank, VOX_PLANE)
+        pieces = []
+        for d in range(ranks):
+            solver = base + (me - d) % ranks * per_rank
+            sources = lax.dynamic_slice_in_dim(slot_source, solver, per_rank, 0)
+            piece = jnp.swapaxes(state[:, sources], 1, 2)
+            pieces.append(shifted(piece, "vox", -d) if d else piece)
         mine = base + me * per_rank
         updated, mean = micro_solve(
-            whole,
+            pieces,
             lax.dynamic_slice_in_dim(slot_strain, mine, per_rank, 1),
             lax.dynamic_slice_in_dim(slot_valid, mine, per_rank, 0),
             moduli,
             tables,
         )
         means.append(mean)
-        slabs = updated.reshape(7, ranks, thickness, per_rank, VOX_PLANE)
-        slabs = lax.all_to_all(slabs, "vox", split_axis=1, concat_axis=1, tiled=True)
-        slabs = jnp.swapaxes(slabs, 2, 3).reshape(7, groups, thickness, VOX_PLANE)
+        slabs = [updated[0]] + [shifted(updated[d], "vox", d) for d in range(1, ranks)]
+        slabs = jnp.swapaxes(by_rank(slabs, 2), 1, 2)
         moved.append(lax.all_to_all(slabs, "macro", split_axis=1, concat_axis=1, tiled=True))
-    averaged = jnp.moveaxis(gather_vox(jnp.stack(means, axis=1)), 0, 2)
-    averaged = averaged.reshape(6, capacity * groups)
+    own_mean = jnp.stack(means, axis=1)
+    parts = [own_mean] + [shifted(own_mean, "vox", d) for d in range(1, ranks)]
+    averaged = by_rank(parts, 2).reshape(6, capacity * groups)
     stress_plastic = jnp.dot(averaged, match_float, precision=FULL_PREC)
     stress = jnp.where(plastic[None, :], stress_plastic, elastic_stress(strain, elastic_moduli))
     forces = nodal_forces(stress, grad_ops, volume)

time: 200 us -> 180 us (0.900)
  starting transfers between devices: 48.8 us -> 25.3 us
  other arithmetic: 6.09 us -> 8.4 us
  local copies, waits for them, and re-layouts: 28 us -> 30.2 us
    ppermute x4 -> x10, waiting for transfers between devices: 10.9 us -> 74.2 us  [shifted(): return lax.ppermute(block, axis, route)]
    all_to_all x3, waiting for transfers between devices: 41.9 us -> 4.02 us  [local(): lax.all_to_all(slabs, 'macro', split_axis=1, concat_axis=1, tiled=True)]
    all_to_all x6 -> x0, waiting for transfers between devices: 25.2 us -> none  [the longest x3 15.5 us: local(): lax.all_to_all(picked, 'vox', split_axis=1, concat_axis=1, tiled=True)]
    all_to_all x6 -> x0, starting transfers between devices: 23.2 us -> none  [the longest x3 11.7 us: local(): lax.all_to_all(picked, 'vox', split_axis=1, concat_axis=1, tiled=True)]
    gather x3 -> x12, local copies, waits for them, and re-layouts: 7.96 us -> 18.1 us  [local(): piece = jnp.swapaxes(state[:, sources], 1, 2)]
    reshape x7 -> x0, local copies, waits for them, and re-layouts: 6.79 us -> none  [the longest x3 3.7 us: local(): slabs = updated.reshape(7, ranks, thickness, per_rank, VOX_PLANE)]
    all_to_all x6 -> x0, local copies, waits for them, and re-layouts: 2.89 us -> none  [the longest x3 1.5 us: local(): lax.all_to_all(slabs, 'vox', split_axis=1, concat_axis=1, tiled=True)]
    ge x3, other arithmetic: 1.14 us -> 3.67 us  [local(): block[6, :, 0, 0] >= 0.0]
  transfers between devices with their start and end apart: 13 -> 13, of which waited for: 8 -> 9; matrix products, arithmetic and copies ran while one was open for 14% -> 15% of each run, Pallas kernels for 16% -> 12%
where the time goes in v2:
time: 180 us; the launch traced here: 178 us
  waiting for transfers between devices  78.2 us (43%)
  Pallas kernels  32.1 us (18%)
  local copies, waits for them, and re-layouts  30.2 us (17%)
  starting transfers between devices  25.3 us (14%)
  other arithmetic  8.4 us (5%)
  matrix products  2.71 us (2%)
    ppermute x10, waiting for transfers between devices, shifted(): return lax.ppermute(block, axis, route)  74.2 us
    pallas_call x3, Pallas kernels, micro_solve(): pl.pallas_call(functools.partial(solve_kernel, ranks), out_shape=[jax.Sha...  32.1 us
    gather x12, local copies, waits for them, and re-layouts, local(): piece = jnp.swapaxes(state[:, sources], 1, 2)  18.1 us
    all_to_all x3, starting transfers between devices, local(): lax.all_to_all(slabs, 'macro', split_axis=1, concat_axis=1, tiled=True)  16 us
    ppermute x10, starting transfers between devices, shifted(): return lax.ppermute(block, axis, route)  9.26 us
    transpose x3, local copies, waits for them, and re-layouts, local(): slabs = jnp.swapaxes(by_rank(slabs, 2), 1, 2)  4.39 us
    unnamed x24, local copies, waits for them, and re-layouts  4.29 us
    all_to_all x3, waiting for transfers between devices, local(): lax.all_to_all(slabs, 'macro', split_axis=1, concat_axis=1, tiled=True)  4.02 us
  transfers between devices with their start and end apart: 13, of which 9 were waited for; matrix products, arithmetic and copies ran while one was open for 15% of the time, Pallas kernels for 12%

profile of v2, /device:TPU:0, one launch (start us, length us, event | category | flops | bytes accessed | tf_op | source)
XLA Modules:
  0.0 178.0 jit_solution(11786650725763945336)
XLA Ops:
  2.2 2.5 %collective-permute-start.1 = (f32[4,8,256]{2,1,0:T(8,128)}, f32[4,8,256]{2,1,0:T(8,128)S(1)}, u32[]{:S(2)}, u32[]{:S(2)}) collective-permute-start(f32[4,8,256]{2,1,0:T(8,128)} %param.24), channel_id=1, source_target_pairs={{1,0},{0,1},{3,2},{2,3},{5,4},{4,5},{7,6},{6,7},{9,8},{8,9},{11,10... | collective-permute-start | bytes 98312 | tf_op jit(solution)/shard_map/ppermute | solution.py:32
  7.2 2.6 %gather_fusion.1 = f32[8,7,8,256]{3,2,1,0:T(8,128)S(1)} fusion(f32[7,64,8,256]{3,2,1,0:T(8,128)} %param.23, s32[1024]{0:T(1024)S(1)} %get-tuple-element.91), kind=kCustom, calls=%fused_computation.1 | custom fusion | bytes 917536 | tf_op jit(solution)/shard_map/gather | solution.py:394
  11.0 2.6 %gather_fusion = f32[8,7,8,256]{3,2,1,0:T(8,128)S(1)} fusion(f32[7,64,8,256]{3,2,1,0:T(8,128)} %param.23, s32[1024]{0:T(1024)S(1)} %get-tuple-element.92), kind=kCustom, calls=%fused_computation | custom fusion | bytes 917536 | tf_op jit(solution)/shard_map/gather | solution.py:394
  14.7 8.4 %collective-permute-done.2.refs_1_ = f32[7,8,8,256]{3,2,1,0:T(8,128)S(1)} collective-permute-done((f32[7,8,8,256]{3,2,1,0:T(8,128)S(1)}, f32[7,8,8,256]{3,2,1,0:T(8,128)S(1)}, u32[]{:S(2)}, u32[]{:S(2)}) %collective-permute-start.2) | collective-permute-done | bytes 458784 | tf_op jit(solution)/shard_map/ppermute | solution.py:32
  23.2 10.7 %shard_map.149 = (f32[7,8,8,256]{3,2,1,0:T(8,128)S(1)}, f32[7,8,8,256]{3,2,1,0:T(8,128)S(1)}, f32[6,8,128]{2,1,0:T(8,128)S(1)}) custom-call(f32[6,8,256]{2,1,0:T(8,128)S(1)} %broadcast_in_dim.55.strain_ref, f32[8,256]{1,0:T(8,128)S(1)} %broadcast_in_dim.56.valid_ref, f32[4,16,256]{2,1,0:T(8,128)S(1)} %constant_dynamic-update-slice_fusion.props_ref, ...), custom_call_target="tpu_custom_call" | custom-call | flops 2415919104 | bytes 1835008 | tf_op jit(solution)/shard_map/pallas_call | solution.py:272
  34.0 12.6 %collective-permute-done.7 = f32[7,8,8,256]{3,2,1,0:T(8,128)S(1)} collective-permute-done((f32[7,8,8,256]{3,2,1,0:T(8,128)S(1)}, f32[7,8,8,256]{3,2,1,0:T(8,128)S(1)}, u32[]{:S(2)}, u32[]{:S(2)}) %collective-permute-start.7) | collective-permute-done | bytes 458784 | tf_op jit(solution)/shard_map/ppermute | solution.py:32
  48.1 5.0 %all-to-all-start = ((f32[7,16,8,256]{3,2,0,1:T(8,128)}), f32[7,16,8,256]{3,2,0,1:T(8,128)S(1)}, u32[]{:S(2)}, u32[]{:S(2)}) async-start(f32[7,16,8,256]{3,2,0,1:T(8,128)} %copy.85), calls=%async_computation | async-start | bytes 1835008 | tf_op jit(solution)/shard_map/all_to_all | solution.py:407
  53.1 2.6 %gather_fusion.5 = f32[8,7,8,256]{3,2,1,0:T(8,128)S(1)} fusion(f32[7,64,8,256]{3,2,1,0:T(8,128)} %param.23, s32[1024]{0:T(1024)S(1)} %get-tuple-element.87), kind=kCustom, calls=%fused_computation.5 | custom fusion | bytes 917536 | tf_op jit(solution)/shard_map/gather | solution.py:394
  57.1 2.6 %gather_fusion.4 = f32[8,7,8,256]{3,2,1,0:T(8,128)S(1)} fusion(f32[7,64,8,256]{3,2,1,0:T(8,128)} %param.23, s32[1024]{0:T(1024)S(1)} %get-tuple-element.88), kind=kCustom, calls=%fused_computation.4 | custom fusion | bytes 917536 | tf_op jit(solution)/shard_map/gather | solution.py:394
  59.9 9.8 %collective-permute-done.4.refs_1_ = f32[7,8,8,256]{3,2,1,0:T(8,128)S(1)} collective-permute-done((f32[7,8,8,256]{3,2,1,0:T(8,128)}, f32[7,8,8,256]{3,2,1,0:T(8,128)S(1)}, u32[]{:S(2)}, u32[]{:S(2)}) %collective-permute-start.4) | collective-permute-done | bytes 458784 | tf_op jit(solution)/shard_map/ppermute | solution.py:32
  69.8 10.7 %shard_map.151 = (f32[7,8,8,256]{3,2,1,0:T(8,128)S(1)}, f32[7,8,8,256]{3,2,1,0:T(8,128)S(1)}, f32[6,8,128]{2,1,0:T(8,128)S(1)}) custom-call(f32[6,8,256]{2,1,0:T(8,128)S(1)} %broadcast_in_dim.68.strain_ref, f32[8,256]{1,0:T(8,128)S(1)} %broadcast_in_dim.69.valid_ref, f32[4,16,256]{2,1,0:T(8,128)S(1)} %constant_dynamic-update-slice_fusion.props_ref, ...), custom_call_target="tpu_custom_call" | custom-call | flops 2415919104 | bytes 1835008 | tf_op jit(solution)/shard_map/pallas_call | solution.py:272
  81.0 11.5 %collective-permute-done.9 = f32[7,8,8,256]{3,2,1,0:T(8,128)S(1)} collective-permute-done((f32[7,8,8,256]{3,2,1,0:T(8,128)S(1)}, f32[7,8,8,256]{3,2,1,0:T(8,128)S(1)}, u32[]{:S(2)}, u32[]{:S(2)}) %collective-permute-start.9) | collective-permute-done | bytes 458784 | tf_op jit(solution)/shard_map/ppermute | solution.py:32
  94.0 5.5 %all-to-all-start.2 = ((f32[7,16,8,256]{3,2,0,1:T(8,128)}), f32[7,16,8,256]{3,2,0,1:T(8,128)}, u32[]{:S(2)}, u32[]{:S(2)}) async-start(f32[7,16,8,256]{3,2,0,1:T(8,128)} %copy.87), calls=%async_computation.2 | async-start | bytes 1835008 | tf_op jit(solution)/shard_map/all_to_all | solution.py:407
  99.5 2.6 %gather_fusion.3 = f32[8,7,8,256]{3,2,1,0:T(8,128)S(1)} fusion(f32[7,64,8,256]{3,2,1,0:T(8,128)} %param.23, s32[1024]{0:T(1024)S(1)} %get-tuple-element.89), kind=kCustom, calls=%fused_computation.3 | custom fusion | bytes 917536 | tf_op jit(solution)/shard_map/gather | solution.py:394
  103.6 2.6 %gather_fusion.2 = f32[8,7,8,256]{3,2,1,0:T(8,128)S(1)} fusion(f32[7,64,8,256]{3,2,1,0:T(8,128)} %param.23, s32[1024]{0:T(1024)S(1)} %get-tuple-element.90), kind=kCustom, calls=%fused_computation.2 | custom fusion | bytes 917536 | tf_op jit(solution)/shard_map/gather | solution.py:394
  106.3 9.7 %collective-permute-done.3.refs_1_ = f32[7,8,8,256]{3,2,1,0:T(8,128)S(1)} collective-permute-done((f32[7,8,8,256]{3,2,1,0:T(8,128)}, f32[7,8,8,256]{3,2,1,0:T(8,128)S(1)}, u32[]{:S(2)}, u32[]{:S(2)}) %collective-permute-start.3) | collective-permute-done | bytes 458784 | tf_op jit(solution)/shard_map/ppermute | solution.py:32
  116.2 10.7 %shard_map.150 = (f32[7,8,8,256]{3,2,1,0:T(8,128)S(1)}, f32[7,8,8,256]{3,2,1,0:T(8,128)S(1)}, f32[6,8,128]{2,1,0:T(8,128)S(1)}) custom-call(f32[6,8,256]{2,1,0:T(8,128)S(1)} %broadcast_in_dim.64.strain_ref, f32[8,256]{1,0:T(8,128)S(1)} %broadcast_in_dim.65.valid_ref, f32[4,16,256]{2,1,0:T(8,128)S(1)} %constant_dynamic-update-slice_fusion.props_ref, ...), custom_call_target="tpu_custom_call" | custom-call | flops 2415919104 | bytes 1835008 | tf_op jit(solution)/shard_map/pallas_call | solution.py:272
  127.6 11.3 %collective-permute-done.8 = f32[7,8,8,256]{3,2,1,0:T(8,128)S(1)} collective-permute-done((f32[7,8,8,256]{3,2,1,0:T(8,128)S(1)}, f32[7,8,8,256]{3,2,1,0:T(8,128)S(1)}, u32[]{:S(2)}, u32[]{:S(2)}) %collective-permute-start.8) | collective-permute-done | bytes 458784 | tf_op jit(solution)/shard_map/ppermute | solution.py:32
  140.4 5.6 %all-to-all-start.1 = ((f32[7,16,8,256]{3,2,0,1:T(8,128)}), f32[7,16,8,256]{3,2,0,1:T(8,128)S(1)}, u32[]{:S(2)}, u32[]{:S(2)}) async-start(f32[7,16,8,256]{3,2,0,1:T(8,128)} %copy.86), calls=%async_computation.1 | async-start | bytes 1835008 | tf_op jit(solution)/shard_map/all_to_all | solution.py:407
  146.7 3.2 %collective-permute-done.5 = f32[6,3,8]{2,1,0:T(4,128)S(1)} collective-permute-done((f32[6,3,8]{2,1,0:T(4,128)S(1)}, f32[6,3,8]{2,1,0:T(4,128)S(1)}, u32[]{:S(2)}, u32[]{:S(2)}) %collective-permute-start.5) | collective-permute-done | bytes 608 | tf_op jit(solution)/shard_map/ppermute | solution.py:32
  150.6 3.5 %collective-permute-start.6 = (f32[3,16]{1,0:T(4,128)S(1)}, f32[3,16]{1,0:T(4,128)S(1)}, u32[]{:S(2)}, u32[]{:S(2)}) collective-permute-start(f32[3,16]{1,0:T(4,128)S(1)} %slice.108), channel_id=1, source_target_pairs={{2,0},{4,2},{6,4},{8,6},{10,8},{12,10},{14,12},{16,14},{18,16},{20... | collective-permute-start | bytes 584 | tf_op jit(solution)/shard_map/ppermute | solution.py:32
  154.1 7.9 %collective-permute-done.6 = f32[3,16]{1,0:T(4,128)S(1)} collective-permute-done((f32[3,16]{1,0:T(4,128)S(1)}, f32[3,16]{1,0:T(4,128)S(1)}, u32[]{:S(2)}, u32[]{:S(2)}) %collective-permute-start.6) | collective-permute-done | bytes 224 | tf_op jit(solution)/shard_map/ppermute | solution.py:32
  162.8 4.0 %all-to-all-done.1 = f32[7,16,8,256]{3,2,0,1:T(8,128)S(1)} async-done(((f32[7,16,8,256]{3,2,0,1:T(8,128)}), f32[7,16,8,256]{3,2,0,1:T(8,128)S(1)}, u32[]{:S(2)}, u32[]{:S(2)}) %all-to-all-start.1) | async-done | bytes 917536 | tf_op jit(solution)/shard_map/all_to_all | solution.py:407
  175.5 2.5 %copy.94 = f32[7,24,8,256]{3,2,1,0:T(8,128)} copy(f32[7,24,8,256]{3,2,0,1:T(8,128)} %bitcast.82) | data formatting | bytes 2752512
  (107 shorter events, 26.3 us)
Async XLA Ops:
  0.6 22.6 %copy-start = (bf16[4,256,256]{2,1,0:T(8,128)(2,1)S(1)}, bf16[4,256,256]{2,1,0:T(8,128)(2,1)}, u32[]{:S(2)}) copy-start(bf16[4,256,256]{2,1,0:T(8,128)(2,1)} %constant.107.plane_ref) | copy-start | bytes 1572868
  0.6 22.6 %copy-start.1 = (f32[21,16,256]{2,1,0:T(8,128)S(1)}, f32[21,16,256]{2,1,0:T(8,128)}, u32[]{:S(2)}) copy-start(f32[21,16,256]{2,1,0:T(8,128)} %constant.92.clone.green_ref) | copy-start | bytes 1032196
  0.7 13.2 %copy-start.8 = (f32[3,64]{1,0:T(4,128)S(1)}, f32[3,64]{1,0:T(4,128)}, u32[]{:S(2)}) copy-start(f32[3,64]{1,0:T(4,128)} %param.14) | copy-start | bytes 2308
  0.7 13.2 %copy-start.7 = (s32[8,64]{1,0:T(8,128)S(1)}, s32[8,64]{1,0:T(8,128)}, u32[]{:S(2)}) copy-start(s32[8,64]{1,0:T(8,128)} %param.16) | copy-start | bytes 6148
  0.7 13.7 %copy-start.4 = (f32[3,8,64]{2,1,0:T(8,128)S(1)}, f32[3,8,64]{2,1,0:T(8,128)}, u32[]{:S(2)}) copy-start(f32[3,8,64]{2,1,0:T(8,128)} %param.18) | copy-start | bytes 18436
  0.7 13.7 %copy-start.5 = (f32[2,64]{1,0:T(2,128)S(1)}, f32[2,64]{1,0:T(2,128)}, u32[]{:S(2)}) copy-start(f32[2,64]{1,0:T(2,128)} %param.20) | copy-start | bytes 1540
  1.6 12.1 %collective-permute-start = (f32[3,16]{1,0:T(4,128)S(1)}, f32[3,16]{1,0:T(4,128)S(1)}, u32[]{:S(2)}, u32[]{:S(2)}) collective-permute-start(f32[3,16]{1,0:T(4,128)S(1)} %convolution_bitcast_fusion.1), channel_id=1, source_target_pairs={{30,0},{0,2},{2,4},{4,6},{6,8},{8,10},{10,12},{12,14},{14,16},{16,... | collective-permute-start | bytes 584 | tf_op jit(solution)/shard_map/ppermute | solution.py:32
  2.2 12.5 %collective-permute-start.1 = (f32[4,8,256]{2,1,0:T(8,128)}, f32[4,8,256]{2,1,0:T(8,128)S(1)}, u32[]{:S(2)}, u32[]{:S(2)}) collective-permute-start(f32[4,8,256]{2,1,0:T(8,128)} %param.24), channel_id=1, source_target_pairs={{1,0},{0,1},{3,2},{2,3},{5,4},{4,5},{7,6},{6,7},{9,8},{8,9},{11,10... | collective-permute-start | bytes 98312 | tf_op jit(solution)/shard_map/ppermute | solution.py:32
  9.9 13.1 %collective-permute-start.2 = (f32[7,8,8,256]{3,2,1,0:T(8,128)S(1)}, f32[7,8,8,256]{3,2,1,0:T(8,128)S(1)}, u32[]{:S(2)}, u32[]{:S(2)}) collective-permute-start(f32[7,8,8,256]{3,2,1,0:T(8,128)S(1)} %bitcast.83), channel_id=1, source_target_pairs={{1,0},{0,1},{3,2},{2,3},{5,4},{4,5},{7,6},{6,7},{9,8},{8,9},{11,10... | collective-permute-start | bytes 1376264 | tf_op jit(solution)/shard_map/ppermute | solution.py:32
  33.9 12.6 %collective-permute-start.7 = (f32[7,8,8,256]{3,2,1,0:T(8,128)S(1)}, f32[7,8,8,256]{3,2,1,0:T(8,128)S(1)}, u32[]{:S(2)}, u32[]{:S(2)}) collective-permute-start(f32[7,8,8,256]{3,2,1,0:T(8,128)S(1)} %get-tuple-element.15), channel_id=1, source_target_pairs={{1,0},{0,1},{3,2},{2,3},{5,4},{4,5},{7,6},{6,7},{9,8},{8,9},{11,10... | collective-permute-start | bytes 1376264 | tf_op jit(solution)/shard_map/ppermute | solution.py:32
  48.1 46.0 %all-to-all-start = ((f32[7,16,8,256]{3,2,0,1:T(8,128)}), f32[7,16,8,256]{3,2,0,1:T(8,128)S(1)}, u32[]{:S(2)}, u32[]{:S(2)}) async-start(f32[7,16,8,256]{3,2,0,1:T(8,128)} %copy.85), calls=%async_computation | async-start | bytes 1835008 | tf_op jit(solution)/shard_map/all_to_all | solution.py:407
  56.6 13.0 %collective-permute-start.4 = (f32[7,8,8,256]{3,2,1,0:T(8,128)}, f32[7,8,8,256]{3,2,1,0:T(8,128)S(1)}, u32[]{:S(2)}, u32[]{:S(2)}) collective-permute-start(f32[7,8,8,256]{3,2,1,0:T(8,128)} %bitcast.73), channel_id=1, source_target_pairs={{1,0},{0,1},{3,2},{2,3},{5,4},{4,5},{7,6},{6,7},{9,8},{8,9},{11,10... | collective-permute-start | bytes 1376264 | tf_op jit(solution)/shard_map/ppermute | solution.py:32
  80.5 12.0 %collective-permute-start.9 = (f32[7,8,8,256]{3,2,1,0:T(8,128)S(1)}, f32[7,8,8,256]{3,2,1,0:T(8,128)S(1)}, u32[]{:S(2)}, u32[]{:S(2)}) collective-permute-start(f32[7,8,8,256]{3,2,1,0:T(8,128)S(1)} %get-tuple-element.19), channel_id=1, source_target_pairs={{1,0},{0,1},{3,2},{2,3},{5,4},{4,5},{7,6},{6,7},{9,8},{8,9},{11,10... | collective-permute-start | bytes 1376264 | tf_op jit(solution)/shard_map/ppermute | solution.py:32
  94.0 72.7 %copy-start.2 = (f32[7,16,8,256]{3,2,0,1:T(8,128)}, f32[7,16,8,256]{3,2,0,1:T(8,128)S(1)}, u32[]{:S(2)}) copy-start(f32[7,16,8,256]{3,2,0,1:T(8,128)S(1)} %all-to-all-done) | copy-start | bytes 2752516
  94.0 46.4 %all-to-all-start.2 = ((f32[7,16,8,256]{3,2,0,1:T(8,128)}), f32[7,16,8,256]{3,2,0,1:T(8,128)}, u32[]{:S(2)}, u32[]{:S(2)}) async-start(f32[7,16,8,256]{3,2,0,1:T(8,128)} %copy.87), calls=%async_computation.2 | async-start | bytes 1835008 | tf_op jit(solution)/shard_map/all_to_all | solution.py:407
  103.1 13.0 %collective-permute-start.3 = (f32[7,8,8,256]{3,2,1,0:T(8,128)}, f32[7,8,8,256]{3,2,1,0:T(8,128)S(1)}, u32[]{:S(2)}, u32[]{:S(2)}) collective-permute-start(f32[7,8,8,256]{3,2,1,0:T(8,128)} %bitcast.75), channel_id=1, source_target_pairs={{1,0},{0,1},{3,2},{2,3},{5,4},{4,5},{7,6},{6,7},{9,8},{8,9},{11,10... | collective-permute-start | bytes 1376264 | tf_op jit(solution)/shard_map/ppermute | solution.py:32
  126.9 11.9 %collective-permute-start.8 = (f32[7,8,8,256]{3,2,1,0:T(8,128)S(1)}, f32[7,8,8,256]{3,2,1,0:T(8,128)S(1)}, u32[]{:S(2)}, u32[]{:S(2)}) collective-permute-start(f32[7,8,8,256]{3,2,1,0:T(8,128)S(1)} %get-tuple-element.17), channel_id=1, source_target_pairs={{1,0},{0,1},{3,2},{2,3},{5,4},{4,5},{7,6},{6,7},{9,8},{8,9},{11,10... | collective-permute-start | bytes 1376264 | tf_op jit(solution)/shard_map/ppermute | solution.py:32
  138.8 11.4 %copy-start.6 = (f32[64]{0:T(128)S(1)}, f32[64]{0:T(128)}, u32[]{:S(2)}) copy-start(f32[64]{0:T(128)} %param.19) | copy-start | bytes 772
  138.9 23.1 %copy-start.9 = (f32[3,64]{1,0:T(4,128)S(1)}, f32[3,64]{1,0:T(4,128)}, u32[]{:S(2)}) copy-start(f32[3,64]{1,0:T(4,128)} %param.15) | copy-start | bytes 2308
  138.9 23.1 %copy-start.10 = (s32[16]{0:T(128)S(1)}, s32[16]{0:T(128)}, u32[]{:S(2)}) copy-start(s32[16]{0:T(128)} %param.17) | copy-start | bytes 196
  140.4 26.4 %all-to-all-start.1 = ((f32[7,16,8,256]{3,2,0,1:T(8,128)}), f32[7,16,8,256]{3,2,0,1:T(8,128)S(1)}, u32[]{:S(2)}, u32[]{:S(2)}) async-start(f32[7,16,8,256]{3,2,0,1:T(8,128)} %copy.86), calls=%async_computation.1 | async-start | bytes 1835008 | tf_op jit(solution)/shard_map/all_to_all | solution.py:407
  146.1 3.8 %collective-permute-start.5 = (f32[6,3,8]{2,1,0:T(4,128)S(1)}, f32[6,3,8]{2,1,0:T(4,128)S(1)}, u32[]{:S(2)}, u32[]{:S(2)}) collective-permute-start(f32[6,3,8]{2,1,0:T(4,128)S(1)} %pad_maximum_fusion.1), channel_id=1, source_target_pairs={{1,0},{0,1},{3,2},{2,3},{5,4},{4,5},{7,6},{6,7},{9,8},{8,9},{11,10... | collective-permute-start | bytes 1736 | tf_op jit(solution)/shard_map/ppermute | solution.py:32
  150.6 11.4 %collective-permute-start.6 = (f32[3,16]{1,0:T(4,128)S(1)}, f32[3,16]{1,0:T(4,128)S(1)}, u32[]{:S(2)}, u32[]{:S(2)}) collective-permute-start(f32[3,16]{1,0:T(4,128)S(1)} %slice.108), channel_id=1, source_target_pairs={{2,0},{4,2},{6,4},{8,6},{10,8},{12,10},{14,12},{16,14},{18,16},{20... | collective-permute-start | bytes 584 | tf_op jit(solution)/shard_map/ppermute | solution.py:32
  166.8 0.9 copy-start.3

commit v3 on v2

--- a/solution.py
+++ b/solution.py
@@ -8,6 +8,7 @@
 from jax.experimental import pallas as pl
 from jax.experimental.pallas import tpu as pltpu
 from jax.sharding import PartitionSpec as P
+
 
 RECV_AGG = 24
 PLASTIC_MAX = 48
@@ -158,7 +159,7 @@
     return stress, shape, (1.5 * two_mu) * factor, gain
 
 
-def solve_kernel(ranks, strain_ref, valid_ref, props_ref, green_ref, plane_ref, *refs):
+def solve_kernel(ranks, strain_ref, props_ref, green_ref, plane_ref, *refs):
     state_refs, new_refs = refs[:ranks], refs[ranks : 2 * ranks]
     mean_ref, eps, work, cos_ref, sin_ref = refs[2 * ranks :]
     thickness, rows = state_refs[0].shape[1:3]
@@ -241,8 +242,6 @@
         return carry
 
     lax.fori_loop(0, SWEEPS, sweep, 0)
-    valid = valid_ref[...] > 0.5
-
     zero = jnp.zeros((rows, VOX_PLANE), jnp.float32)
     totals = (zero,) * 6
     for slab, (state_ref, new_ref) in enumerate(zip(state_refs, new_refs)):
@@ -253,7 +252,7 @@
             stress, shape, scale, gain = voxel_law(strain, state_ref, props_ref, place, x)
             for c in range(6):
                 new_ref[c, place] = state_ref[c, place] + scale * shape[c]
-            new_ref[6, place] = jnp.where(valid, state_ref[6, place] + gain, -1.0)
+            new_ref[6, place] = state_ref[6, place] + gain
             return tuple(totals[c] + stress[c] for c in range(6))
 
         totals = lax.fori_loop(0, thickness, finish, totals)
@@ -262,18 +261,17 @@
         mean_ref[c] = jnp.broadcast_to(total, mean_ref.shape[1:])
 
 
-def micro_solve(pieces, strains, valid, moduli, tables):
+def micro_solve(pieces, strains, moduli, tables):
     ranks = len(pieces)
     rows = pieces[0].shape[2]
     strain_rows = jnp.broadcast_to(strains[:, :, None], (6, rows, VOX_PLANE))
-    valid_rows = jnp.broadcast_to(valid[:, None], (rows, VOX_PLANE))
     vmem = pl.BlockSpec(memory_space=pltpu.VMEM)
     cells = VOX_SIDE * rows * VOX_PLANE
     results = pl.pallas_call(
         functools.partial(solve_kernel, ranks),
         out_shape=[jax.ShapeDtypeStruct(pieces[0].shape, jnp.float32)] * ranks
         + [jax.ShapeDtypeStruct((6, rows, 128), jnp.float32)],
-        in_specs=[vmem] * (5 + ranks),
+        in_specs=[vmem] * (4 + ranks),
         out_specs=[vmem] * (ranks + 1),
         scratch_shapes=[
             pltpu.VMEM((6, VOX_SIDE, rows, VOX_PLANE), jnp.float32),
@@ -287,8 +285,39 @@
             bytes_accessed=2 * 7 * cells * 4,
             transcendentals=SWEEPS * cells,
         ),
-    )(strain_rows, valid_rows, moduli, *tables, *pieces)
+    )(strain_rows, moduli, *tables, *pieces)
     return results[:ranks], results[ranks][:, :, 0]
+
+
+def pick_kernel(order_ref, *refs):
+    out_ref = refs[-1]
+
+    def place(j, carry):
+        low = 0
+        for part in refs[:-1]:
+            size = part.shape[1]
+            spot = order_ref[j] - low
+
+            @pl.when((spot >= 0) & (spot < size))
+            def _(part=part, spot=spot):
+                out_ref[:, j] = part[:, spot]
+
+            low += size
+        return carry
+
+    lax.fori_loop(0, out_ref.shape[1], place, 0)
+
+
+def pick_rows(order, parts):
+    shape = (parts[0].shape[0], order.shape[0]) + parts[0].shape[2:]
+    vmem = pl.BlockSpec(memory_space=pltpu.VMEM)
+    return pl.pallas_call(
+        pick_kernel,
+        out_shape=jax.ShapeDtypeStruct(shape, jnp.float32),
+        in_specs=[pl.BlockSpec(memory_space=pltpu.SMEM)] + [vmem] * len(parts),
+        out_specs=vmem,
+        compiler_params=pltpu.CompilerParams(vmem_limit_bytes=16 * 2**20),
+    )(order, *parts)
 
 
 def strain_tensor(disp_el, grad_el):
@@ -352,7 +381,6 @@
     me = lax.axis_index("vox")
     own_nodes = displacement.shape[1]
     elements = conn.shape[1]
-    thickness = state.shape[2]
     per_rank = groups // ranks
     tables = (jnp.asarray(green_tables()), plane_tables())
     moduli = jnp.concatenate(
@@ -384,7 +412,18 @@
     slot_valid = jnp.sum(match_float, axis=1)
     slot_source = jnp.sum(jnp.where(slot_match, point_ids[None, :], 0), axis=1)
     slot_strain = jnp.dot(strain, match_float.T, precision=FULL_PREC)
-    moved, means = [], []
+    valid_rows = jnp.swapaxes(slot_valid.reshape(capacity, groups), 0, 1)
+    got_valid = lax.all_to_all(valid_rows, "macro", split_axis=0, concat_axis=0, tiled=True)
+    full = got_valid.reshape(-1) > 0.5
+    places = jnp.arange(groups * capacity, dtype=jnp.int32)
+    origin, turn = places // capacity, places % capacity
+    places = jnp.where(turn == 0, origin, groups + origin * (capacity - 1) + turn - 1)
+    earlier = (slot_ids[:, None] < slot_ids[None, :]) & full[:, None]
+    position = jnp.sum(earlier.astype(jnp.int32), axis=0)
+    wanted = jnp.arange(RECV_AGG, dtype=jnp.int32)
+    wanted_match = (wanted[:, None] == position[None, :]) & full[None, :]
+    order = jnp.sum(jnp.where(wanted_match, places[None, :], 0), axis=1)
+    solved, means = [], []
     for chunk in range(capacity):
         base = chunk * groups
         pieces = []
@@ -394,17 +433,17 @@
             piece = jnp.swapaxes(state[:, sources], 1, 2)
             pieces.append(shifted(piece, "vox", -d) if d else piece)
         mine = base + me * per_rank
-        updated, mean = micro_solve(
-            pieces,
-            lax.dynamic_slice_in_dim(slot_strain, mine, per_rank, 1),
-            lax.dynamic_slice_in_dim(slot_valid, mine, per_rank, 0),
-            moduli,
-            tables,
-        )
+        own_strain = lax.dynamic_slice_in_dim(slot_strain, mine, per_rank, 1)
+        updated, mean = micro_solve(pieces, own_strain, moduli, tables)
         means.append(mean)
         slabs = [updated[0]] + [shifted(updated[d], "vox", d) for d in range(1, ranks)]
         slabs = jnp.swapaxes(by_rank(slabs, 2), 1, 2)
-        moved.append(lax.all_to_all(slabs, "macro", split_axis=1, concat_axis=1, tiled=True))
+        solved.append(slabs)
+    moved = [lax.all_to_all(solved[0], "macro", split_axis=1, concat_axis=1, tiled=True)]
+    if capacity > 1:
+        rest = jnp.stack(solved[1:], axis=2)
+        rest = lax.all_to_all(rest, "macro", split_axis=1, concat_axis=1, tiled=True)
+        moved.append(rest.reshape((7, -1) + rest.shape[3:]))
     own_mean = jnp.stack(means, axis=1)
     parts = [own_mean] + [shifted(own_mean, "vox", d) for d in range(1, ranks)]
     averaged = by_rank(parts, 2).reshape(6, capacity * groups)
@@ -416,16 +455,7 @@
     residual = (
         assembled[:, :own_nodes] + jnp.dot(returned_force, halo_match, precision=FULL_PREC) - load
     )
-    arrived = jnp.concatenate(moved, axis=1)
-    full = jnp.stack([block[6, :, 0, 0] >= 0.0 for block in moved], axis=1).reshape(-1)
-    position = jnp.cumsum(full.astype(jnp.int32)) - 1
-    wanted = jnp.arange(RECV_AGG, dtype=jnp.int32)
-    places = jnp.arange(groups * capacity, dtype=jnp.int32)
-    places = (places % capacity) * groups + places // capacity
-    chosen = jnp.sum(
-        jnp.where((wanted[:, None] == position[None, :]) & full[None, :], places[None, :], 0), axis=1
-    )
-    return (residual, arrived[:, chosen])
+    return (residual, pick_rows(order, moved))
 
 
 def solution(mesh):

time: 180 us -> 157 us (0.87)
  the two profiles are of different devices: /device:TPU:0 before, /device:TPU:11 now
where the time goes in v3:
time: 157 us
  waiting for transfers between devices  60.6 us (39%)
  Pallas kernels  34 us (22%)
  starting transfers between devices  29.8 us (19%)
  local copies, waits for them, and re-layouts  25.2 us (16%)
  other arithmetic  3.43 us (2%)
  matrix products  2.65 us (2%)
    ppermute x10, waiting for transfers between devices, shifted(): return lax.ppermute(block, axis, route)  60.6 us
    pallas_call x3, Pallas kernels, micro_solve(): pl.pallas_call(functools.partial(solve_kernel, ranks), out_shape=[jax.Sha...  31.8 us
    gather x12, local copies, waits for them, and re-layouts, local(): piece = jnp.swapaxes(state[:, sources], 1, 2)  18.2 us
    ppermute x10, starting transfers between devices, shifted(): return lax.ppermute(block, axis, route)  9.1 us
    all_to_all x1, starting transfers between devices, local(): lax.all_to_all(rest, 'macro', split_axis=1, concat_axis=1, tiled=True)  9.04 us
    all_to_all x1, starting transfers between devices, local(): lax.all_to_all(solved[0], 'macro', split_axis=1, concat_axis=1, tiled=True)  6.04 us
    all_to_all x1, starting transfers between devices, local(): lax.all_to_all(valid_rows, 'macro', split_axis=0, concat_axis=0, tiled=True)  5.63 us
  transfers between devices with their start and end apart: 13, of which 6 were waited for; matrix products, arithmetic and copies ran while one was open for 19% of the time, Pallas kernels for 14%

profile of v3, /device:TPU:11, one launch (start us, length us, event | category | flops | bytes accessed | tf_op | source)
XLA Modules:
  0.0 156.7 jit_solution(2386420257295588866)
XLA Ops:
  1.5 1.8 %collective-permute-start = (f32[3,16]{1,0:T(4,128)S(1)}, f32[3,16]{1,0:T(4,128)S(1)}, u32[]{:S(2)}, u32[]{:S(2)}) collective-permute-start(f32[3,16]{1,0:T(4,128)S(1)} %convolution_bitcast_fusion.1), channel_id=1, source_target_pairs={{30,0},{0,2},{2,4},{4,6},{6,8},{8,10},{10,12},{12,14},{14,16},{16,... | collective-permute-start | bytes 584 | tf_op jit(solution)/shard_map/ppermute | solution.py:33
  7.2 2.7 %gather_fusion.1 = f32[8,7,8,256]{3,2,1,0:T(8,128)S(1)} fusion(f32[7,64,8,256]{3,2,1,0:T(8,128)} %param.23, s32[1024]{0:T(1024)S(1)} %get-tuple-element.76), kind=kCustom, calls=%fused_computation.1 | custom fusion | bytes 917536 | tf_op jit(solution)/shard_map/gather | solution.py:433
  10.3 2.6 %gather_fusion = f32[8,7,8,256]{3,2,1,0:T(8,128)S(1)} fusion(f32[7,64,8,256]{3,2,1,0:T(8,128)} %param.23, s32[1024]{0:T(1024)S(1)} %get-tuple-element.77), kind=kCustom, calls=%fused_computation | custom fusion | bytes 917536 | tf_op jit(solution)/shard_map/gather | solution.py:433
  14.0 8.0 %collective-permute-done.2.refs_1_ = f32[7,8,8,256]{3,2,1,0:T(8,128)S(1)} collective-permute-done((f32[7,8,8,256]{3,2,1,0:T(8,128)S(1)}, f32[7,8,8,256]{3,2,1,0:T(8,128)S(1)}, u32[]{:S(2)}, u32[]{:S(2)}) %collective-permute-start.2) | collective-permute-done | bytes 458784 | tf_op jit(solution)/shard_map/ppermute | solution.py:33
  22.0 10.6 %shard_map.149 = (f32[7,8,8,256]{3,2,1,0:T(8,128)S(1)}, f32[7,8,8,256]{3,2,1,0:T(8,128)S(1)}, f32[6,8,128]{2,1,0:T(8,128)S(1)}) custom-call(f32[6,8,256]{2,1,0:T(8,128)S(1)} %broadcast_in_dim.53.strain_ref, f32[4,16,256]{2,1,0:T(8,128)S(1)} %constant_dynamic-update-slice_fusion.props_ref, f32[21,16,256]{2,1,0:T(8,128)S(1)} %copy-done.1, ...), custom_call_target="tpu_custom_call" | custom-call | flops 2415919104 | bytes 1835008 | tf_op jit(solution)/shard_map/pallas_call | solution.py:270
  33.7 5.6 %all-to-all-start = ((f32[16,1,3]{2,1,0:T(1,128)}), f32[16,1,3]{2,1,0:T(1,128)S(1)}, u32[]{:S(2)}, u32[]{:S(2)}) async-start(f32[16,1,3]{2,1,0:T(1,128)} %copy.88), calls=%async_computation | async-start | bytes 16384 | tf_op jit(solution)/shard_map/all_to_all | solution.py:416
  39.4 5.1 %collective-permute-done.7 = f32[7,8,8,256]{3,2,1,0:T(8,128)S(1)} collective-permute-done((f32[7,8,8,256]{3,2,1,0:T(8,128)S(1)}, f32[7,8,8,256]{3,2,1,0:T(8,128)S(1)}, u32[]{:S(2)}, u32[]{:S(2)}) %collective-permute-start.7) | collective-permute-done | bytes 458784 | tf_op jit(solution)/shard_map/ppermute | solution.py:33
  44.5 1.5 copy.89
  46.0 6.0 %all-to-all-start.1 = ((f32[7,16,8,256]{3,2,0,1:T(8,128)}), f32[7,16,8,256]{3,2,0,1:T(8,128)}, u32[]{:S(2)}, u32[]{:S(2)}) async-start(f32[7,16,8,256]{3,2,0,1:T(8,128)} %copy.89), calls=%async_computation.1 | async-start | bytes 1835008 | tf_op jit(solution)/shard_map/all_to_all | solution.py:442
  52.1 2.6 %gather_fusion.3 = f32[8,7,8,256]{3,2,1,0:T(8,128)S(1)} fusion(f32[7,64,8,256]{3,2,1,0:T(8,128)} %param.23, s32[1024]{0:T(1024)S(1)} %get-tuple-element.74), kind=kCustom, calls=%fused_computation.3 | custom fusion | bytes 917536 | tf_op jit(solution)/shard_map/gather | solution.py:433
  55.8 2.6 %gather_fusion.5 = f32[8,7,8,256]{3,2,1,0:T(8,128)S(1)} fusion(f32[7,64,8,256]{3,2,1,0:T(8,128)} %param.23, s32[1024]{0:T(1024)S(1)} %get-tuple-element.72), kind=kCustom, calls=%fused_computation.5 | custom fusion | bytes 917536 | tf_op jit(solution)/shard_map/gather | solution.py:433
  60.6 2.6 %gather_fusion.2 = f32[8,7,8,256]{3,2,1,0:T(8,128)S(1)} fusion(f32[7,64,8,256]{3,2,1,0:T(8,128)} %param.23, s32[1024]{0:T(1024)S(1)} %get-tuple-element.75), kind=kCustom, calls=%fused_computation.2 | custom fusion | bytes 917536 | tf_op jit(solution)/shard_map/gather | solution.py:433
  63.4 2.6 %gather_fusion.4 = f32[8,7,8,256]{3,2,1,0:T(8,128)S(1)} fusion(f32[7,64,8,256]{3,2,1,0:T(8,128)} %param.23, s32[1024]{0:T(1024)S(1)} %get-tuple-element.73), kind=kCustom, calls=%fused_computation.4 | custom fusion | bytes 917536 | tf_op jit(solution)/shard_map/gather | solution.py:433
  66.1 1.4 collective-permute-done.3.refs_1_
  67.6 10.6 %shard_map.150 = (f32[7,8,8,256]{3,2,1,0:T(8,128)S(1)}, f32[7,8,8,256]{3,2,1,0:T(8,128)S(1)}, f32[6,8,128]{2,1,0:T(8,128)S(1)}) custom-call(f32[6,8,256]{2,1,0:T(8,128)S(1)} %broadcast_in_dim.58.strain_ref, f32[4,16,256]{2,1,0:T(8,128)S(1)} %constant_dynamic-update-slice_fusion.props_ref, f32[21,16,256]{2,1,0:T(8,128)S(1)} %copy-done.1, ...), custom_call_target="tpu_custom_call" | custom-call | flops 2415919104 | bytes 1835008 | tf_op jit(solution)/shard_map/pallas_call | solution.py:270
  78.5 10.6 %shard_map.151 = (f32[7,8,8,256]{3,2,1,0:T(8,128)S(1)}, f32[7,8,8,256]{3,2,1,0:T(8,128)S(1)}, f32[6,8,128]{2,1,0:T(8,128)S(1)}) custom-call(f32[6,8,256]{2,1,0:T(8,128)S(1)} %broadcast_in_dim.64.strain_ref, f32[4,16,256]{2,1,0:T(8,128)S(1)} %constant_dynamic-update-slice_fusion.props_ref, f32[21,16,256]{2,1,0:T(8,128)S(1)} %copy-done.1, ...), custom_call_target="tpu_custom_call" | custom-call | flops 2415919104 | bytes 1835008 | tf_op jit(solution)/shard_map/pallas_call | solution.py:270
  90.4 8.4 %collective-permute-done.9 = f32[7,8,8,256]{3,2,1,0:T(8,128)S(1)} collective-permute-done((f32[7,8,8,256]{3,2,1,0:T(8,128)S(1)}, f32[7,8,8,256]{3,2,1,0:T(8,128)S(1)}, u32[]{:S(2)}, u32[]{:S(2)}) %collective-permute-start.9) | collective-permute-done | bytes 458784 | tf_op jit(solution)/shard_map/ppermute | solution.py:33
  99.1 2.3 %copy.90 = f32[7,16,2,8,256]{4,3,0,2,1:T(8,128)} copy(f32[7,16,2,8,256]{4,1,3,0,2:T(8,128)S(1)} %pad_maximum_fusion) | data formatting | bytes 3670016 | tf_op jit(solution)/shard_map/stack | solution.py:444
  101.4 9.0 %all-to-all-start.2 = ((f32[7,16,2,8,256]{4,3,0,2,1:T(8,128)}), f32[7,16,2,8,256]{4,3,0,2,1:T(8,128)S(1)}, u32[]{:S(2)}, u32[]{:S(2)}) async-start(f32[7,16,2,8,256]{4,3,0,2,1:T(8,128)} %copy.90), calls=%async_computation.2 | async-start | bytes 3670016 | tf_op jit(solution)/shard_map/all_to_all | solution.py:445
  110.9 1.3 collective-permute-start.5
  112.3 1.5 collective-permute-done.5
  114.6 1.3 collective-permute-start.6
  115.9 36.3 %collective-permute-done.6 = f32[3,16]{1,0:T(4,128)S(1)} collective-permute-done((f32[3,16]{1,0:T(4,128)S(1)}, f32[3,16]{1,0:T(4,128)S(1)}, u32[]{:S(2)}, u32[]{:S(2)}) %collective-permute-start.6) | collective-permute-done | bytes 224 | tf_op jit(solution)/shard_map/ppermute | solution.py:33
  154.5 2.2 %shard_map.152 = f32[7,24,8,256]{3,2,1,0:T(8,128)} custom-call(s32[24]{0:T(128)S(1)} %select_reduce_fusion.1.order_ref, f32[7,16,8,256]{3,2,1,0:T(8,128)S(1)} %copy.92.refs_0_, f32[7,32,8,256]{3,2,1,0:T(8,128)S(1)} %bitcast.79), custom_call_target="tpu_custom_call" | custom-call | tf_op jit(solution)/shard_map/pallas_call | solution.py:314
  (93 shorter events, 16.4 us)
Async XLA Ops:
  0.6 9.7 %copy-start.3 = (f32[4,8,256]{2,1,0:T(8,128)S(1)}, f32[4,8,256]{2,1,0:T(8,128)}, u32[]{:S(2)}) copy-start(f32[4,8,256]{2,1,0:T(8,128)} %param.24) | copy-start | bytes 98308
  1.5 11.6 %collective-permute-start = (f32[3,16]{1,0:T(4,128)S(1)}, f32[3,16]{1,0:T(4,128)S(1)}, u32[]{:S(2)}, u32[]{:S(2)}) collective-permute-start(f32[3,16]{1,0:T(4,128)S(1)} %convolution_bitcast_fusion.1), channel_id=1, source_target_pairs={{30,0},{0,2},{2,4},{4,6},{6,8},{8,10},{10,12},{12,14},{14,16},{16,... | collective-permute-start | bytes 584 | tf_op jit(solution)/shard_map/ppermute | solution.py:33
  3.4 10.6 %collective-permute-start.1 = (f32[4,8,256]{2,1,0:T(8,128)}, f32[4,8,256]{2,1,0:T(8,128)S(1)}, u32[]{:S(2)}, u32[]{:S(2)}) collective-permute-start(f32[4,8,256]{2,1,0:T(8,128)} %param.24), channel_id=1, source_target_pairs={{1,0},{0,1},{3,2},{2,3},{5,4},{4,5},{7,6},{6,7},{9,8},{8,9},{11,10... | collective-permute-start | bytes 98312 | tf_op jit(solution)/shard_map/ppermute | solution.py:33
  7.1 6.0 %copy-start.6 = (s32[8,64]{1,0:T(8,128)S(1)}, s32[8,64]{1,0:T(8,128)}, u32[]{:S(2)}) copy-start(s32[8,64]{1,0:T(8,128)} %param.16) | copy-start | bytes 6148
  7.1 6.0 %copy-start.7 = (f32[3,64]{1,0:T(4,128)S(1)}, f32[3,64]{1,0:T(4,128)}, u32[]{:S(2)}) copy-start(f32[3,64]{1,0:T(4,128)} %param.14) | copy-start | bytes 2308
  7.1 6.5 %copy-start.2 = (f32[3,8,64]{2,1,0:T(8,128)S(1)}, f32[3,8,64]{2,1,0:T(8,128)}, u32[]{:S(2)}) copy-start(f32[3,8,64]{2,1,0:T(8,128)} %param.18) | copy-start | bytes 18436
  7.1 6.5 %copy-start.4 = (f32[2,64]{1,0:T(2,128)S(1)}, f32[2,64]{1,0:T(2,128)}, u32[]{:S(2)}) copy-start(f32[2,64]{1,0:T(2,128)} %param.20) | copy-start | bytes 1540
  7.2 14.9 %copy-start = (bf16[4,256,256]{2,1,0:T(8,128)(2,1)S(1)}, bf16[4,256,256]{2,1,0:T(8,128)(2,1)}, u32[]{:S(2)}) copy-start(bf16[4,256,256]{2,1,0:T(8,128)(2,1)} %constant.104.plane_ref) | copy-start | bytes 1572868
  7.2 14.9 %copy-start.1 = (f32[21,16,256]{2,1,0:T(8,128)S(1)}, f32[21,16,256]{2,1,0:T(8,128)}, u32[]{:S(2)}) copy-start(f32[21,16,256]{2,1,0:T(8,128)} %constant.89.clone.green_ref) | copy-start | bytes 1032196
  10.0 11.9 %collective-permute-start.2 = (f32[7,8,8,256]{3,2,1,0:T(8,128)S(1)}, f32[7,8,8,256]{3,2,1,0:T(8,128)S(1)}, u32[]{:S(2)}, u32[]{:S(2)}) collective-permute-start(f32[7,8,8,256]{3,2,1,0:T(8,128)S(1)} %bitcast.83), channel_id=1, source_target_pairs={{1,0},{0,1},{3,2},{2,3},{5,4},{4,5},{7,6},{6,7},{9,8},{8,9},{11,10... | collective-permute-start | bytes 1376264 | tf_op jit(solution)/shard_map/ppermute | solution.py:33
  32.6 11.8 %collective-permute-start.7 = (f32[7,8,8,256]{3,2,1,0:T(8,128)S(1)}, f32[7,8,8,256]{3,2,1,0:T(8,128)S(1)}, u32[]{:S(2)}, u32[]{:S(2)}) collective-permute-start(f32[7,8,8,256]{3,2,1,0:T(8,128)S(1)} %get-tuple-element.15), channel_id=1, source_target_pairs={{1,0},{0,1},{3,2},{2,3},{5,4},{4,5},{7,6},{6,7},{9,8},{8,9},{11,10... | collective-permute-start | bytes 1376264 | tf_op jit(solution)/shard_map/ppermute | solution.py:33
  33.7 12.3 %all-to-all-start = ((f32[16,1,3]{2,1,0:T(1,128)}), f32[16,1,3]{2,1,0:T(1,128)S(1)}, u32[]{:S(2)}, u32[]{:S(2)}) async-start(f32[16,1,3]{2,1,0:T(1,128)} %copy.88), calls=%async_computation | async-start | bytes 16384 | tf_op jit(solution)/shard_map/all_to_all | solution.py:416
  46.0 55.4 %all-to-all-start.1 = ((f32[7,16,8,256]{3,2,0,1:T(8,128)}), f32[7,16,8,256]{3,2,0,1:T(8,128)}, u32[]{:S(2)}, u32[]{:S(2)}) async-start(f32[7,16,8,256]{3,2,0,1:T(8,128)} %copy.89), calls=%async_computation.1 | async-start | bytes 1835008 | tf_op jit(solution)/shard_map/all_to_all | solution.py:442
  55.6 11.9 %collective-permute-start.3 = (f32[7,8,8,256]{3,2,1,0:T(8,128)}, f32[7,8,8,256]{3,2,1,0:T(8,128)S(1)}, u32[]{:S(2)}, u32[]{:S(2)}) collective-permute-start(f32[7,8,8,256]{3,2,1,0:T(8,128)} %bitcast.75), channel_id=1, source_target_pairs={{1,0},{0,1},{3,2},{2,3},{5,4},{4,5},{7,6},{6,7},{9,8},{8,9},{11,10... | collective-permute-start | bytes 1376264 | tf_op jit(solution)/shard_map/ppermute | solution.py:33
  59.4 19.1 %collective-permute-start.4 = (f32[7,8,8,256]{3,2,1,0:T(8,128)}, f32[7,8,8,256]{3,2,1,0:T(8,128)S(1)}, u32[]{:S(2)}, u32[]{:S(2)}) collective-permute-start(f32[7,8,8,256]{3,2,1,0:T(8,128)} %bitcast.73), channel_id=1, source_target_pairs={{1,0},{0,1},{3,2},{2,3},{5,4},{4,5},{7,6},{6,7},{9,8},{8,9},{11,10... | collective-permute-start | bytes 1376264 | tf_op jit(solution)/shard_map/ppermute | solution.py:33
  78.2 12.2 %collective-permute-start.8 = (f32[7,8,8,256]{3,2,1,0:T(8,128)S(1)}, f32[7,8,8,256]{3,2,1,0:T(8,128)S(1)}, u32[]{:S(2)}, u32[]{:S(2)}) collective-permute-start(f32[7,8,8,256]{3,2,1,0:T(8,128)S(1)} %get-tuple-element.17), channel_id=1, source_target_pairs={{1,0},{0,1},{3,2},{2,3},{5,4},{4,5},{7,6},{6,7},{9,8},{8,9},{11,10... | collective-permute-start | bytes 1376264 | tf_op jit(solution)/shard_map/ppermute | solution.py:33
  89.1 9.7 %collective-permute-start.9 = (f32[7,8,8,256]{3,2,1,0:T(8,128)S(1)}, f32[7,8,8,256]{3,2,1,0:T(8,128)S(1)}, u32[]{:S(2)}, u32[]{:S(2)}) collective-permute-start(f32[7,8,8,256]{3,2,1,0:T(8,128)S(1)} %get-tuple-element.19), channel_id=1, source_target_pairs={{1,0},{0,1},{3,2},{2,3},{5,4},{4,5},{7,6},{6,7},{9,8},{8,9},{11,10... | collective-permute-start | bytes 1376264 | tf_op jit(solution)/shard_map/ppermute | solution.py:33
  101.4 12.8 %copy-start.5 = (f32[64]{0:T(128)S(1)}, f32[64]{0:T(128)}, u32[]{:S(2)}) copy-start(f32[64]{0:T(128)} %param.19) | copy-start | bytes 772
  101.4 50.8 %copy-start.8 = (f32[3,64]{1,0:T(4,128)S(1)}, f32[3,64]{1,0:T(4,128)}, u32[]{:S(2)}) copy-start(f32[3,64]{1,0:T(4,128)} %param.15) | copy-start | bytes 2308
  101.4 50.8 %copy-start.9 = (s32[16]{0:T(128)S(1)}, s32[16]{0:T(128)}, u32[]{:S(2)}) copy-start(s32[16]{0:T(128)} %param.17) | copy-start | bytes 196
  101.4 52.9 %all-to-all-start.2 = ((f32[7,16,2,8,256]{4,3,0,2,1:T(8,128)}), f32[7,16,2,8,256]{4,3,0,2,1:T(8,128)S(1)}, u32[]{:S(2)}, u32[]{:S(2)}) async-start(f32[7,16,2,8,256]{4,3,0,2,1:T(8,128)} %copy.90), calls=%async_computation.2 | async-start | bytes 3670016 | tf_op jit(solution)/shard_map/all_to_all | solution.py:445
  110.9 2.9 %collective-permute-start.5 = (f32[6,3,8]{2,1,0:T(4,128)S(1)}, f32[6,3,8]{2,1,0:T(4,128)S(1)}, u32[]{:S(2)}, u32[]{:S(2)}) collective-permute-start(f32[6,3,8]{2,1,0:T(4,128)S(1)} %pad_maximum_fusion.1), channel_id=1, source_target_pairs={{1,0},{0,1},{3,2},{2,3},{5,4},{4,5},{7,6},{6,7},{9,8},{8,9},{11,10... | collective-permute-start | bytes 1736 | tf_op jit(solution)/shard_map/ppermute | solution.py:33
  114.6 37.7 %collective-permute-start.6 = (f32[3,16]{1,0:T(4,128)S(1)}, f32[3,16]{1,0:T(4,128)S(1)}, u32[]{:S(2)}, u32[]{:S(2)}) collective-permute-start(f32[3,16]{1,0:T(4,128)S(1)} %slice.99), channel_id=1, source_target_pairs={{2,0},{4,2},{6,4},{8,6},{10,8},{12,10},{14,12},{16,14},{18,16},{20... | collective-permute-start | bytes 584 | tf_op jit(solution)/shard_map/ppermute | solution.py:33

commit v4 on v3

--- a/solution.py
+++ b/solution.py
@@ -412,41 +412,59 @@
     slot_valid = jnp.sum(match_float, axis=1)
     slot_source = jnp.sum(jnp.where(slot_match, point_ids[None, :], 0), axis=1)
     slot_strain = jnp.dot(strain, match_float.T, precision=FULL_PREC)
+    here = capacity - 1 if capacity > 1 else capacity
+    full_width = groups * here
     valid_rows = jnp.swapaxes(slot_valid.reshape(capacity, groups), 0, 1)
-    got_valid = lax.all_to_all(valid_rows, "macro", split_axis=0, concat_axis=0, tiled=True)
-    full = got_valid.reshape(-1) > 0.5
-    places = jnp.arange(groups * capacity, dtype=jnp.int32)
-    origin, turn = places // capacity, places % capacity
-    places = jnp.where(turn == 0, origin, groups + origin * (capacity - 1) + turn - 1)
+    if here < capacity:
+        early = lax.all_to_all(
+            state[:, slot_source[full_width:]], "macro", split_axis=1, concat_axis=1, tiled=True
+        )
+        valid_rows = jnp.concatenate([valid_rows, slot_strain[:, full_width:].T], axis=1)
+    got_rows = lax.all_to_all(valid_rows, "macro", split_axis=0, concat_axis=0, tiled=True)
+    full = got_rows[:, :capacity].reshape(-1) > 0.5
+    places = slot_ids % capacity * groups + slot_ids // capacity
     earlier = (slot_ids[:, None] < slot_ids[None, :]) & full[:, None]
     position = jnp.sum(earlier.astype(jnp.int32), axis=0)
     wanted = jnp.arange(RECV_AGG, dtype=jnp.int32)
     wanted_match = (wanted[:, None] == position[None, :]) & full[None, :]
     order = jnp.sum(jnp.where(wanted_match, places[None, :], 0), axis=1)
-    solved, means = [], []
-    for chunk in range(capacity):
-        base = chunk * groups
+
+    def solve_chunk(select, chunk_strain):
         pieces = []
         for d in range(ranks):
-            solver = base + (me - d) % ranks * per_rank
-            sources = lax.dynamic_slice_in_dim(slot_source, solver, per_rank, 0)
-            piece = jnp.swapaxes(state[:, sources], 1, 2)
+            piece = jnp.swapaxes(select((me - d) % ranks * per_rank), 1, 2)
             pieces.append(shifted(piece, "vox", -d) if d else piece)
-        mine = base + me * per_rank
-        own_strain = lax.dynamic_slice_in_dim(slot_strain, mine, per_rank, 1)
+        own_strain = lax.dynamic_slice_in_dim(chunk_strain, me * per_rank, per_rank, 1)
         updated, mean = micro_solve(pieces, own_strain, moduli, tables)
+        slabs = [updated[0]] + [shifted(updated[d], "vox", d) for d in range(1, ranks)]
+        return jnp.swapaxes(by_rank(slabs, 2), 1, 2), mean
+
+    moved, means = [], []
+    for chunk in range(here):
+        base = chunk * groups
+
+        def select(start, base=base):
+            return state[:, lax.dynamic_slice_in_dim(slot_source, base + start, per_rank, 0)]
+
+        slabs, mean = solve_chunk(select, slot_strain[:, base : base + groups])
         means.append(mean)
-        slabs = [updated[0]] + [shifted(updated[d], "vox", d) for d in range(1, ranks)]
-        slabs = jnp.swapaxes(by_rank(slabs, 2), 1, 2)
-        solved.append(slabs)
-    moved = [lax.all_to_all(solved[0], "macro", split_axis=1, concat_axis=1, tiled=True)]
-    if capacity > 1:
-        rest = jnp.stack(solved[1:], axis=2)
-        rest = lax.all_to_all(rest, "macro", split_axis=1, concat_axis=1, tiled=True)
-        moved.append(rest.reshape((7, -1) + rest.shape[3:]))
+        moved.append(lax.all_to_all(slabs, "macro", split_axis=1, concat_axis=1, tiled=True))
+    if here < capacity:
+
+        def select(start):
+            return lax.dynamic_slice_in_dim(early, start, per_rank, 1)
+
+        slabs, mean = solve_chunk(select, got_rows[:, capacity:].T)
+        means.append(mean)
+        moved.append(slabs)
     own_mean = jnp.stack(means, axis=1)
     parts = [own_mean] + [shifted(own_mean, "vox", d) for d in range(1, ranks)]
     averaged = by_rank(parts, 2).reshape(6, capacity * groups)
+    if here < capacity:
+        returned = lax.all_to_all(
+            averaged[:, full_width:].T, "macro", split_axis=0, concat_axis=0, tiled=True
+        )
+        averaged = jnp.concatenate([averaged[:, :full_width], returned.T], axis=1)
     stress_plastic = jnp.dot(averaged, match_float, precision=FULL_PREC)
     stress = jnp.where(plastic[None, :], stress_plastic, elastic_stress(strain, elastic_moduli))
     forces = nodal_forces(stress, grad_ops, volume)

time: 157 us -> 160 us (1.019)
  the two profiles are of different devices: /device:TPU:11 before, /device:TPU:0 now
where the time goes in v4:
time: 160 us; the launch traced here: 158 us
  waiting for transfers between devices  46.3 us (29%)
  starting transfers between devices  39.8 us (25%)
  Pallas kernels  34.2 us (21%)
  local copies, waits for them, and re-layouts  25.6 us (16%)
  other arithmetic  7.14 us (4%)
  matrix products  3.41 us (2%)
    pallas_call x3, Pallas kernels, micro_solve(): pl.pallas_call(functools.partial(solve_kernel, ranks), out_shape=[jax.Sha...  31.8 us
    ppermute x10, waiting for transfers between devices, shifted(): return lax.ppermute(block, axis, route)  24.8 us
    ppermute x10, starting transfers between devices, shifted(): return lax.ppermute(block, axis, route)  16 us
    gather x8, local copies, waits for them, and re-layouts, select(): state[:, lax.dynamic_slice_in_dim(slot_source, base + start, per_rank, 0)]  12.6 us
    all_to_all x2, waiting for transfers between devices, local(): lax.all_to_all(slabs, 'macro', split_axis=1, concat_axis=1, tiled=True)  10.7 us
    all_to_all x2, starting transfers between devices, local(): lax.all_to_all(slabs, 'macro', split_axis=1, concat_axis=1, tiled=True)  9.72 us
    all_to_all x1, starting transfers between devices, local(): lax.all_to_all(averaged[:, full_width:].T, 'macro', split_axis=0, concat_...  6.04 us
    all_to_all x1, starting transfers between devices, local(): lax.all_to_all(state[:, slot_source[full_width:]], 'macro', split_axis=1,...  4.31 us
  transfers between devices with their start and end apart: 15, of which 9 were waited for; matrix products, arithmetic and copies ran while one was open for 19% of the time, Pallas kernels for 20%

profile of v4, /device:TPU:0, one launch (start us, length us, event | category | flops | bytes accessed | tf_op | source)
XLA Modules:
  0.0 157.5 jit_solution(1493291747062367072)
XLA Ops:
  4.7 3.6 %collective-permute-done = f32[3,16]{1,0:T(4,128)S(1)} collective-permute-done((f32[3,16]{1,0:T(4,128)S(1)}, f32[3,16]{1,0:T(4,128)S(1)}, u32[]{:S(2)}, u32[]{:S(2)}) %collective-permute-start) | collective-permute-done | bytes 224 | tf_op jit(solution)/shard_map/ppermute | solution.py:33
  11.9 3.7 %all-to-all-start = ((f32[16,1,9]{2,1,0:T(1,128)}), f32[16,1,9]{2,1,0:T(1,128)S(1)}, u32[]{:S(2)}, u32[]{:S(2)}) async-start(f32[16,1,9]{2,1,0:T(1,128)} %copy.106), calls=%async_computation | async-start | bytes 16384 | tf_op jit(solution)/shard_map/all_to_all | solution.py:423
  15.6 3.6 %gather_fusion.4 = f32[16,7,8,256]{3,2,1,0:T(8,128)} fusion(f32[7,64,8,256]{3,2,1,0:T(8,128)} %param.23, s32[1024]{0:T(1024)S(1)} %pad_clamp_fusion), kind=kCustom, calls=%fused_computation.4 | custom fusion | bytes 1835072 | tf_op jit(solution)/shard_map/gather | solution.py:420
  19.2 2.8 %all-to-all-done = f32[16,1,9]{2,1,0:T(1,128)S(1)} async-done(((f32[16,1,9]{2,1,0:T(1,128)}), f32[16,1,9]{2,1,0:T(1,128)S(1)}, u32[]{:S(2)}, u32[]{:S(2)}) %all-to-all-start) | async-done | bytes 608 | tf_op jit(solution)/shard_map/all_to_all | solution.py:423
  22.1 4.3 %all-to-all-start.1 = ((f32[7,16,8,256]{3,2,0,1:T(8,128)}), f32[7,16,8,256]{3,2,0,1:T(8,128)}, u32[]{:S(2)}, u32[]{:S(2)}) async-start(f32[7,16,8,256]{3,2,0,1:T(8,128)} %bitcast.17), calls=%async_computation.1 | async-start | bytes 1835008 | tf_op jit(solution)/shard_map/all_to_all | solution.py:419
  28.3 2.6 %gather_fusion.1 = f32[8,7,8,256]{3,2,1,0:T(8,128)S(1)} fusion(f32[7,64,8,256]{3,2,1,0:T(8,128)} %param.23, s32[1024]{0:T(1024)S(1)} %get-tuple-element.74), kind=kCustom, calls=%fused_computation.1 | custom fusion | bytes 917536 | tf_op jit(solution)/shard_map/gather | solution.py:447
  32.1 2.6 %gather_fusion.3 = f32[8,7,8,256]{3,2,1,0:T(8,128)S(1)} fusion(f32[7,64,8,256]{3,2,1,0:T(8,128)} %param.23, s32[1024]{0:T(1024)S(1)} %get-tuple-element.72), kind=kCustom, calls=%fused_computation.3 | custom fusion | bytes 917536 | tf_op jit(solution)/shard_map/gather | solution.py:447
  37.5 2.6 %gather_fusion.2 = f32[8,7,8,256]{3,2,1,0:T(8,128)S(1)} fusion(f32[7,64,8,256]{3,2,1,0:T(8,128)} %param.23, s32[1024]{0:T(1024)S(1)} %get-tuple-element.73), kind=kCustom, calls=%fused_computation.2 | custom fusion | bytes 917536 | tf_op jit(solution)/shard_map/gather | solution.py:447
  40.2 2.6 %gather_fusion = f32[8,7,8,256]{3,2,1,0:T(8,128)S(1)} fusion(f32[7,64,8,256]{3,2,1,0:T(8,128)} %param.23, s32[1024]{0:T(1024)S(1)} %get-tuple-element.75), kind=kCustom, calls=%fused_computation | custom fusion | bytes 917536 | tf_op jit(solution)/shard_map/gather | solution.py:447
  43.3 3.8 %all-to-all-done.1 = f32[7,16,8,256]{3,2,0,1:T(8,128)} async-done(((f32[7,16,8,256]{3,2,0,1:T(8,128)}), f32[7,16,8,256]{3,2,0,1:T(8,128)}, u32[]{:S(2)}, u32[]{:S(2)}) %all-to-all-start.1) | async-done | bytes 917536 | tf_op jit(solution)/shard_map/all_to_all | solution.py:419
  50.5 10.6 %shard_map.149 = (f32[7,8,8,256]{3,2,1,0:T(8,128)S(1)}, f32[7,8,8,256]{3,2,1,0:T(8,128)S(1)}, f32[6,8,128]{2,1,0:T(8,128)S(1)}) custom-call(f32[6,8,256]{2,1,0:T(8,128)S(1)} %broadcast_in_dim.51.strain_ref, f32[4,16,256]{2,1,0:T(8,128)S(1)} %constant_dynamic-update-slice_fusion.props_ref, f32[21,16,256]{2,1,0:T(8,128)S(1)} %copy-done.1, ...), custom_call_target="tpu_custom_call" | custom-call | flops 2415919104 | bytes 1835008 | tf_op jit(solution)/shard_map/pallas_call | solution.py:270
  62.4 10.6 %shard_map.150 = (f32[7,8,8,256]{3,2,1,0:T(8,128)S(1)}, f32[7,8,8,256]{3,2,1,0:T(8,128)S(1)}, f32[6,8,128]{2,1,0:T(8,128)S(1)}) custom-call(f32[6,8,256]{2,1,0:T(8,128)S(1)} %broadcast_in_dim.56.strain_ref, f32[4,16,256]{2,1,0:T(8,128)S(1)} %constant_dynamic-update-slice_fusion.props_ref, f32[21,16,256]{2,1,0:T(8,128)S(1)} %copy-done.2, ...), custom_call_target="tpu_custom_call" | custom-call | flops 2415919104 | bytes 1835008 | tf_op jit(solution)/shard_map/pallas_call | solution.py:270
  73.3 10.6 %shard_map.151 = (f32[7,8,8,256]{3,2,1,0:T(8,128)S(1)}, f32[7,8,8,256]{3,2,1,0:T(8,128)S(1)}, f32[6,8,128]{2,1,0:T(8,128)S(1)}) custom-call(f32[6,8,256]{2,1,0:T(8,128)S(1)} %broadcast_in_dim.62.strain_ref, f32[4,16,256]{2,1,0:T(8,128)S(1)} %constant_dynamic-update-slice_fusion.props_ref, f32[21,16,256]{2,1,0:T(8,128)S(1)} %copy-done.2, ...), custom_call_target="tpu_custom_call" | custom-call | flops 2415919104 | bytes 1835008 | tf_op jit(solution)/shard_map/pallas_call | solution.py:270
  84.1 1.8 %collective-permute-start.5 = (f32[6,3,8]{2,1,0:T(4,128)S(1)}, f32[6,3,8]{2,1,0:T(4,128)S(1)}, u32[]{:S(2)}, u32[]{:S(2)}) collective-permute-start(f32[6,3,8]{2,1,0:T(4,128)S(1)} %pad_maximum_fusion), channel_id=1, source_target_pairs={{1,0},{0,1},{3,2},{2,3},{5,4},{4,5},{7,6},{6,7},{9,8},{8,9},{11,10... | collective-permute-start | bytes 1736 | tf_op jit(solution)/shard_map/ppermute | solution.py:33
  88.8 6.0 %all-to-all-start.2 = ((f32[16,1,6]{2,1,0:T(1,128)}), f32[16,1,6]{2,1,0:T(1,128)S(1)}, u32[]{:S(2)}, u32[]{:S(2)}) async-start(f32[16,1,6]{2,1,0:T(1,128)} %copy.110), calls=%async_computation.2 | async-start | bytes 16384 | tf_op jit(solution)/shard_map/all_to_all | solution.py:464
  97.1 4.2 %all-to-all-done.2 = f32[16,1,6]{2,1,0:T(1,128)S(1)} async-done(((f32[16,1,6]{2,1,0:T(1,128)}), f32[16,1,6]{2,1,0:T(1,128)S(1)}, u32[]{:S(2)}, u32[]{:S(2)}) %all-to-all-start.2) | async-done | bytes 416 | tf_op jit(solution)/shard_map/all_to_all | solution.py:464
  101.2 3.6 %all-to-all-start.3 = ((f32[7,16,8,256]{3,2,0,1:T(8,128)}), f32[7,16,8,256]{3,2,0,1:T(8,128)S(1)}, u32[]{:S(2)}, u32[]{:S(2)}) async-start(f32[7,16,8,256]{3,2,0,1:T(8,128)} %copy.116), calls=%async_computation.3 | async-start | bytes 1835008 | tf_op jit(solution)/shard_map/all_to_all | solution.py:451
  107.1 10.7 %collective-permute-done.8 = f32[7,8,8,256]{3,1,2,0:T(8,128)S(1)} collective-permute-done((f32[7,8,8,256]{3,1,2,0:T(8,128)S(1)}, f32[7,8,8,256]{3,1,2,0:T(8,128)S(1)}, u32[]{:S(2)}, u32[]{:S(2)}) %collective-permute-start.8) | collective-permute-done | bytes 458784 | tf_op jit(solution)/shard_map/ppermute | solution.py:33
  119.0 6.7 %all-to-all-done.3 = f32[7,16,8,256]{3,2,0,1:T(8,128)S(1)} async-done(((f32[7,16,8,256]{3,2,0,1:T(8,128)}), f32[7,16,8,256]{3,2,0,1:T(8,128)S(1)}, u32[]{:S(2)}, u32[]{:S(2)}) %all-to-all-start.3) | async-done | bytes 917536 | tf_op jit(solution)/shard_map/all_to_all | solution.py:451
  125.6 6.1 %all-to-all-start.4 = ((f32[7,16,8,256]{3,2,0,1:T(8,128)}), f32[7,16,8,256]{3,2,0,1:T(8,128)}, u32[]{:S(2)}, u32[]{:S(2)}) async-start(f32[7,16,8,256]{3,2,0,1:T(8,128)} %copy.120), calls=%async_computation.4 | async-start | bytes 1835008 | tf_op jit(solution)/shard_map/all_to_all | solution.py:451
  134.7 4.0 %collective-permute-start.6 = (f32[3,16]{1,0:T(4,128)S(1)}, f32[3,16]{1,0:T(4,128)S(1)}, u32[]{:S(2)}, u32[]{:S(2)}) collective-permute-start(f32[3,16]{1,0:T(4,128)S(1)} %slice.130), channel_id=1, source_target_pairs={{2,0},{4,2},{6,4},{8,6},{10,8},{12,10},{14,12},{16,14},{18,16},{20... | collective-permute-start | bytes 584 | tf_op jit(solution)/shard_map/ppermute | solution.py:33
  139.0 8.7 %collective-permute-done.6 = f32[3,16]{1,0:T(4,128)S(1)} collective-permute-done((f32[3,16]{1,0:T(4,128)S(1)}, f32[3,16]{1,0:T(4,128)S(1)}, u32[]{:S(2)}, u32[]{:S(2)}) %collective-permute-start.6) | collective-permute-done | bytes 224 | tf_op jit(solution)/shard_map/ppermute | solution.py:33
  148.5 4.0 %all-to-all-done.4 = f32[7,16,8,256]{3,2,0,1:T(8,128)} async-done(((f32[7,16,8,256]{3,2,0,1:T(8,128)}), f32[7,16,8,256]{3,2,0,1:T(8,128)}, u32[]{:S(2)}, u32[]{:S(2)}) %all-to-all-start.4) | async-done | bytes 917536 | tf_op jit(solution)/shard_map/all_to_all | solution.py:451
  155.1 2.5 %shard_map.152 = f32[7,24,8,256]{3,2,1,0:T(8,128)} custom-call(s32[24]{0:T(128)S(1)} %select_reduce_fusion.1.order_ref, f32[7,16,8,256]{3,2,1,0:T(8,128)S(1)} %copy.124.refs_0_, f32[7,16,8,256]{3,2,1,0:T(8,128)S(1)} %copy.125.refs_1_, f32[7,16,8,256]{3,2,1,0:T(8,128)S(1)} %fusion.3.refs_2_), custom_call_target="tpu_custom_call" | custom-call | tf_op jit(solution)/shard_map/pallas_call | solution.py:314
  (112 shorter events, 34.0 us)
Async XLA Ops:
  0.6 25.7 %copy-start.4 = (f32[4,8,256]{2,1,0:T(8,128)S(1)}, f32[4,8,256]{2,1,0:T(8,128)}, u32[]{:S(2)}) copy-start(f32[4,8,256]{2,1,0:T(8,128)} %param.24) | copy-start | bytes 98308
  1.5 6.7 %collective-permute-start = (f32[3,16]{1,0:T(4,128)S(1)}, f32[3,16]{1,0:T(4,128)S(1)}, u32[]{:S(2)}, u32[]{:S(2)}) collective-permute-start(f32[3,16]{1,0:T(4,128)S(1)} %convolution_bitcast_fusion.1), channel_id=1, source_target_pairs={{30,0},{0,2},{2,4},{4,6},{6,8},{8,10},{10,12},{12,14},{14,16},{16,... | collective-permute-start | bytes 584 | tf_op jit(solution)/shard_map/ppermute | solution.py:33
  11.9 10.1 %all-to-all-start = ((f32[16,1,9]{2,1,0:T(1,128)}), f32[16,1,9]{2,1,0:T(1,128)S(1)}, u32[]{:S(2)}, u32[]{:S(2)}) async-start(f32[16,1,9]{2,1,0:T(1,128)} %copy.106), calls=%async_computation | async-start | bytes 16384 | tf_op jit(solution)/shard_map/all_to_all | solution.py:423
  22.1 25.1 %all-to-all-start.1 = ((f32[7,16,8,256]{3,2,0,1:T(8,128)}), f32[7,16,8,256]{3,2,0,1:T(8,128)}, u32[]{:S(2)}, u32[]{:S(2)}) async-start(f32[7,16,8,256]{3,2,0,1:T(8,128)} %bitcast.17), calls=%async_computation.1 | async-start | bytes 1835008 | tf_op jit(solution)/shard_map/all_to_all | solution.py:419
  26.4 17.0 %collective-permute-start.1 = (f32[4,8,256]{2,1,0:T(8,128)S(1)}, f32[4,8,256]{2,1,0:T(8,128)S(1)}, u32[]{:S(2)}, u32[]{:S(2)}) collective-permute-start(f32[4,8,256]{2,1,0:T(8,128)S(1)} %copy-done.4), channel_id=1, source_target_pairs={{1,0},{0,1},{3,2},{2,3},{5,4},{4,5},{7,6},{6,7},{9,8},{8,9},{11,10... | collective-permute-start | bytes 98312 | tf_op jit(solution)/shard_map/ppermute | solution.py:33
  31.9 18.5 %collective-permute-start.2 = (f32[7,8,8,256]{3,2,1,0:T(8,128)}, f32[7,8,8,256]{3,2,1,0:T(8,128)S(1)}, u32[]{:S(2)}, u32[]{:S(2)}) collective-permute-start(f32[7,8,8,256]{3,2,1,0:T(8,128)} %bitcast.84), channel_id=1, source_target_pairs={{1,0},{0,1},{3,2},{2,3},{5,4},{4,5},{7,6},{6,7},{9,8},{8,9},{11,10... | collective-permute-start | bytes 1376264 | tf_op jit(solution)/shard_map/ppermute | solution.py:33
  34.8 15.7 %copy-start = (bf16[4,256,256]{2,1,0:T(8,128)(2,1)S(1)}, bf16[4,256,256]{2,1,0:T(8,128)(2,1)}, u32[]{:S(2)}) copy-start(bf16[4,256,256]{2,1,0:T(8,128)(2,1)} %constant.95.plane_ref) | copy-start | bytes 1572868
  34.8 15.7 %copy-start.1 = (f32[21,16,256]{2,1,0:T(8,128)S(1)}, f32[21,16,256]{2,1,0:T(8,128)}, u32[]{:S(2)}) copy-start(f32[21,16,256]{2,1,0:T(8,128)} %constant.80.clone.green_ref) | copy-start | bytes 1032196
  35.7 26.6 %collective-permute-start.3 = (f32[7,8,8,256]{3,2,1,0:T(8,128)}, f32[7,8,8,256]{3,2,1,0:T(8,128)S(1)}, u32[]{:S(2)}, u32[]{:S(2)}) collective-permute-start(f32[7,8,8,256]{3,2,1,0:T(8,128)} %bitcast.82), channel_id=1, source_target_pairs={{1,0},{0,1},{3,2},{2,3},{5,4},{4,5},{7,6},{6,7},{9,8},{8,9},{11,10... | collective-permute-start | bytes 1376264 | tf_op jit(solution)/shard_map/ppermute | solution.py:33
  48.6 24.7 %collective-permute-start.4 = (f32[7,8,8,256]{3,2,1,0:T(8,128)S(1)}, f32[7,8,8,256]{3,2,1,0:T(8,128)S(1)}, u32[]{:S(2)}, u32[]{:S(2)}) collective-permute-start(f32[7,8,8,256]{3,2,1,0:T(8,128)S(1)} %bitcast.90), channel_id=1, source_target_pairs={{1,0},{0,1},{3,2},{2,3},{5,4},{4,5},{7,6},{6,7},{9,8},{8,9},{11,10... | collective-permute-start | bytes 1376264 | tf_op jit(solution)/shard_map/ppermute | solution.py:33
  62.1 32.7 %collective-permute-start.7 = (f32[7,8,8,256]{3,1,2,0:T(8,128)}, f32[7,8,8,256]{3,1,2,0:T(8,128)}, u32[]{:S(2)}, u32[]{:S(2)}) collective-permute-start(f32[7,8,8,256]{3,1,2,0:T(8,128)} %copy.113), channel_id=1, source_target_pairs={{1,0},{0,1},{3,2},{2,3},{5,4},{4,5},{7,6},{6,7},{9,8},{8,9},{11,10... | collective-permute-start | bytes 1376264 | tf_op jit(solution)/shard_map/ppermute | solution.py:33
  84.1 3.8 %collective-permute-start.5 = (f32[6,3,8]{2,1,0:T(4,128)S(1)}, f32[6,3,8]{2,1,0:T(4,128)S(1)}, u32[]{:S(2)}, u32[]{:S(2)}) collective-permute-start(f32[6,3,8]{2,1,0:T(4,128)S(1)} %pad_maximum_fusion), channel_id=1, source_target_pairs={{1,0},{0,1},{3,2},{2,3},{5,4},{4,5},{7,6},{6,7},{9,8},{8,9},{11,10... | collective-permute-start | bytes 1736 | tf_op jit(solution)/shard_map/ppermute | solution.py:33
  88.8 12.5 %all-to-all-start.2 = ((f32[16,1,6]{2,1,0:T(1,128)}), f32[16,1,6]{2,1,0:T(1,128)S(1)}, u32[]{:S(2)}, u32[]{:S(2)}) async-start(f32[16,1,6]{2,1,0:T(1,128)} %copy.110), calls=%async_computation.2 | async-start | bytes 16384 | tf_op jit(solution)/shard_map/all_to_all | solution.py:464
  101.2 24.4 %all-to-all-start.3 = ((f32[7,16,8,256]{3,2,0,1:T(8,128)}), f32[7,16,8,256]{3,2,0,1:T(8,128)S(1)}, u32[]{:S(2)}, u32[]{:S(2)}) async-start(f32[7,16,8,256]{3,2,0,1:T(8,128)} %copy.116), calls=%async_computation.3 | async-start | bytes 1835008 | tf_op jit(solution)/shard_map/all_to_all | solution.py:451
  104.9 26.8 %copy-start.5 = (f32[2,64]{1,0:T(2,128)S(1)}, f32[2,64]{1,0:T(2,128)}, u32[]{:S(2)}) copy-start(f32[2,64]{1,0:T(2,128)} %param.20) | copy-start | bytes 1540
  105.0 12.8 %collective-permute-start.8 = (f32[7,8,8,256]{3,1,2,0:T(8,128)S(1)}, f32[7,8,8,256]{3,1,2,0:T(8,128)S(1)}, u32[]{:S(2)}, u32[]{:S(2)}) collective-permute-start(f32[7,8,8,256]{3,1,2,0:T(8,128)S(1)} %copy.117), channel_id=1, source_target_pairs={{1,0},{0,1},{3,2},{2,3},{5,4},{4,5},{7,6},{6,7},{9,8},{8,9},{11,10... | collective-permute-start | bytes 1376264 | tf_op jit(solution)/shard_map/ppermute | solution.py:33
  106.9 27.4 %copy-start.3 = (f32[3,8,64]{2,1,0:T(8,128)S(1)}, f32[3,8,64]{2,1,0:T(8,128)}, u32[]{:S(2)}) copy-start(f32[3,8,64]{2,1,0:T(8,128)} %param.18) | copy-start | bytes 18436
  106.9 27.3 %copy-start.6 = (f32[64]{0:T(128)S(1)}, f32[64]{0:T(128)}, u32[]{:S(2)}) copy-start(f32[64]{0:T(128)} %param.19) | copy-start | bytes 772
  106.9 27.4 %copy-start.7 = (s32[8,64]{1,0:T(8,128)S(1)}, s32[8,64]{1,0:T(8,128)}, u32[]{:S(2)}) copy-start(s32[8,64]{1,0:T(8,128)} %param.16) | copy-start | bytes 6148
  107.1 40.6 %copy-start.8 = (f32[3,64]{1,0:T(4,128)S(1)}, f32[3,64]{1,0:T(4,128)}, u32[]{:S(2)}) copy-start(f32[3,64]{1,0:T(4,128)} %param.15) | copy-start | bytes 2308
  107.1 40.6 %copy-start.9 = (s32[16]{0:T(128)S(1)}, s32[16]{0:T(128)}, u32[]{:S(2)}) copy-start(s32[16]{0:T(128)} %param.17) | copy-start | bytes 196
  125.6 26.9 %all-to-all-start.4 = ((f32[7,16,8,256]{3,2,0,1:T(8,128)}), f32[7,16,8,256]{3,2,0,1:T(8,128)}, u32[]{:S(2)}, u32[]{:S(2)}) async-start(f32[7,16,8,256]{3,2,0,1:T(8,128)} %copy.120), calls=%async_computation.4 | async-start | bytes 1835008 | tf_op jit(solution)/shard_map/all_to_all | solution.py:451
  132.1 21.7 %collective-permute-start.9 = (f32[7,8,8,256]{3,1,2,0:T(8,128)S(1)}, f32[7,8,8,256]{3,1,2,0:T(8,128)}, u32[]{:S(2)}, u32[]{:S(2)}) collective-permute-start(f32[7,8,8,256]{3,1,2,0:T(8,128)S(1)} %copy.121), channel_id=1, source_target_pairs={{1,0},{0,1},{3,2},{2,3},{5,4},{4,5},{7,6},{6,7},{9,8},{8,9},{11,10... | collective-permute-start | bytes 1376264 | tf_op jit(solution)/shard_map/ppermute | solution.py:33
  134.7 13.0 %collective-permute-start.6 = (f32[3,16]{1,0:T(4,128)S(1)}, f32[3,16]{1,0:T(4,128)S(1)}, u32[]{:S(2)}, u32[]{:S(2)}) collective-permute-start(f32[3,16]{1,0:T(4,128)S(1)} %slice.130), channel_id=1, source_target_pairs={{2,0},{4,2},{6,4},{8,6},{10,8},{12,10},{14,12},{16,14},{18,16},{20... | collective-permute-start | bytes 584 | tf_op jit(solution)/shard_map/ppermute | solution.py:33
  (1 other events, 11.9 us)

commit v5 on v4

--- a/solution.py
+++ b/solution.py
@@ -457,14 +457,15 @@
         slabs, mean = solve_chunk(select, got_rows[:, capacity:].T)
         means.append(mean)
         moved.append(slabs)
-    own_mean = jnp.stack(means, axis=1)
+    own_mean = jnp.stack(means[:here], axis=1)
     parts = [own_mean] + [shifted(own_mean, "vox", d) for d in range(1, ranks)]
-    averaged = by_rank(parts, 2).reshape(6, capacity * groups)
+    averaged = by_rank(parts, 2).reshape(6, full_width)
     if here < capacity:
+        parts = [means[here]] + [shifted(means[here], "vox", d) for d in range(1, ranks)]
         returned = lax.all_to_all(
-            averaged[:, full_width:].T, "macro", split_axis=0, concat_axis=0, tiled=True
+            by_rank(parts, 1).T, "macro", split_axis=0, concat_axis=0, tiled=True
         )
-        averaged = jnp.concatenate([averaged[:, :full_width], returned.T], axis=1)
+        averaged = jnp.concatenate([averaged, returned.T], axis=1)
     stress_plastic = jnp.dot(averaged, match_float, precision=FULL_PREC)
     stress = jnp.where(plastic[None, :], stress_plastic, elastic_stress(strain, elastic_moduli))
     forces = nodal_forces(stress, grad_ops, volume)

time: 160 us -> 165 us (1.031)
  waiting for transfers between devices: 46.3 us -> 51.6 us
    all_to_all x1, waiting for transfers between devices: 3.82 us -> 12.7 us  [local(): lax.all_to_all(state[:, slot_source[full_width:]], 'macro', split_axis=1,...]
    all_to_all x2, waiting for transfers between devices: 10.7 us -> 2.76 us  [local(): lax.all_to_all(slabs, 'macro', split_axis=1, concat_axis=1, tiled=True)]
    ppermute x10 -> x11, waiting for transfers between devices: 24.8 us -> 28.3 us  [shifted(): return lax.ppermute(block, axis, route)]
    all_to_all x1, starting transfers between devices: 6.04 us -> 3.44 us  [local(): lax.all_to_all(by_rank(parts, 1).T, 'macro', split_axis=0, concat_axis=0,...]
    all_to_all x1, starting transfers between devices: 3.68 us -> 6.08 us  [local(): lax.all_to_all(valid_rows, 'macro', split_axis=0, concat_axis=0, tiled=True)]
    ppermute x10 -> x11, starting transfers between devices: 16 us -> 15.7 us  [shifted(): return lax.ppermute(block, axis, route)]
  transfers between devices with their start and end apart: 15 -> 16, of which waited for: 9 -> 9; matrix products, arithmetic and copies ran while one was open for 19% -> 19% of each run, Pallas kernels for 20% -> 20%
where the time goes in v5:
time: 165 us; the launch traced here: 161 us
  waiting for transfers between devices  51.6 us (31%)
  starting transfers between devices  41.3 us (25%)
  Pallas kernels  34.2 us (21%)
  local copies, waits for them, and re-layouts  24.8 us (15%)
  other arithmetic  5.76 us (3%)
  matrix products  2.71 us (2%)
    pallas_call x3, Pallas kernels, micro_solve(): pl.pallas_call(functools.partial(solve_kernel, ranks), out_shape=[jax.Sha...  31.8 us
    ppermute x11, waiting for transfers between devices, shifted(): return lax.ppermute(block, axis, route)  28.3 us
    ppermute x11, starting transfers between devices, shifted(): return lax.ppermute(block, axis, route)  15.7 us
    all_to_all x1, waiting for transfers between devices, local(): lax.all_to_all(state[:, slot_source[full_width:]], 'macro', split_axis=1,...  12.7 us
    gather x8, local copies, waits for them, and re-layouts, select(): state[:, lax.dynamic_slice_in_dim(slot_source, base + start, per_rank, 0)]  11.1 us
    all_to_all x2, starting transfers between devices, local(): lax.all_to_all(slabs, 'macro', split_axis=1, concat_axis=1, tiled=True)  10.1 us
    all_to_all x1, starting transfers between devices, local(): lax.all_to_all(valid_rows, 'macro', split_axis=0, concat_axis=0, tiled=True)  6.08 us
    all_to_all x1, starting transfers between devices, local(): lax.all_to_all(state[:, slot_source[full_width:]], 'macro', split_axis=1,...  5.95 us
  transfers between devices with their start and end apart: 16, of which 9 were waited for; matrix products, arithmetic and copies ran while one was open for 19% of the time, Pallas kernels for 20%

profile of v5, /device:TPU:0, one launch (start us, length us, event | category | flops | bytes accessed | tf_op | source)
XLA Modules:
  0.0 161.4 jit_solution(4777191615809274244)
XLA Ops:
  2.0 2.5 %collective-permute-start.1 = (f32[4,8,256]{2,1,0:T(8,128)}, f32[4,8,256]{2,1,0:T(8,128)S(1)}, u32[]{:S(2)}, u32[]{:S(2)}) collective-permute-start(f32[4,8,256]{2,1,0:T(8,128)} %param.24), channel_id=1, source_target_pairs={{1,0},{0,1},{3,2},{2,3},{5,4},{4,5},{7,6},{6,7},{9,8},{8,9},{11,10... | collective-permute-start | bytes 98312 | tf_op jit(solution)/shard_map/ppermute | solution.py:33
  7.1 3.6 %gather_fusion.4 = f32[16,7,8,256]{3,2,1,0:T(8,128)} fusion(f32[7,64,8,256]{3,2,1,0:T(8,128)} %param.23, s32[1024]{0:T(1024)S(1)} %pad_clamp_fusion), kind=kCustom, calls=%fused_computation.4 | custom fusion | bytes 1835072 | tf_op jit(solution)/shard_map/gather | solution.py:420
  10.7 6.0 %all-to-all-start.1 = ((f32[7,16,8,256]{3,2,0,1:T(8,128)}), f32[7,16,8,256]{3,2,0,1:T(8,128)}, u32[]{:S(2)}, u32[]{:S(2)}) async-start(f32[7,16,8,256]{3,2,0,1:T(8,128)} %bitcast.17), calls=%async_computation.1 | async-start | bytes 1835008 | tf_op jit(solution)/shard_map/all_to_all | solution.py:419
  16.8 2.7 %gather_fusion.1 = f32[8,7,8,256]{3,2,1,0:T(8,128)S(1)} fusion(f32[7,64,8,256]{3,2,1,0:T(8,128)} %param.23, s32[1024]{0:T(1024)S(1)} %get-tuple-element.74), kind=kCustom, calls=%fused_computation.1 | custom fusion | bytes 917536 | tf_op jit(solution)/shard_map/gather | solution.py:447
  20.4 2.6 %gather_fusion = f32[8,7,8,256]{3,2,1,0:T(8,128)S(1)} fusion(f32[7,64,8,256]{3,2,1,0:T(8,128)} %param.23, s32[1024]{0:T(1024)S(1)} %get-tuple-element.75), kind=kCustom, calls=%fused_computation | custom fusion | bytes 917536 | tf_op jit(solution)/shard_map/gather | solution.py:447
  24.8 12.7 %all-to-all-done.1 = f32[7,16,8,256]{3,2,0,1:T(8,128)} async-done(((f32[7,16,8,256]{3,2,0,1:T(8,128)}), f32[7,16,8,256]{3,2,0,1:T(8,128)}, u32[]{:S(2)}, u32[]{:S(2)}) %all-to-all-start.1) | async-done | bytes 917536 | tf_op jit(solution)/shard_map/all_to_all | solution.py:419
  37.5 6.1 %all-to-all-start = ((f32[16,1,9]{2,1,0:T(1,128)}), f32[16,1,9]{2,1,0:T(1,128)S(1)}, u32[]{:S(2)}, u32[]{:S(2)}) async-start(f32[16,1,9]{2,1,0:T(1,128)} %copy.106), calls=%async_computation | async-start | bytes 16384 | tf_op jit(solution)/shard_map/all_to_all | solution.py:423
  46.3 3.7 %all-to-all-done = f32[16,1,9]{2,1,0:T(1,128)S(1)} async-done(((f32[16,1,9]{2,1,0:T(1,128)}), f32[16,1,9]{2,1,0:T(1,128)S(1)}, u32[]{:S(2)}, u32[]{:S(2)}) %all-to-all-start) | async-done | bytes 608 | tf_op jit(solution)/shard_map/all_to_all | solution.py:423
  50.2 10.6 %shard_map.149 = (f32[7,8,8,256]{3,2,1,0:T(8,128)S(1)}, f32[7,8,8,256]{3,2,1,0:T(8,128)S(1)}, f32[6,8,128]{2,1,0:T(8,128)S(1)}) custom-call(f32[6,8,256]{2,1,0:T(8,128)S(1)} %broadcast_in_dim.51.strain_ref, f32[4,16,256]{2,1,0:T(8,128)S(1)} %constant_dynamic-update-slice_fusion.props_ref, f32[21,16,256]{2,1,0:T(8,128)S(1)} %copy-done.1, ...), custom_call_target="tpu_custom_call" | custom-call | flops 2415919104 | bytes 1835008 | tf_op jit(solution)/shard_map/pallas_call | solution.py:270
  62.5 10.6 %shard_map.151 = (f32[7,8,8,256]{3,2,1,0:T(8,128)S(1)}, f32[7,8,8,256]{3,2,1,0:T(8,128)S(1)}, f32[6,8,128]{2,1,0:T(8,128)S(1)}) custom-call(f32[6,8,256]{2,1,0:T(8,128)S(1)} %broadcast_in_dim.62.strain_ref, f32[4,16,256]{2,1,0:T(8,128)S(1)} %constant_dynamic-update-slice_fusion.props_ref, f32[21,16,256]{2,1,0:T(8,128)S(1)} %copy-done.1, ...), custom_call_target="tpu_custom_call" | custom-call | flops 2415919104 | bytes 1835008 | tf_op jit(solution)/shard_map/pallas_call | solution.py:270
  77.6 3.4 %all-to-all-start.2 = ((f32[16,1,6]{2,1,0:T(1,128)}), f32[16,1,6]{2,1,0:T(1,128)S(1)}, u32[]{:S(2)}, u32[]{:S(2)}) async-start(f32[16,1,6]{2,1,0:T(1,128)} %copy.110), calls=%async_computation.2 | async-start | bytes 16384 | tf_op jit(solution)/shard_map/all_to_all | solution.py:465
  83.3 4.1 %all-to-all-done.2 = f32[16,1,6]{2,1,0:T(1,128)S(1)} async-done(((f32[16,1,6]{2,1,0:T(1,128)}), f32[16,1,6]{2,1,0:T(1,128)S(1)}, u32[]{:S(2)}, u32[]{:S(2)}) %all-to-all-start.2) | async-done | bytes 416 | tf_op jit(solution)/shard_map/all_to_all | solution.py:465
  87.4 4.3 %all-to-all-start.3 = ((f32[7,16,8,256]{3,2,0,1:T(8,128)}), f32[7,16,8,256]{3,2,0,1:T(8,128)}, u32[]{:S(2)}, u32[]{:S(2)}) async-start(f32[7,16,8,256]{3,2,0,1:T(8,128)} %copy.116), calls=%async_computation.3 | async-start | bytes 1835008 | tf_op jit(solution)/shard_map/all_to_all | solution.py:451
  91.7 2.6 %gather_fusion.3 = f32[8,7,8,256]{3,2,1,0:T(8,128)S(1)} fusion(f32[7,64,8,256]{3,2,1,0:T(8,128)} %param.23, s32[1024]{0:T(1024)S(1)} %get-tuple-element.72), kind=kCustom, calls=%fused_computation.3 | custom fusion | bytes 917536 | tf_op jit(solution)/shard_map/gather | solution.py:447
  96.1 2.6 %gather_fusion.2 = f32[8,7,8,256]{3,2,1,0:T(8,128)S(1)} fusion(f32[7,64,8,256]{3,2,1,0:T(8,128)} %param.23, s32[1024]{0:T(1024)S(1)} %get-tuple-element.73), kind=kCustom, calls=%fused_computation.2 | custom fusion | bytes 917536 | tf_op jit(solution)/shard_map/gather | solution.py:447
  98.9 8.3 %collective-permute-done.3.refs_1_ = f32[7,8,8,256]{3,2,1,0:T(8,128)S(1)} collective-permute-done((f32[7,8,8,256]{3,2,1,0:T(8,128)S(1)}, f32[7,8,8,256]{3,2,1,0:T(8,128)S(1)}, u32[]{:S(2)}, u32[]{:S(2)}) %collective-permute-start.3) | collective-permute-done | bytes 458784 | tf_op jit(solution)/shard_map/ppermute | solution.py:33
  107.3 10.6 %shard_map.150 = (f32[7,8,8,256]{3,2,1,0:T(8,128)S(1)}, f32[7,8,8,256]{3,2,1,0:T(8,128)S(1)}, f32[6,8,128]{2,1,0:T(8,128)S(1)}) custom-call(f32[6,8,256]{2,1,0:T(8,128)S(1)} %broadcast_in_dim.56.strain_ref, f32[4,16,256]{2,1,0:T(8,128)S(1)} %constant_dynamic-update-slice_fusion.props_ref, f32[21,16,256]{2,1,0:T(8,128)S(1)} %copy-done.1, ...), custom_call_target="tpu_custom_call" | custom-call | flops 2415919104 | bytes 1835008 | tf_op jit(solution)/shard_map/pallas_call | solution.py:270
  120.0 9.9 %collective-permute-done.9 = f32[7,8,8,256]{3,1,2,0:T(8,128)S(1)} collective-permute-done((f32[7,8,8,256]{3,1,2,0:T(8,128)S(1)}, f32[7,8,8,256]{3,1,2,0:T(8,128)S(1)}, u32[]{:S(2)}, u32[]{:S(2)}) %collective-permute-start.9) | collective-permute-done | bytes 458784 | tf_op jit(solution)/shard_map/ppermute | solution.py:33
  131.0 5.8 %all-to-all-start.4 = ((f32[7,16,8,256]{3,2,0,1:T(8,128)}), f32[7,16,8,256]{3,2,0,1:T(8,128)S(1)}, u32[]{:S(2)}, u32[]{:S(2)}) async-start(f32[7,16,8,256]{3,2,0,1:T(8,128)} %copy.120), calls=%async_computation.4 | async-start | bytes 1835008 | tf_op jit(solution)/shard_map/all_to_all | solution.py:451
  138.7 2.0 %collective-permute-done.4 = f32[6,2,8]{2,1,0:T(2,128)S(1)} collective-permute-done((f32[6,2,8]{2,1,0:T(2,128)S(1)}, f32[6,2,8]{2,1,0:T(2,128)S(1)}, u32[]{:S(2)}, u32[]{:S(2)}) %collective-permute-start.4) | collective-permute-done | bytes 416 | tf_op jit(solution)/shard_map/ppermute | solution.py:33
  143.3 3.2 %collective-permute-start.7 = (f32[3,16]{1,0:T(4,128)S(1)}, f32[3,16]{1,0:T(4,128)S(1)}, u32[]{:S(2)}, u32[]{:S(2)}) collective-permute-start(f32[3,16]{1,0:T(4,128)S(1)} %slice.122), channel_id=1, source_target_pairs={{2,0},{4,2},{6,4},{8,6},{10,8},{12,10},{14,12},{16,14},{18,16},{20... | collective-permute-start | bytes 584 | tf_op jit(solution)/shard_map/ppermute | solution.py:33
  146.8 6.0 %collective-permute-done.7 = f32[3,16]{1,0:T(4,128)S(1)} collective-permute-done((f32[3,16]{1,0:T(4,128)S(1)}, f32[3,16]{1,0:T(4,128)S(1)}, u32[]{:S(2)}, u32[]{:S(2)}) %collective-permute-start.7) | collective-permute-done | bytes 224 | tf_op jit(solution)/shard_map/ppermute | solution.py:33
  154.9 2.8 %all-to-all-done.4 = f32[7,16,8,256]{3,2,0,1:T(8,128)S(1)} async-done(((f32[7,16,8,256]{3,2,0,1:T(8,128)}), f32[7,16,8,256]{3,2,0,1:T(8,128)S(1)}, u32[]{:S(2)}, u32[]{:S(2)}) %all-to-all-start.4) | async-done | bytes 917536 | tf_op jit(solution)/shard_map/all_to_all | solution.py:451
  159.0 2.5 %shard_map.152 = f32[7,24,8,256]{3,2,1,0:T(8,128)} custom-call(s32[24]{0:T(128)S(1)} %select_reduce_fusion.1.order_ref, f32[7,16,8,256]{3,2,1,0:T(8,128)S(1)} %copy.124.refs_0_, f32[7,16,8,256]{3,2,1,0:T(8,128)S(1)} %copy.125.refs_1_, f32[7,16,8,256]{3,2,1,0:T(8,128)S(1)} %fusion.3.refs_2_), custom_call_target="tpu_custom_call" | custom-call | tf_op jit(solution)/shard_map/pallas_call | solution.py:314
  (113 shorter events, 31.0 us)
Async XLA Ops:
  0.6 19.8 %copy-start.3 = (f32[4,8,256]{2,1,0:T(8,128)S(1)}, f32[4,8,256]{2,1,0:T(8,128)}, u32[]{:S(2)}) copy-start(f32[4,8,256]{2,1,0:T(8,128)} %param.24) | copy-start | bytes 98308
  1.5 21.7 %collective-permute-start = (f32[3,16]{1,0:T(4,128)S(1)}, f32[3,16]{1,0:T(4,128)S(1)}, u32[]{:S(2)}, u32[]{:S(2)}) collective-permute-start(f32[3,16]{1,0:T(4,128)S(1)} %convolution_bitcast_fusion.1), channel_id=1, source_target_pairs={{30,0},{0,2},{2,4},{4,6},{6,8},{8,10},{10,12},{12,14},{14,16},{16,... | collective-permute-start | bytes 584 | tf_op jit(solution)/shard_map/ppermute | solution.py:33
  2.0 48.0 %collective-permute-start.1 = (f32[4,8,256]{2,1,0:T(8,128)}, f32[4,8,256]{2,1,0:T(8,128)S(1)}, u32[]{:S(2)}, u32[]{:S(2)}) collective-permute-start(f32[4,8,256]{2,1,0:T(8,128)} %param.24), channel_id=1, source_target_pairs={{1,0},{0,1},{3,2},{2,3},{5,4},{4,5},{7,6},{6,7},{9,8},{8,9},{11,10... | collective-permute-start | bytes 98312 | tf_op jit(solution)/shard_map/ppermute | solution.py:33
  7.0 16.7 %copy-start.2 = (f32[3,8,64]{2,1,0:T(8,128)S(1)}, f32[3,8,64]{2,1,0:T(8,128)}, u32[]{:S(2)}) copy-start(f32[3,8,64]{2,1,0:T(8,128)} %param.18) | copy-start | bytes 18436
  7.1 16.7 %copy-start.4 = (f32[2,64]{1,0:T(2,128)S(1)}, f32[2,64]{1,0:T(2,128)}, u32[]{:S(2)}) copy-start(f32[2,64]{1,0:T(2,128)} %param.20) | copy-start | bytes 1540
  10.7 26.8 %all-to-all-start.1 = ((f32[7,16,8,256]{3,2,0,1:T(8,128)}), f32[7,16,8,256]{3,2,0,1:T(8,128)}, u32[]{:S(2)}, u32[]{:S(2)}) async-start(f32[7,16,8,256]{3,2,0,1:T(8,128)} %bitcast.17), calls=%async_computation.1 | async-start | bytes 1835008 | tf_op jit(solution)/shard_map/all_to_all | solution.py:419
  16.6 33.5 %copy-start = (bf16[4,256,256]{2,1,0:T(8,128)(2,1)S(1)}, bf16[4,256,256]{2,1,0:T(8,128)(2,1)}, u32[]{:S(2)}) copy-start(bf16[4,256,256]{2,1,0:T(8,128)(2,1)} %constant.95.plane_ref) | copy-start | bytes 1572868
  16.6 33.5 %copy-start.1 = (f32[21,16,256]{2,1,0:T(8,128)S(1)}, f32[21,16,256]{2,1,0:T(8,128)}, u32[]{:S(2)}) copy-start(f32[21,16,256]{2,1,0:T(8,128)} %constant.80.clone.green_ref) | copy-start | bytes 1032196
  19.7 30.4 %collective-permute-start.2 = (f32[7,8,8,256]{3,2,1,0:T(8,128)S(1)}, f32[7,8,8,256]{3,2,1,0:T(8,128)S(1)}, u32[]{:S(2)}, u32[]{:S(2)}) collective-permute-start(f32[7,8,8,256]{3,2,1,0:T(8,128)S(1)} %bitcast.89), channel_id=1, source_target_pairs={{1,0},{0,1},{3,2},{2,3},{5,4},{4,5},{7,6},{6,7},{9,8},{8,9},{11,10... | collective-permute-start | bytes 1376264 | tf_op jit(solution)/shard_map/ppermute | solution.py:33
  37.5 12.5 %all-to-all-start = ((f32[16,1,9]{2,1,0:T(1,128)}), f32[16,1,9]{2,1,0:T(1,128)S(1)}, u32[]{:S(2)}, u32[]{:S(2)}) async-start(f32[16,1,9]{2,1,0:T(1,128)} %copy.106), calls=%async_computation | async-start | bytes 16384 | tf_op jit(solution)/shard_map/all_to_all | solution.py:423
  45.7 16.7 %collective-permute-start.5 = (f32[7,8,8,256]{3,2,1,0:T(8,128)}, f32[7,8,8,256]{3,2,1,0:T(8,128)S(1)}, u32[]{:S(2)}, u32[]{:S(2)}) collective-permute-start(f32[7,8,8,256]{3,2,1,0:T(8,128)} %bitcast.80), channel_id=1, source_target_pairs={{1,0},{0,1},{3,2},{2,3},{5,4},{4,5},{7,6},{6,7},{9,8},{8,9},{11,10... | collective-permute-start | bytes 1376264 | tf_op jit(solution)/shard_map/ppermute | solution.py:33
  61.7 19.3 %collective-permute-start.8 = (f32[7,8,8,256]{3,1,2,0:T(8,128)}, f32[7,8,8,256]{3,1,2,0:T(8,128)}, u32[]{:S(2)}, u32[]{:S(2)}) collective-permute-start(f32[7,8,8,256]{3,1,2,0:T(8,128)} %copy.113), channel_id=1, source_target_pairs={{1,0},{0,1},{3,2},{2,3},{5,4},{4,5},{7,6},{6,7},{9,8},{8,9},{11,10... | collective-permute-start | bytes 1376264 | tf_op jit(solution)/shard_map/ppermute | solution.py:33
  73.2 3.6 %collective-permute-start.6 = (f32[6,8]{1,0:T(8,128)S(1)}, f32[6,8]{1,0:T(8,128)S(1)}, u32[]{:S(2)}, u32[]{:S(2)}) collective-permute-start(f32[6,8]{1,0:T(8,128)S(1)} %slice_reduce_fusion), channel_id=1, source_target_pairs={{1,0},{0,1},{3,2},{2,3},{5,4},{4,5},{7,6},{6,7},{9,8},{8,9},{11,10... | collective-permute-start | bytes 584 | tf_op jit(solution)/shard_map/ppermute | solution.py:33
  77.6 9.8 %all-to-all-start.2 = ((f32[16,1,6]{2,1,0:T(1,128)}), f32[16,1,6]{2,1,0:T(1,128)S(1)}, u32[]{:S(2)}, u32[]{:S(2)}) async-start(f32[16,1,6]{2,1,0:T(1,128)} %copy.110), calls=%async_computation.2 | async-start | bytes 16384 | tf_op jit(solution)/shard_map/all_to_all | solution.py:465
  87.4 43.6 %all-to-all-start.3 = ((f32[7,16,8,256]{3,2,0,1:T(8,128)}), f32[7,16,8,256]{3,2,0,1:T(8,128)}, u32[]{:S(2)}, u32[]{:S(2)}) async-start(f32[7,16,8,256]{3,2,0,1:T(8,128)} %copy.116), calls=%async_computation.3 | async-start | bytes 1835008 | tf_op jit(solution)/shard_map/all_to_all | solution.py:451
  94.5 12.7 %collective-permute-start.3 = (f32[7,8,8,256]{3,2,1,0:T(8,128)S(1)}, f32[7,8,8,256]{3,2,1,0:T(8,128)S(1)}, u32[]{:S(2)}, u32[]{:S(2)}) collective-permute-start(f32[7,8,8,256]{3,2,1,0:T(8,128)S(1)} %bitcast.90), channel_id=1, source_target_pairs={{1,0},{0,1},{3,2},{2,3},{5,4},{4,5},{7,6},{6,7},{9,8},{8,9},{11,10... | collective-permute-start | bytes 1376264 | tf_op jit(solution)/shard_map/ppermute | solution.py:33
  118.0 11.9 %collective-permute-start.9 = (f32[7,8,8,256]{3,1,2,0:T(8,128)S(1)}, f32[7,8,8,256]{3,1,2,0:T(8,128)S(1)}, u32[]{:S(2)}, u32[]{:S(2)}) collective-permute-start(f32[7,8,8,256]{3,1,2,0:T(8,128)S(1)} %copy.117), channel_id=1, source_target_pairs={{1,0},{0,1},{3,2},{2,3},{5,4},{4,5},{7,6},{6,7},{9,8},{8,9},{11,10... | collective-permute-start | bytes 1376264 | tf_op jit(solution)/shard_map/ppermute | solution.py:33
  119.8 23.1 %copy-start.5 = (f32[64]{0:T(128)S(1)}, f32[64]{0:T(128)}, u32[]{:S(2)}) copy-start(f32[64]{0:T(128)} %param.19) | copy-start | bytes 772
  120.0 32.9 %copy-start.8 = (f32[3,64]{1,0:T(4,128)S(1)}, f32[3,64]{1,0:T(4,128)}, u32[]{:S(2)}) copy-start(f32[3,64]{1,0:T(4,128)} %param.15) | copy-start | bytes 2308
  120.0 32.9 %copy-start.9 = (s32[16]{0:T(128)S(1)}, s32[16]{0:T(128)}, u32[]{:S(2)}) copy-start(s32[16]{0:T(128)} %param.17) | copy-start | bytes 196
  131.0 26.6 %all-to-all-start.4 = ((f32[7,16,8,256]{3,2,0,1:T(8,128)}), f32[7,16,8,256]{3,2,0,1:T(8,128)S(1)}, u32[]{:S(2)}, u32[]{:S(2)}) async-start(f32[7,16,8,256]{3,2,0,1:T(8,128)} %copy.120), calls=%async_computation.4 | async-start | bytes 1835008 | tf_op jit(solution)/shard_map/all_to_all | solution.py:451
  137.0 3.7 %collective-permute-start.4 = (f32[6,2,8]{2,1,0:T(2,128)S(1)}, f32[6,2,8]{2,1,0:T(2,128)S(1)}, u32[]{:S(2)}, u32[]{:S(2)}) collective-permute-start(f32[6,2,8]{2,1,0:T(2,128)S(1)} %pad_maximum_fusion.1), channel_id=1, source_target_pairs={{1,0},{0,1},{3,2},{2,3},{5,4},{4,5},{7,6},{6,7},{9,8},{8,9},{11,10... | collective-permute-start | bytes 1160 | tf_op jit(solution)/shard_map/ppermute | solution.py:33
  141.1 16.7 %collective-permute-start.10 = (f32[7,8,8,256]{3,1,2,0:T(8,128)S(1)}, f32[7,8,8,256]{3,1,2,0:T(8,128)}, u32[]{:S(2)}, u32[]{:S(2)}) collective-permute-start(f32[7,8,8,256]{3,1,2,0:T(8,128)S(1)} %copy.121), channel_id=1, source_target_pairs={{1,0},{0,1},{3,2},{2,3},{5,4},{4,5},{7,6},{6,7},{9,8},{8,9},{11,10... | collective-permute-start | bytes 1376264 | tf_op jit(solution)/shard_map/ppermute | solution.py:33
  143.3 9.5 %collective-permute-start.7 = (f32[3,16]{1,0:T(4,128)S(1)}, f32[3,16]{1,0:T(4,128)S(1)}, u32[]{:S(2)}, u32[]{:S(2)}) collective-permute-start(f32[3,16]{1,0:T(4,128)S(1)} %slice.122), channel_id=1, source_target_pairs={{2,0},{4,2},{6,4},{8,6},{10,8},{12,10},{14,12},{16,14},{18,16},{20... | collective-permute-start | bytes 584 | tf_op jit(solution)/shard_map/ppermute | solution.py:33
  (2 other events, 32.4 us)
